TPU v7x, 32 devices: a whole 2x2x4 slice. The times are simulated.
32 devices in a mesh: dp: 16 (over z, x, core), tensor: 2 (over y).
Axes of the slice: x: 2, y: 2, z: 4, core: 2. Of those that a mesh axis runs over, the one named last changes fastest.
Arguments:
- tokens: bfloat16 [6144, 2048], P(('dp', 'tensor')), may hold values from -6 to 6
- attn_gain: bfloat16 [2048], P('dp'), may hold values from 0.5 to 1.5
- q_weight: bfloat16 [2048, 4096], P('dp', 'tensor'), may hold values from -0.125 to 0.125
- key_matrix: bfloat16 [2048, 512], P('dp', 'tensor'), may hold values from -0.125 to 0.125
- value_matrix: bfloat16 [2048, 512], P('dp', 'tensor'), may hold values from -0.125 to 0.125
- o_weight: bfloat16 [4096, 2048], P('tensor', 'dp'), may hold values from -0.75 to 0.75
- query_norm_gain: bfloat16 [128], P('dp'), may hold values from 0.5 to 1.5
- k_gain: bfloat16 [128], P('dp'), may hold values from 0.5 to 1.5
- ffn_gain: bfloat16 [2048], P('dp'), may hold values from 0.5 to 1.5
- router_weight: bfloat16 [2048, 32], P('dp'), may hold values from -0.024902344 to 0.024902344
- gate_weight: bfloat16 [32, 2048, 768], P('dp', None, 'tensor'), may hold values from -0.125 to 0.125
- up_weight: bfloat16 [32, 2048, 768], P('dp', None, 'tensor'), may hold values from -0.125 to 0.125
- down_weight: bfloat16 [32, 768, 2048], P('dp', 'tensor'), may hold values from -0.625 to 0.625
- expert_ids: int32 [6144, 8], P('dp'), may hold values from 0 to 31, all different within a row; in each aligned block of 384 rows (0 to 383, 384 to 767, ...) at most 120 rows name the same one
- cotangent: bfloat16 [6144, 2048], P(('dp', 'tensor')), may hold values from -6 to 6
Outputs:
- output: bfloat16 [6144, 2048], P(('dp', 'tensor'))
- tokens_grad: float32 [6144, 2048], P(('dp', 'tensor'))
- attn_gain_grad: float32 [2048], P('dp')
- q_weight_grad: float32 [2048, 4096], P('dp', 'tensor')
- k_weight_grad: float32 [2048, 512], P('dp', 'tensor')
- v_weight_grad: float32 [2048, 512], P('dp', 'tensor')
- o_weight_grad: float32 [4096, 2048], P('tensor', 'dp')
- q_gain_grad: float32 [128], P('dp')
- k_gain_grad: float32 [128], P('dp')
- ffn_gain_grad: float32 [2048], P('dp')
- router_weight_grad: float32 [2048, 32], P('dp')
- gate_weight_grad: float32 [32, 2048, 768], P('dp', None, 'tensor')
- up_weight_grad: float32 [32, 2048, 768], P('dp', None, 'tensor')
- down_weight_grad: float32 [32, 768, 2048], P('dp', 'tensor')
Inputs may be any that keep to these rules, and one draw needn't show every extreme that they name: `expert_ids`: each row names 8 different experts. Among the 384 tokens of one sequence (the rows of one device) no expert is named more than 120 times, a bound that some block reaches.
All inputs are finite; a program needn't handle non-finite values.
Results may differ from a plain program's by a relative error of at most 0.019.
Values may be sent and summed in bfloat16 or wider, within the bound.
No kernel may reach another device: no remote copies, remote signals or barrier semaphores. Data moves between devices by JAX's collectives and lax.ppermute only.
A program may use at most 320 MiB of HBM per device.

v0:
```python
import jax
import jax.numpy as jnp
from jax import lax
from jax.experimental import pallas as pl
from jax.experimental.pallas import tpu as pltpu
from jax.sharding import PartitionSpec as P


HEAD = 128
EPS = 1e-06
THETA = 1000000.0
BF = jnp.bfloat16
F32 = jnp.float32


def dot(a, b, ca, cb):
    return lax.dot_general(a, b, (((ca,), (cb,)), ((), ())), preferred_element_type=F32)


def rms(v, gain):
    return v * lax.rsqrt(jnp.mean(v * v, axis=-1, keepdims=True) + EPS) * gain


def rms_back(v, gain, u):
    inv = lax.rsqrt(jnp.mean(v * v, axis=-1, keepdims=True) + EPS)
    ug = u * gain
    grad = ug * inv - v * (jnp.mean(ug * v, axis=-1, keepdims=True) * inv * inv * inv)
    return grad, u * v * inv


def rope_tables(count):
    inverse = THETA ** (-(jnp.arange(HEAD // 2, dtype=F32) * 2.0 / HEAD))
    angles = jnp.arange(count, dtype=F32)[:, None] * inverse[None, :]
    cos, sin = jnp.cos(angles), jnp.sin(angles)
    return jnp.concatenate([cos, cos], axis=1), jnp.concatenate([-sin, sin], axis=1)


def half_turn(v):
    return pltpu.roll(v, HEAD // 2, 1)


def turned(raw, gain, cos, sin):
    v = rms(raw, gain)
    return (v * cos + half_turn(v) * sin).astype(BF)


def soft(q, k):
    scores = lax.dot_general(q, k, (((1,), (1,)), ((), ())), preferred_element_type=F32)
    scores = scores * HEAD ** (-0.5)
    row = lax.broadcasted_iota(jnp.int32, scores.shape, 0)
    column = lax.broadcasted_iota(jnp.int32, scores.shape, 1)
    e = jnp.where(row >= column, jnp.exp(scores), 0.0)
    return e * (1.0 / jnp.sum(e, axis=1, keepdims=True))


def attend_kernel(q_raw, k_raw, v_raw, gains, cos, sin, context, keys):
    @pl.when(pl.program_id(1) == 0)
    def _():
        keys[...] = turned(k_raw[...], gains[1:2], cos[...], sin[...])

    v = v_raw[...].astype(BF)
    for h in range(2):
        part = slice(h * HEAD, (h + 1) * HEAD)
        q = turned(q_raw[:, part], gains[0:1], cos[...], sin[...])
        p = soft(q, keys[...]).astype(BF)
        context[:, part] = lax.dot_general(
            p, v, (((1,), (0,)), ((), ())), preferred_element_type=F32
        ).astype(BF)


def attend_back_kernel(
    q_raw, k_raw, v_raw, d_context, gains, cos, sin, d_q, d_k, d_v, d_gains, keys, k_sum, v_sum
):
    at = pl.program_id(0)

    @pl.when(at == 0)
    def _():
        keys[...] = turned(k_raw[...], gains[1:2], cos[...], sin[...])
        k_sum[...] = jnp.zeros_like(k_sum)
        v_sum[...] = jnp.zeros_like(v_sum)
        d_gains[...] = jnp.zeros_like(d_gains)

    def back(raw, gain, u):
        return rms_back(raw, gain, u * cos[...] - half_turn(u) * sin[...])

    v = v_raw[...].astype(BF)
    scale = HEAD ** (-0.5)
    for h in range(2):
        part = slice(h * HEAD, (h + 1) * HEAD)
        raw = q_raw[:, part]
        q = turned(raw, gains[0:1], cos[...], sin[...])
        p = soft(q, keys[...])
        dc = d_context[:, part]
        dp = lax.dot_general(dc, v, (((1,), (1,)), ((), ())), preferred_element_type=F32)
        v_sum[...] += lax.dot_general(
            p.astype(BF), dc, (((0,), (0,)), ((), ())), preferred_element_type=F32
        )
        ds = (p * (dp - jnp.sum(p * dp, axis=1, keepdims=True))).astype(BF)
        dq = lax.dot_general(
            ds, keys[...], (((1,), (0,)), ((), ())), preferred_element_type=F32
        )
        k_sum[...] += lax.dot_general(ds, q, (((0,), (0,)), ((), ())), preferred_element_type=F32)
        grad, gain_rows = back(raw, gains[0:1], dq * scale)
        d_q[:, part] = grad.astype(BF)
        d_gains[0:1, :] += jnp.sum(gain_rows, axis=0, keepdims=True)

    @pl.when(at == pl.num_programs(0) - 1)
    def _():
        grad, gain_rows = back(k_raw[...], gains[1:2], k_sum[...] * scale)
        d_k[...] = grad.astype(BF)
        d_v[...] = v_sum[...].astype(BF)
        d_gains[1:2, :] += jnp.sum(gain_rows, axis=0, keepdims=True)


def run_attend(qkv, gains, cos, sin, hq, hk):
    seq = qkv.shape[0]
    pairs = hq // hk // 2
    block = lambda width, index: pl.BlockSpec((seq, width * HEAD), index)
    whole = lambda rows: pl.BlockSpec((rows, HEAD), lambda i, j: (0, 0))
    return pl.pallas_call(
        attend_kernel,
        grid=(hk, pairs),
        in_specs=[
            block(2, lambda i, j: (0, i * pairs + j)),
            block(1, lambda i, j: (0, hq + i)),
            block(1, lambda i, j: (0, hq + hk + i)),
            whole(8),
            whole(seq),
            whole(seq),
        ],
        out_specs=block(2, lambda i, j: (0, i * pairs + j)),
        out_shape=jax.ShapeDtypeStruct((seq, hq * HEAD), BF),
        scratch_shapes=[pltpu.VMEM((seq, HEAD), BF)],
        name="attend",
    )(qkv, qkv, qkv, gains, cos, sin)


def run_attend_back(head, qkv, d_context, gains, cos, sin, hq, hk):
    seq = qkv.shape[0]
    pairs = hq // hk // 2
    block = lambda width, index: pl.BlockSpec((seq, width * HEAD), index)
    whole = lambda rows: pl.BlockSpec((rows, HEAD), lambda j: (0, 0))
    return pl.pallas_call(
        attend_back_kernel,
        grid=(pairs,),
        in_specs=[
            block(2, lambda j: (0, head * pairs + j)),
            block(1, lambda j: (0, hq + head)),
            block(1, lambda j: (0, hq + hk + head)),
            block(2, lambda j: (0, head * pairs + j)),
            whole(8),
            whole(seq),
            whole(seq),
        ],
        out_specs=[block(2, lambda j: (0, j)), whole(seq), whole(seq), whole(8)],
        out_shape=[
            jax.ShapeDtypeStruct((seq, 2 * pairs * HEAD), BF),
            jax.ShapeDtypeStruct((seq, HEAD), BF),
            jax.ShapeDtypeStruct((seq, HEAD), BF),
            jax.ShapeDtypeStruct((8, HEAD), F32),
        ],
        scratch_shapes=[
            pltpu.VMEM((seq, HEAD), BF),
            pltpu.VMEM((seq, HEAD), F32),
            pltpu.VMEM((seq, HEAD), F32),
        ],
        name="attend_back",
    )(qkv, qkv, qkv, d_context, gains, cos, sin)


def split2(v):
    high = v.astype(BF)
    return high, (v - high.astype(F32)).astype(BF)


def gather_dp(v):
    return lax.all_gather(v, "dp", axis=0, tiled=True)


def gather_all(v):
    return lax.all_gather(v, ("dp", "tensor"), axis=0, tiled=True)


def scatter_all(v):
    return lax.psum_scatter(v, ("dp", "tensor"), scatter_dimension=0, tiled=True)


def scatter_dp(v):
    return lax.psum_scatter(v, "dp", scatter_dimension=0, tiled=True)


def pieces(width, dp, seq):
    count = 1 if dp * seq <= 8192 else 4
    step = width // count // 128 * 128
    edges = [step * i for i in range(count)] + [width]
    return list(zip(edges[:-1], edges[1:]))


def after(v, earlier):
    return v if earlier is None else lax.optimization_barrier((v, earlier))[0]


def dispatch(pick, own, dp, seq, earlier):
    blocks = []
    for low, high in pieces(own.shape[1], dp, seq):
        every = gather_all(after(own[:, low:high], earlier)).reshape(dp, seq, high - low)
        block = jnp.einsum("gest,gtd->gesd", pick, every, preferred_element_type=F32).astype(BF)
        blocks.append(block)
        earlier = block if len(pieces(own.shape[1], dp, seq)) > 1 else None
    return jnp.concatenate(blocks, axis=3)


def combine(pick, rows, dp, seq, earlier):
    blocks = []
    for low, high in pieces(rows.shape[3], dp, seq):
        tok = jnp.einsum(
            "gest,gesd->gtd",
            pick,
            after(rows[:, :, :, low:high], earlier),
            preferred_element_type=F32,
        ).astype(BF)
        blocks.append(scatter_all(tok.reshape(dp * seq, high - low)))
        earlier = blocks[-1] if len(pieces(rows.shape[3], dp, seq)) > 1 else None
    return jnp.concatenate(blocks, axis=1).astype(F32)


GRID = [(z, x, c) for z in range(4) for x in range(2) for c in range(2)]
SPLIT = (0, 768, 1536, 1792, 2048)


def at(z, x, c):
    return z % 4 * 4 + x % 2 * 2 + c % 2


def shift_z(v, k):
    return lax.ppermute(v, "dp", [(at(z, x, c), at(z + k, x, c)) for z, x, c in GRID])


def swap_x(v):
    return lax.ppermute(v, "dp", [(at(z, x, c), at(z, x + 1, c)) for z, x, c in GRID])


def swap_c(v):
    return lax.ppermute(v, "dp", [(at(z, x, c), at(z, x, c + 1)) for z, x, c in GRID])


def swap_y(v):
    return lax.ppermute(v, "tensor", [(0, 1), (1, 0)])


def gather_y(v):
    other = swap_y(v)
    first = lax.axis_index("tensor") == 0
    return jnp.concatenate([jnp.where(first, v, other), jnp.where(first, other, v)])


def scatter_y(v):
    a, b = jnp.split(v, 2)
    first = lax.axis_index("tensor") == 0
    kept, sent = jnp.where(first, a, b), jnp.where(first, b, a)
    other = swap_y(sent.astype(BF))
    return kept.astype(F32) + other.astype(F32)


def gather_z(v, way):
    one, three = shift_z(v, 1), shift_z(v, -1)
    two = shift_z(one, 1) if way > 0 else shift_z(three, -1)
    return jnp.stack([v, one, two, three])


def add2(a, b):
    return (a.astype(F32) + b.astype(F32)).astype(BF)


def reduce_z(v, way, two=None):
    if two is None:
        two = first_hop(v, way)
    side = shift_z(v[3 if way > 0 else 1], way)
    relay = shift_z(add2(v[1 if way > 0 else 3], two), -way)
    return (v[0].astype(F32) + side.astype(F32) + relay.astype(F32)).astype(BF)


def first_hop(v, way):
    return shift_z(v[2], -way)


def tied(v, w):
    return lax.optimization_barrier((v, w))


def gather_rel(v1, v2, v5, v6, plan, aside):
    w5 = jnp.stack([v5, swap_x(v5)])
    w6 = jnp.stack([v6, swap_y(v6)])
    s1 = gather_z(v1, 1)
    s2 = gather_z(v2, -1)
    w5 = jnp.stack([w5, swap_y(w5)])
    w6 = jnp.stack([w6, swap_x(w6)])
    s1, s2, w5, w6, plan = lax.optimization_barrier((s1, s2, w5, w6, plan))
    s1x, s2y = swap_x(s1), swap_y(s2)
    five = [shift_z(w5, 1), shift_z(w5, -1)]
    six = [shift_z(w6, 1), shift_z(w6, -1)]
    far = aside(1, plan)
    five, six, s1x, s2y, far = lax.optimization_barrier((five, six, s1x, s2y, far))
    s1 = jnp.stack([s1, s1x])
    s2 = jnp.stack([s2, s2y])
    s1y, s2x = swap_y(s1), swap_x(s2)
    five.append(shift_z(five[0], 1))
    six.append(shift_z(six[1], -1))
    plan, (five, six) = tied(plan, (five, six))
    o5 = jnp.stack([w5, five[0], five[2], five[1]])
    o6 = jnp.stack([w6, six[0], six[2], six[1]])
    (s1y, s2x), near = tied((s1y, s2x), aside(0, plan))
    first = (s1, s1y, s2, s2x, o5, o6)
    return first, tuple(swap_c(v) for v in first), plan, (near, far)


def scatter_core(near, far):
    p5, p6, p1, p2 = [add2(near[i], swap_c(far[i])) for i in (2, 3, 0, 1)]
    return p1, p2, p5, p6


def step_x(v):
    other = swap_x(v[1])
    return add2(v[0], other)


def step_y(v):
    other = swap_y(v[1])
    return add2(v[0], other)


def scatter_rows_core(near, far):
    a = swap_c(far[0])
    b = swap_c(far[1])
    return add2(near[0], a), add2(near[1], b)


def scatter_rows(a, b):
    b = reduce_z(b, -1)
    a = step_x(a)
    b = step_x(b)
    return jnp.concatenate([reduce_z(a, 1), b], axis=1)


def sequence_at(dc, dz, dx):
    at = lax.axis_index("dp")
    return (at // 4 - dz) % 4 * 4 + (at // 2 % 2 + dx) % 2 * 2 + (at % 2 + dc) % 2


def nn(a, b):
    return lax.dot_general(a, b, (((1,), (0,)), ((), ())), preferred_element_type=F32)


def nt(a, b):
    return lax.dot_general(a, b, (((1,), (1,)), ((), ())), preferred_element_type=F32)


def pick_rows(rank, slots):
    at_slot = lax.broadcasted_iota(jnp.int32, (slots, rank.shape[1]), 0).astype(F32)
    return jnp.concatenate(
        [(rank[e : e + 1, :] == at_slot).astype(F32).astype(BF) for e in range(rank.shape[0])],
        axis=0,
    )


def pick_cols(rank, slots):
    at_slot = lax.broadcasted_iota(jnp.int32, (rank.shape[0], slots), 1).astype(F32)
    return jnp.concatenate(
        [(rank[:, e : e + 1] == at_slot).astype(F32).astype(BF) for e in range(rank.shape[1])],
        axis=1,
    )


def cot_kernel(where, rank, cot_a, cot_b, down, cots, d_act):
    slots = cots.shape[2] // 2
    for dx, cot in enumerate((cot_a, cot_b)):
        both = nn(pick_rows(rank[dx], slots), cot[0]).astype(BF)
        for e in range(2):
            cots[e, 0, dx * slots : (dx + 1) * slots, :] = both[e * slots : (e + 1) * slots]
    for e in range(2):
        d_act[e, 0] = nt(cots[e, 0], down[e])


def expert_kernel(
    rank, rank_t, cols, d_act, x1a, x1b, x2a, x2b, x5, x6, weights,
    rows, scaled, d_g, d_u, t1, t2, t5, t6, back,
):
    slots = rows.shape[2] // 2
    n = x1a.shape[2]
    gates = []
    for dx, x2 in enumerate((x2a, x2b)):
        pick = pick_rows(rank[dx], slots)
        low, high = pick[:, :n], pick[:, n:]
        block1 = nn(low, x1a[dx, 0]) + nn(high, x1b[dx, 0])
        block2 = nn(low, x2[0, 0]) + nn(high, x2[1, 0])
        block5 = nn(low, x5[0, 0, dx]) + nn(high, x5[0, 1, dx])
        block6 = nn(low, x6[0, dx, 0]) + nn(high, x6[0, dx, 1])
        low = dx * slots
        for e in range(2):
            part = slice(e * slots, (e + 1) * slots)
            rows[e, 0, low : low + slots, 0:768] = block1[part].astype(BF)
            rows[e, 0, low : low + slots, 768:1536] = block2[part].astype(BF)
            rows[e, 0, low : low + slots, 1536:1792] = block5[part, :256].astype(BF)
            rows[e, 0, low : low + slots, 1792:2048] = block6[part].astype(BF)
            both = cols[e, 0:1, :] + cols[e, 1:2, :]
            gates.append(jnp.sum(block5[part, 256:] * both, axis=1, keepdims=True))
    extras = []
    for e in range(2):
        gate = jnp.concatenate([gates[e], gates[2 + e]], axis=0)
        g = nn(rows[e, 0], weights[e])
        g, u = jnp.split(g, 2, axis=1)
        da = d_act[e, 0]
        sig = 1.0 / (1.0 + jnp.exp(-g))
        silu = g * sig
        act = silu * u
        scaled[e, 0] = (act * gate).astype(BF)
        d_gate = jnp.sum(act * da, axis=1, keepdims=True)
        da = da * gate
        dg = (da * u * sig * (1.0 + g * (1.0 - sig))).astype(BF)
        du = (da * silu).astype(BF)
        d_g[e, 0] = dg
        d_u[e, 0] = du
        high = d_gate.astype(BF).astype(F32)
        extras.append(high * cols[e, 0:1, :] + (d_gate - high) * cols[e, 1:2, :])
        dr = nt(jnp.concatenate([dg, du], axis=1), weights[e]).astype(BF)
        for dx in range(2):
            back[dx, e * slots : (e + 1) * slots, :] = dr[dx * slots : (dx + 1) * slots]
    extra = [
        jnp.concatenate([extras[e][dx * slots : (dx + 1) * slots] for e in range(2)], axis=0)
        for dx in range(2)
    ]
    put_back(rank_t, back, t1, t2, t5, t6, slots, extra)


def put_back(rank_t, back, t1, t2, t5, t6, slots, extra=None):
    for dx in range(2):
        pick_t = pick_cols(rank_t[dx], slots)
        n = pick_t.shape[0] // 2
        p1, p2, p5, p6 = [
            nn(pick_t, back[dx, :, a:b]).astype(BF) for a, b in zip(SPLIT[:-1], SPLIT[1:])
        ]
        for dy in range(2):
            half = slice(dy * n, (dy + 1) * n)
            t1[dy, dx, 0] = p1[half]
            t2[dx, dy, 0] = p2[half]
            t5[0, dy, dx, :, 0:256] = p5[half]
            t6[0, dx, dy] = p6[half]
        if extra is not None:
            p7 = nn(pick_t, extra[dx].astype(BF)).astype(BF)
            for dy in range(2):
                t5[0, dy, dx, :, 256:] = p7[dy * n : (dy + 1) * n]


def out_kernel(rank_t, scaled, down, t1, t2, t5, t6, back):
    slots = scaled.shape[2] // 2
    for e in range(2):
        y = nn(scaled[e, 0], down[e]).astype(BF)
        for dx in range(2):
            back[dx, e * slots : (e + 1) * slots, :] = y[dx * slots : (dx + 1) * slots]
    put_back(rank_t, back, t1, t2, t5, t6, slots)


def grad_kernel(where, left, right, small, heads, a, b):
    both = lax.dot_general(
        left[...], right[...], (((0,), (0,)), ((), ())), preferred_element_type=F32
    ).astype(BF)
    width = a.shape[-1]
    a[0, 0] = both[:, :width]
    b[0, 0, :, : both.shape[1] - width] = both[:, width:]
    rest = jnp.zeros((small.shape[0] - heads.shape[0], small.shape[1]), F32)
    both_small = small[...] + jnp.concatenate([heads[...], rest], axis=0)
    b[0, 0, :, both.shape[1] - width :] = both_small.astype(BF)


def run_grad(where, left, right, small, heads):
    count, columns = right.shape
    rest = small.shape[1]
    width = columns * 9 // 16 // 128 * 128
    shard = left.shape[1] // 16
    return pl.pallas_call(
        grad_kernel,
        grid_spec=pltpu.PrefetchScalarGridSpec(
            num_scalar_prefetch=1,
            grid=(2, 4),
            in_specs=[
                pl.BlockSpec((count, shard), lambda dx, dz, w: (0, w[2 * dz + dx])),
                pl.BlockSpec((count, columns), lambda dx, dz, w: (0, 0)),
                pl.BlockSpec((shard, rest), lambda dx, dz, w: (w[2 * dz + dx], 0)),
                pl.BlockSpec((HEAD // 16, rest), lambda dx, dz, w: (w[2 * dz + dx], 0)),
            ],
            out_specs=[
                pl.BlockSpec((1, 1, shard, width), lambda dx, dz, w: (dx, dz, 0, 0)),
                pl.BlockSpec((1, 1, shard, columns - width + rest), lambda dx, dz, w: (dz, dx, 0, 0)),
            ],
        ),
        out_shape=[
            shaped((2, 4, shard, width), BF),
            shaped((4, 2, shard, columns - width + rest), BF),
        ],
        compiler_params=LIMIT,
        name="grad",
    )(where, left, right, small, heads)


def pair(*tail):
    return pl.BlockSpec((2, *tail), lambda i, *_: (i,) + (0,) * len(tail))


def z_last(*lead):
    def spec(rows, columns):
        return pl.BlockSpec(
            (*lead, 1, rows, columns), lambda i, *_: (0,) * len(lead) + (i, 0, 0)
        )

    return spec


def z_first(rows, columns):
    return pl.BlockSpec((1, 2, 2, rows, columns), lambda i, *_: (i, 0, 0, 0, 0))


def block_specs(n, extra):
    return [z_last(2, 2)(n, 768), z_last(2, 2)(n, 768), z_first(n, 256 + extra), z_first(n, 256)]


def block_shapes(n, extra):
    shapes = [(2, 2, 4, n, 768), (2, 2, 4, n, 768), (4, 2, 2, n, 256 + extra), (4, 2, 2, n, 256)]
    return [shaped(v, BF) for v in shapes]


def by_expert(*tail):
    return pl.BlockSpec((2, 1, *tail), lambda i, *_: (0, i) + (0,) * len(tail))


def fixed(*shape):
    return pl.BlockSpec(
        shape, lambda i, *_: (0,) * len(shape), pipeline_mode=pl.Buffered(1)
    )


def shaped(shape, kind):
    return jax.ShapeDtypeStruct(shape, kind)


LIMIT = pltpu.CompilerParams(vmem_limit_bytes=58 * 1024 * 1024)


def run_cots(where, rank, cot_all, down, slots):
    seq, width = cot_all.shape[1:]
    ff = down.shape[1]
    return pl.pallas_call(
        cot_kernel,
        grid_spec=pltpu.PrefetchScalarGridSpec(
            num_scalar_prefetch=1,
            grid=(4,),
            in_specs=[
                pair(2, seq),
                pl.BlockSpec((1, seq, width), lambda i, w: (w[2 * i], 0, 0)),
                pl.BlockSpec((1, seq, width), lambda i, w: (w[2 * i + 1], 0, 0)),
                fixed(2, ff, width),
            ],
            out_specs=[by_expert(2 * slots, width), by_expert(2 * slots, ff)],
        ),
        out_shape=[shaped((2, 4, 2 * slots, width), BF), shaped((2, 4, 2 * slots, ff), F32)],
        compiler_params=LIMIT,
        name="cots",
    )(where, rank, cot_all, cot_all, down)


def run_experts(rank, rank_t, cols, d_act, parts, weights, slots):
    s1, s1y, s2, s2x, o5, o6 = parts
    n = s1.shape[2]
    seq, width, ff = 2 * n, weights.shape[1], weights.shape[2] // 2
    return pl.pallas_call(
        expert_kernel,
        grid=(4,),
        in_specs=[
            pair(2, seq),
            pair(seq, 2),
            fixed(*cols.shape),
            by_expert(2 * slots, ff),
            z_last(2)(n, 768),
            z_last(2)(n, 768),
            z_last(2)(n, 768),
            z_last(2)(n, 768),
            z_first(n, 384),
            z_first(n, 256),
            fixed(2, width, 2 * ff),
        ],
        out_specs=[
            by_expert(2 * slots, width),
            by_expert(2 * slots, ff),
            by_expert(2 * slots, ff),
            by_expert(2 * slots, ff),
        ]
        + block_specs(n, 128),
        out_shape=[
            shaped((2, 4, 2 * slots, width), BF),
            shaped((2, 4, 2 * slots, ff), BF),
            shaped((2, 4, 2 * slots, ff), BF),
            shaped((2, 4, 2 * slots, ff), BF),
        ]
        + block_shapes(n, 128),
        scratch_shapes=[pltpu.VMEM((2, 2 * slots, width), BF)],
        compiler_params=LIMIT,
        name="experts",
    )(
        rank, rank_t, cols, d_act, s1, s1y, s2, s2x, o5, o6, weights,
    )


def run_outs(rank_t, scaled, down, slots):
    seq, ff, width = rank_t.shape[1], down.shape[1], down.shape[2]
    return pl.pallas_call(
        out_kernel,
        grid=(4,),
        in_specs=[pair(seq, 2), by_expert(2 * slots, ff), fixed(2, ff, width)],
        out_specs=block_specs(seq // 2, 0),
        out_shape=block_shapes(seq // 2, 0),
        scratch_shapes=[pltpu.VMEM((2, 2 * slots, width), BF)],
        compiler_params=LIMIT,
        name="outs",
    )(rank_t, scaled, down)


def flip(v, axis, y):
    a, b = jnp.split(v, 2, axis=axis)
    return jnp.where(y == 0, v, jnp.concatenate([b, a], axis=axis))


def slot_plan(ids_all, experts):
    y = lax.axis_index("tensor")
    seq = ids_all.shape[1]
    mine = lax.axis_index("dp") * 2 + jnp.arange(2, dtype=jnp.int32)
    mask = jnp.any(ids_all[:, None, :, :] == mine[None, :, None, None], axis=3)
    before = (jnp.arange(seq)[:, None] < jnp.arange(seq)[None, :]).astype(BF)
    rank = jnp.einsum("gea,ab->geb", mask.astype(BF), before, preferred_element_type=F32)
    rank = jnp.where(mask, rank, -1.0)
    d = jnp.arange(16)
    where = sequence_at(d // 8, d // 2 % 4, d % 2)
    rank = jnp.take(rank, where, axis=0)
    rank_rel = flip(rank, 2, y)
    rank_t = jnp.swapaxes(rank_rel, 1, 2)
    column = jnp.arange(128)
    cols = (
        column[None, None, :] == (mine[:, None] + jnp.array([[0, experts]]))[:, :, None]
    ).astype(F32)
    halves = lambda v: (v[:8], v[8:])
    return halves(where.astype(jnp.int32)), halves(rank), halves(rank_rel), halves(rank_t), cols


def moe_small(plan, cot_all, ffn_in, gate_x, weights, down_weight, slots):

    def cot_rows(k, plan):
        return run_cots(plan[0][k], plan[1][k], cot_all, down_weight, slots)

    v1, v2, v5, v6 = [ffn_in[:, a:b] for a, b in zip(SPLIT[:-1], SPLIT[1:])]
    v5 = jnp.concatenate([v5, gate_x], axis=1)
    *parts, plan, both = gather_rel(v1, v2, v5, v6, plan, cot_rows)
    rank_rel, rank_t, cols = plan[2:]
    cots, d_act = zip(*both)
    far, near = [
        run_experts(rank_rel[k], rank_t[k], cols, d_act[k], parts[k], weights, slots)
        for k in (1, 0)
    ]
    p1, p2, p5, p6 = scatter_core(near[4:], far[4:])
    kept = lambda i: (near[i], far[i])
    total = lambda spec, a, b: jnp.einsum(spec, a[0], b[0], preferred_element_type=F32) + jnp.einsum(
        spec, a[1], b[1], preferred_element_type=F32
    )
    p5 = reduce_z(p5, 1)
    p6 = reduce_z(p6, -1)
    p1 = step_y(p1)
    p2 = step_x(p2)
    down_grad = total("egsf,egsd->efd", kept(1), cots)
    outs = []
    for k in (0, 1):
        outs.append(run_outs(rank_t[k], kept(1)[k], down_weight, slots))
    (p1, p2, p5, p6), (outs, down_grad) = tied((p1, p2, p5, p6), (outs, down_grad))
    p5 = step_y(p5)
    p6 = step_x(p6)
    p1 = step_x(p1)
    p2 = step_y(p2)
    up_grad = total("egsd,egsf->edf", kept(0), kept(3))
    (p1, p2, p5, p6), up_grad = tied((p1, p2, p5, p6), up_grad)
    d5 = step_x(p5)
    d6 = step_y(p6)
    d1 = reduce_z(p1, 1)
    d2 = reduce_z(p2, -1)
    p1, p2, p5, p6 = scatter_core(*outs)
    p2, (d5, d6) = tied(p2, (d5, d6))
    p2 = step_x(p2)
    d_sum = jnp.concatenate([d1, d2, d5[:, :256], d6, d5[:, 256:]], axis=1)
    d_sum, (p1, p5, p6) = tied(d_sum, (p1, p5, p6))
    d_sum = d_sum.astype(F32)

    def gate_later(aside):
        (rows, grads), aside = tied((kept(0), kept(2)), aside)
        return total("egsd,egsf->edf", rows, grads), aside

    return d_sum, (p1, p2, p5, p6), gate_later, up_grad, down_grad


def moe_large(
    ids_all, cotangent, ffn_in, gate_x, gate_weight, up_weight, down_weight, experts, slots
):
    dp, seq = ids_all.shape[:2]
    local = gate_weight.shape[0]
    dp_at = lax.axis_index("dp")
    mine = dp_at * local + jnp.arange(local, dtype=jnp.int32)
    mask = jnp.any(ids_all[:, :, None, :] == mine[None, None, :, None], axis=3).astype(BF)
    gate_all = gather_all(gate_x).reshape(dp, seq, -1)
    before = (jnp.arange(seq)[:, None] > jnp.arange(seq)[None, :]).astype(BF)
    rank = jnp.einsum("ab,gbe->gea", before, mask, preferred_element_type=F32)
    rank = jnp.where(jnp.swapaxes(mask, 1, 2) > 0, rank, -1.0)
    pick = (rank[:, :, None, :] == jnp.arange(slots, dtype=F32)[None, None, :, None]).astype(BF)

    cots = dispatch(pick, cotangent, dp, seq, None)
    rows = dispatch(pick, ffn_in, dp, seq, cots)
    gate_tok = lax.dynamic_slice_in_dim(gate_all, dp_at * local, local, 2).astype(
        F32
    ) + lax.dynamic_slice_in_dim(gate_all, experts + dp_at * local, local, 2).astype(F32)
    gate_slot = jnp.sum(pick.astype(F32) * jnp.swapaxes(gate_tok, 1, 2)[:, :, None, :], axis=3)

    g_proj = jnp.einsum("gesd,edf->gesf", rows, gate_weight, preferred_element_type=F32)
    u_proj = jnp.einsum("gesd,edf->gesf", rows, up_weight, preferred_element_type=F32)
    d_act = jnp.einsum("gesd,efd->gesf", cots, down_weight, preferred_element_type=F32)
    sig = 1.0 / (1.0 + jnp.exp(-g_proj))
    silu = g_proj * sig
    act = silu * u_proj
    scaled = (act * gate_slot[..., None]).astype(BF)
    d_gate_slot = jnp.sum(act * d_act, axis=3)
    d_act = d_act * gate_slot[..., None]
    d_g = (d_act * u_proj * sig * (1.0 + g_proj * (1.0 - sig))).astype(BF)
    d_u = (d_act * silu).astype(BF)
    d_rows = (
        jnp.einsum("gesf,edf->gesd", d_g, gate_weight, preferred_element_type=F32)
        + jnp.einsum("gesf,edf->gesd", d_u, up_weight, preferred_element_type=F32)
    ).astype(BF)
    dg_high, dg_low = split2(d_gate_slot)
    column = jnp.arange(lanes(2 * experts))
    high_col = (column[None, :] == mine[:, None])[None, :, None, :]
    low_col = (column[None, :] == experts + mine[:, None])[None, :, None, :]
    extra = jnp.where(high_col, dg_high[..., None], jnp.where(low_col, dg_low[..., None], 0.0))
    d_rows = jnp.concatenate([d_rows, extra.astype(BF)], axis=3)
    d_sum = combine(pick, d_rows, dp, seq, None)

    y_rows = jnp.einsum("gesf,efd->gesd", scaled, down_weight, preferred_element_type=F32)
    y_sum = combine(pick, y_rows.astype(BF), dp, seq, d_sum)
    down_grad = jnp.einsum("gesf,gesd->efd", scaled, cots, preferred_element_type=F32)
    gate_grad = jnp.einsum("gesd,gesf->edf", rows, d_g, preferred_element_type=F32)
    up_grad = jnp.einsum("gesd,gesf->edf", rows, d_u, preferred_element_type=F32)

    return d_sum, y_sum, gate_grad, up_grad, down_grad


def pad_to(v, width):
    return jnp.pad(v, ((0, 0), (0, width - v.shape[1])))


def lanes(count):
    return -(-count // 128) * 128


def on_device(
    tokens,
    attn_gain,
    q_weight,
    key_matrix,
    value_matrix,
    o_weight,
    query_norm_gain,
    k_gain,
    ffn_gain,
    router_weight,
    gate_weight,
    up_weight,
    down_weight,
    expert_ids,
    cotangent,
):
    dp = lax.axis_size("dp")
    tensor = lax.axis_size("tensor")
    own, width = tokens.shape
    seq = expert_ids.shape[0]
    begin = lax.axis_index("tensor") * own
    local = gate_weight.shape[0]
    experts = local * dp
    slots = 10 * seq * expert_ids.shape[1] // (8 * experts)
    slots = -(-slots // 16) * 16
    shard = q_weight.shape[0]
    gshard = query_norm_gain.shape[0]
    hq = q_weight.shape[1] // HEAD
    hk = key_matrix.shape[1] // HEAD
    qkv_width = (hq + 2 * hk) * HEAD
    top = expert_ids.shape[1]
    fast = (dp, tensor, local, seq, width) == (16, 2, 2, 384, 2048)

    arange_e = jnp.arange(experts, dtype=jnp.int32)
    own_ids = lax.dynamic_slice_in_dim(expert_ids, begin, own, 0)
    own_mask = jnp.any(own_ids[:, :, None] == arange_e[None, None, :], axis=1)

    gain_rows = jnp.stack(
        [
            attn_gain,
            ffn_gain,
            jnp.pad(query_norm_gain, (0, shard - gshard)),
            jnp.pad(k_gain, (0, shard - gshard)),
        ],
        axis=1,
    )
    ids_rows = expert_ids.reshape(shard, -1).astype(BF)
    small = jnp.concatenate([router_weight, gain_rows, ids_rows], axis=1)
    small = pad_to(small, lanes(small.shape[1]))
    small_end = qkv_width + small.shape[1]
    all_in = gather_dp(
        jnp.concatenate([q_weight, key_matrix, value_matrix, small, o_weight.T], axis=1)
    )
    layer_in = gather_y(tokens)
    if fast:
        weights = jnp.concatenate([gate_weight, up_weight], axis=2)
        layer_in, weights = tied(layer_in, weights)
    o_t = all_in[:, small_end:]
    if fast:
        cot_all = gather_dp(gather_y(cotangent)).reshape(dp, seq, width)

    w_qkv = all_in[:, :qkv_width]
    router = all_in[:, qkv_width : qkv_width + experts]
    gains = all_in[:, qkv_width + experts : qkv_width + experts + 4].astype(F32)
    ids_all = all_in[:, qkv_width + experts + 4 :][:, : seq * top // shard]
    ids_all = ids_all.astype(jnp.int32).reshape(dp, seq, top)
    attn_gain32 = gains[:, 0]
    ffn_gain32 = gains[:, 1]
    q_gain32 = gains[:, 2].reshape(dp, shard)[:, :gshard].reshape(-1)
    k_gain32 = gains[:, 3].reshape(dp, shard)[:, :gshard].reshape(-1)

    residual = layer_in.astype(F32)
    normed = rms(residual, attn_gain32).astype(BF)
    qkv = dot(normed, w_qkv, 1, 0)
    cos, sin = rope_tables(seq)
    head_gains = jnp.pad(jnp.stack([q_gain32, k_gain32]), ((0, 6), (0, 0)))
    context = run_attend(qkv, head_gains, cos, sin, hq, hk)
    attn_part = dot(context, o_t, 1, 1)
    if fast:
        attn_part, ids_all = tied(attn_part, ids_all)
        plan = slot_plan(ids_all, experts)
    hidden = tokens.astype(F32) + scatter_y(attn_part)

    ffn_in = rms(hidden, ffn_gain32).astype(BF)
    logits = dot(ffn_in, router, 1, 0)
    chosen = jnp.where(own_mask, jnp.exp(logits), 0.0)
    gates = chosen / jnp.sum(chosen, axis=1, keepdims=True)
    gate_high, gate_low = split2(gates)
    gate_x = pad_to(jnp.concatenate([gate_high, gate_low], axis=1), lanes(2 * experts))
    args = (gate_weight, up_weight, down_weight)
    if fast:
        d_sum, y_sum, gate_later, up_grad, down_grad = moe_small(
            plan, cot_all, ffn_in, gate_x, weights, down_weight, slots
        )
    else:
        d_sum, y_sum, gate_grad, up_grad, down_grad = moe_large(
            ids_all, cotangent, ffn_in, gate_x, *args, experts, slots
        )
    d_gates = d_sum[:, width : width + experts] + d_sum[:, width + experts : width + 2 * experts]
    d_logits = gates * (d_gates - jnp.sum(gates * d_gates, axis=1, keepdims=True))
    d_high, d_low = split2(d_logits)
    d_ffn = d_sum[:, :width] + dot(d_high, router, 1, 1) + dot(d_low, router, 1, 1)
    router_part = dot(ffn_in, d_high, 0, 0) + dot(ffn_in, d_low, 0, 0)
    d_hidden, ffn_gain_rows = rms_back(hidden, ffn_gain32, d_ffn)
    ffn_gain_part = jnp.sum(ffn_gain_rows, axis=0)
    d_hidden = d_hidden + cotangent.astype(F32)
    d_attn = gather_y(d_hidden.astype(BF))

    o_part = dot(d_attn, context, 0, 0).astype(BF)
    d_attn, o_part = tied(d_attn, o_part)
    o_sum = scatter_dp(o_part).astype(F32)
    if fast:
        p1, p2, p5, p6 = y_sum
        d_attn, p1 = tied(d_attn, p1)
        p1 = step_y(p1)
        two5, two6 = first_hop(p5, 1), first_hop(p6, -1)
        gate_grad, d_attn = gate_later(d_attn)
    d_context = dot(d_attn, o_t, 1, 0).astype(BF)
    heads = []
    for head in range(hk):
        heads.append(run_attend_back(head, qkv, d_context, head_gains, cos, sin, hq, hk))
        if fast and head == 0:
            aside = (p1, p2, two5, two6, gate_grad)
            d_context, heads, aside = lax.optimization_barrier((d_context, heads, aside))
            p1, p2, two5, two6, gate_grad = aside
            p1 = step_x(p1)
            p2 = step_y(p2)
            p5 = reduce_z(p5, 1, two5)
            p6 = reduce_z(p6, -1, two6)
    d_qkv = jnp.concatenate([h[k] for k in range(3) for h in heads], axis=1)
    small_part = jnp.concatenate([router_part, ffn_gain_part[:, None]], axis=1)
    small_part = pad_to(small_part, lanes(experts + 3))
    column = jnp.arange(small_part.shape[1])[None, :]
    head_part = sum(h[3][0] for h in heads)[:, None] * (column == experts + 1).astype(F32)
    head_part += sum(h[3][1] for h in heads)[:, None] * (column == experts + 2).astype(F32)
    if fast:
        d_qkv, (p1, p2, p5, p6) = tied(d_qkv, (p1, p2, p5, p6))
        y_sum = (reduce_z(p1, 1), reduce_z(p2, -1), step_x(step_y(p5)), step_y(step_x(p6)))
        far = run_grad(plan[0][1], normed, d_qkv, small_part, head_part)
        near = run_grad(plan[0][0], normed, d_qkv, small_part, head_part)
        a, b = scatter_rows_core(near, far)
        qkv_sum = scatter_rows(a, b).astype(F32)
        qkv_sum, small_sum = qkv_sum[:, :qkv_width], qkv_sum[:, qkv_width:]
        y_sum = jnp.concatenate(y_sum, axis=1).astype(F32)
    else:
        qkv_sum = scatter_dp(dot(normed, d_qkv, 0, 0).astype(BF)).astype(F32)
        head_part = jnp.pad(
            head_part.reshape(dp, gshard, -1), ((0, 0), (0, shard - gshard), (0, 0))
        )
        small_sum = scatter_dp(small_part + head_part.reshape(small_part.shape))
    output = (hidden + y_sum).astype(BF)
    d_normed = dot(d_qkv, w_qkv, 1, 1)
    d_normed = scatter_y(d_normed)
    d_tokens, _ = rms_back(tokens.astype(F32), attn_gain32, d_normed)
    tokens_grad = d_tokens + d_hidden

    weights = jnp.concatenate([q_weight, key_matrix, value_matrix], axis=1).astype(F32)
    gain_part = jnp.sum(weights * qkv_sum, axis=1) / attn_gain.astype(F32)
    small_sum = jnp.concatenate([small_sum, gain_part[:, None]], axis=1)
    small_sum = small_sum + swap_y(small_sum)
    return (
        output,
        tokens_grad,
        small_sum[:, -1],
        qkv_sum[:, : hq * HEAD],
        qkv_sum[:, hq * HEAD : (hq + hk) * HEAD],
        qkv_sum[:, (hq + hk) * HEAD :],
        o_sum.T,
        small_sum[:gshard, experts + 1],
        small_sum[:gshard, experts + 2],
        small_sum[:, experts],
        small_sum[:, :experts],
        gate_grad,
        up_grad,
        down_grad,
    )


def solution(mesh):
    rows = P(("dp", "tensor"), None)
    both = P("dp", "tensor")
    return jax.shard_map(
        on_device,
        mesh=mesh,
        in_specs=(
            rows,
            P("dp"),
            both,
            both,
            both,
            P("tensor", "dp"),
            P("dp"),
            P("dp"),
            P("dp"),
            P("dp", None),
            P("dp", None, "tensor"),
            P("dp", None, "tensor"),
            P("dp", "tensor", None),
            P("dp", None),
            rows,
        ),
        out_specs=(
            rows,
            rows,
            P("dp"),
            both,
            both,
            both,
            P("tensor", "dp"),
            P("dp"),
            P("dp"),
            P("dp"),
            P("dp", None),
            P("dp", None, "tensor"),
            P("dp", None, "tensor"),
            P("dp", "tensor", None),
        ),
        check_vma=False,
    )
```

profile of v0, /device:TPU:0, one launch (start us, length us, event | category | flops | bytes accessed | tf_op | source)
XLA Modules:
  0.0 1008.3 jit_solution(2774262289317695912)
XLA Ops:
  14.7 17.5 %collective-permute-done.18 = bf16[192,2048]{1,0:T(8,128)(2,1)S(1)} collective-permute-done((bf16[192,2048]{1,0:T(8,128)(2,1)S(1)}, bf16[192,2048]{1,0:T(8,128)(2,1)S(1)}, u32[]{:S(2)}, u32[]{:S(2)}) %collective-permute-start.18) | collective-permute-done | bytes 786464 | tf_op jit(solution)/shard_map/ppermute | solution.py:248
  45.1 7.7 collective-permute-done
  54.6 68.0 %all-gather.3.cloned.1.call-done = bf16[2048,4736]{0,1:T(8,128)(2,1)} async-done(((bf16[128,4736]{0,1:T(8,128)(2,1)}), bf16[2048,4736]{0,1:T(8,128)(2,1)}) %all-gather.3.cloned.1.call-update) | async-done | bytes 19398672 | tf_op jit(solution)/shard_map/all_gather | solution.py:177
  128.6 10.9 %fusion.2.q_raw.k_raw.v_raw = f32[384,2560]{1,0:T(8,128)} fusion(bf16[384,2048]{1,0:T(8,128)(2,1)S(1)} %fusion.14.left, bf16[2048,4736]{0,1:T(8,128)(2,1)} %all-gather.3.cloned.1.call-done), kind=kOutput, calls=%fused_computation.7 | convolution fusion | flops 4026531840 | bytes 15990784 | tf_op jit(solution)/shard_map/dot_general | solution.py:17
  139.5 14.4 %attend.1 = bf16[384,2048]{1,0:T(8,128)(2,1)} custom-call(f32[384,2560]{1,0:T(8,128)} %fusion.2.q_raw.k_raw.v_raw, f32[384,2560]{1,0:T(8,128)} %fusion.2.q_raw.k_raw.v_raw, f32[384,2560]{1,0:T(8,128)} %fusion.2.q_raw.k_raw.v_raw, f32[8,128]{1,0:T(8,128)} %select_maximum_fusion.gains, f32[384,128]{1,0:T(8,128)} %get-tuple-element.415.cos, ...), custom_call_target="tpu_custom_call" | custom-call | tf_op jit(solution)/shard_map/attend/pallas_call | solution.py:120
  153.9 9.1 fusion.6
  185.3 13.7 %collective-permute-done.1 = bf16[192,2048]{1,0:T(8,128)(2,1)S(1)} collective-permute-done((bf16[192,2048]{1,0:T(8,128)(2,1)S(1)}, bf16[192,2048]{1,0:T(8,128)(2,1)S(1)}, u32[]{:S(2)}, u32[]{:S(2)}) %collective-permute-start.1) | collective-permute-done | bytes 786464 | tf_op jit(solution)/shard_map/ppermute | solution.py:248
  213.6 7.1 collective-permute-done.6
  225.6 20.9 %collective-permute-done.2 = bf16[192,768]{1,0:T(8,128)(2,1)S(1)} collective-permute-done((bf16[192,768]{1,0:T(8,128)(2,1)S(1)}, bf16[192,768]{1,0:T(8,128)(2,1)S(1)}, u32[]{:S(2)}, u32[]{:S(2)}) %collective-permute-start.2) | collective-permute-done | bytes 294944 | tf_op jit(solution)/shard_map/ppermute | solution.py:236
  248.0 9.2 collective-permute-done.7
  258.4 11.5 %collective-permute-done.4 = bf16[192,768]{1,0:T(8,128)(2,1)S(1)} collective-permute-done((bf16[192,768]{1,0:T(8,128)(2,1)S(1)}, bf16[192,768]{1,0:T(8,128)(2,1)S(1)}, u32[]{:S(2)}, u32[]{:S(2)}) %collective-permute-start.4) | collective-permute-done | bytes 294944 | tf_op jit(solution)/shard_map/ppermute | solution.py:236
  269.9 13.9 %collective-permute-done.3 = bf16[192,768]{1,0:T(8,128)(2,1)S(1)} collective-permute-done((bf16[192,768]{1,0:T(8,128)(2,1)S(1)}, bf16[192,768]{1,0:T(8,128)(2,1)S(1)}, u32[]{:S(2)}, u32[]{:S(2)}) %collective-permute-start.3) | collective-permute-done | bytes 294944 | tf_op jit(solution)/shard_map/ppermute | solution.py:236
  291.0 8.9 collective-permute-done.14
  301.7 15.7 %cots.2 = (bf16[2,4,256,2048]{3,2,1,0:T(8,128)(2,1)}, f32[2,4,256,384]{3,2,1,0:T(8,128)}) custom-call(s32[8]{0:T(128)} %get-tuple-element.149.where, f32[8,2,384]{2,1,0:T(2,128)} %copy.119.rank, bf16[16,384,2048]{2,1,0:T(8,128)(2,1)} %bitcast.320, bf16[16,384,2048]{2,1,0:T(8,128)(2,1)} %bitcast.321, bf16[2,384,2048]{2,1,0:T(8,128)(2,1)} %down.7), custom_call_target="tpu_custom_call" | custom-call | tf_op jit(solution)/shard_map/cots/pallas_call | solution.py:551
  317.5 12.0 %collective-permute-done.15 = bf16[2,2,192,256]{3,2,1,0:T(8,128)(2,1)} collective-permute-done((bf16[2,2,192,256]{3,2,1,0:T(8,128)(2,1)S(1)}, bf16[2,2,192,256]{3,2,1,0:T(8,128)(2,1)}, u32[]{:S(2)}, u32[]{:S(2)}) %collective-permute-start.15) | collective-permute-done | bytes 393248 | tf_op jit(solution)/shard_map/ppermute | solution.py:236
  342.5 19.5 %collective-permute-done.20 = bf16[2,2,192,256]{3,2,1,0:T(8,128)(2,1)S(1)} collective-permute-done((bf16[2,2,192,256]{3,2,1,0:T(8,128)(2,1)}, bf16[2,2,192,256]{3,2,1,0:T(8,128)(2,1)S(1)}, u32[]{:S(2)}, u32[]{:S(2)}) %collective-permute-start.20) | collective-permute-done | bytes 393248 | tf_op jit(solution)/shard_map/ppermute | solution.py:236
  367.1 16.1 %cots.3 = (bf16[2,4,256,2048]{3,2,1,0:T(8,128)(2,1)}, f32[2,4,256,384]{3,2,1,0:T(8,128)}) custom-call(s32[8]{0:T(128)} %get-tuple-element.172.where, f32[8,2,384]{2,1,0:T(2,128)} %copy.120.rank, bf16[16,384,2048]{2,1,0:T(8,128)(2,1)} %bitcast.322, bf16[16,384,2048]{2,1,0:T(8,128)(2,1)} %bitcast.323, bf16[2,384,2048]{2,1,0:T(8,128)(2,1)} %down.7), custom_call_target="tpu_custom_call" | custom-call | tf_op jit(solution)/shard_map/cots/pallas_call | solution.py:551
  398.1 34.5 %experts.3 = (bf16[2,4,256,2048]{3,2,1,0:T(8,128)(2,1)}, bf16[2,4,256,384]{3,2,1,0:T(8,128)(2,1)}, bf16[2,4,256,384]{3,2,1,0:T(8,128)(2,1)}, bf16[2,4,256,384]{3...) custom-call(f32[8,2,384]{2,1,0:T(2,128)} %copy.122.rank, ...), custom_call_target="tpu_custom_call" | custom-call | tf_op jit(solution)/shard_map/experts/pallas_call | solution.py:574
  434.8 34.9 %experts.2 = (bf16[2,4,256,2048]{3,2,1,0:T(8,128)(2,1)}, bf16[2,4,256,384]{3,2,1,0:T(8,128)(2,1)}, bf16[2,4,256,384]{3,2,1,0:T(8,128)(2,1)}, bf16[2,4,256,384]{3...) custom-call(f32[8,2,384]{2,1,0:T(2,128)} %copy.121.rank, ...), custom_call_target="tpu_custom_call" | custom-call | tf_op jit(solution)/shard_map/experts/pallas_call | solution.py:574
  469.7 12.4 %outs.2 = (bf16[2,2,4,192,768]{4,3,2,1,0:T(8,128)(2,1)}, bf16[2,2,4,192,768]{4,3,2,1,0:T(8,128)(2,1)}, bf16[4,2,2,192,256]{4,3,2,1,0:T(8,128)(2,1)}, bf16[4,2,2,192,256]{4,3,2,1,0:T(8,128)(2,1)}) custom-call(f32[8,384,2]{2,1,0:T(8,128)} %get-tuple-element.168.rank_t, bf16[2,4,256,384]{3,2,1,0:T(8,128)(2,1)} %get-tuple-element.201.scaled, ...), custom_call_target="tpu_custom_call" | custom-call | tf_op jit(solution)/shard_map/outs/pallas_call | solution.py:614
  488.8 11.2 %fusion.125 = f32[2,2048,384,1]{2,1,3,0:T(8,128)} fusion(bf16[2,4,256,2048]{3,2,1,0:T(8,128)(2,1)} %get-tuple-element.246, bf16[2,4,256,384]{3,2,1,0:T(8,128)(2,1)} %get-tuple-element.217), kind=kOutput, calls=%fused_computation.379 | convolution fusion | flops 3221225472 | bytes 16252928 | tf_op jit(solution)/shard_map/egsd,egsf->edf/dot_general | solution.py:668
  528.7 7.6 collective-permute-done.35
  541.6 9.6 bitcast_add_fusion.2
  551.2 12.5 %outs.3 = (bf16[2,2,4,192,768]{4,3,2,1,0:T(8,128)(2,1)}, bf16[2,2,4,192,768]{4,3,2,1,0:T(8,128)(2,1)}, bf16[4,2,2,192,256]{4,3,2,1,0:T(8,128)(2,1)}, bf16[4,2,2,192,256]{4,3,2,1,0:T(8,128)(2,1)}) custom-call(f32[8,384,2]{2,1,0:T(8,128)} %get-tuple-element.188.rank_t, bf16[2,4,256,384]{3,2,1,0:T(8,128)(2,1)} %get-tuple-element.206.scaled, ...), custom_call_target="tpu_custom_call" | custom-call | tf_op jit(solution)/shard_map/outs/pallas_call | solution.py:614
  587.4 13.0 %bitcast_add_fusion.1 = f32[2,2048,384]{2,1,0:T(8,128)} fusion(f32[2,2048,384,1]{2,1,3,0:T(8,128)} %fusion.125, bf16[2,4,256,2048]{3,2,1,0:T(8,128)(2,1)} %get-tuple-element.248, bf16[2,4,256,384]{3,2,1,0:T(8,128)(2,1)} %get-tuple-element.218), kind=kOutput, calls=%fused_computation.16 | convolution fusion | flops 3222798336 | bytes 22544384 | tf_op jit(solution)/shard_map/egsd,egsf->edf/dot_general | solution.py:668
  603.6 10.9 %collective-permute-done.42 = bf16[4,192,768]{2,1,0:T(8,128)(2,1)S(1)} collective-permute-done((bf16[4,192,768]{2,1,0:T(8,128)(2,1)}, bf16[4,192,768]{2,1,0:T(8,128)(2,1)S(1)}, u32[]{:S(2)}, u32[]{:S(2)}) %collective-permute-start.42) | collective-permute-done | bytes 1179680 | tf_op jit(solution)/shard_map/ppermute | solution.py:248
  626.5 10.1 %collective-permute-done.49 = bf16[192,768]{1,0:T(8,128)(2,1)S(1)} collective-permute-done((bf16[192,768]{1,0:T(8,128)(2,1)S(1)}, bf16[192,768]{1,0:T(8,128)(2,1)S(1)}, u32[]{:S(2)}, u32[]{:S(2)}) %collective-permute-start.49) | collective-permute-done | bytes 294944 | tf_op jit(solution)/shard_map/ppermute | solution.py:236
  636.8 6.9 collective-permute-done.46
  648.2 7.1 collective-permute-done.45
  660.1 8.6 collective-permute-done.47
  674.4 7.6 add_convert_fusion
  721.3 8.0 fusion.16.d_context
  729.3 12.6 %attend_back.2 = (bf16[384,1024]{1,0:T(8,128)(2,1)}, bf16[384,128]{1,0:T(8,128)(2,1)}, bf16[384,128]{1,0:T(8,128)(2,1)}, f32[8,128]{1,0:T(8,128)}) custom-call(f32[384,2560]{1,0:T(8,128)} %fusion.2.q_raw.k_raw.v_raw, f32[384,2560]{1,0:T(8,128)} %fusion.2.q_raw.k_raw.v_raw, f32[384,2560]{1,0:T(8,128)} %fusion.2.q_raw.k_raw.v_raw, ...), custom_call_target="tpu_custom_call" | custom-call | tf_op jit(solution)/shard_map/attend_back/pallas_call | solution.py:143
  742.0 11.6 %fusion.126 = f32[2,2048,384,1]{2,1,3,0:T(8,128)} fusion(bf16[2,4,256,2048]{3,2,1,0:T(8,128)(2,1)} %get-tuple-element.246, bf16[2,4,256,384]{3,2,1,0:T(8,128)(2,1)} %get-tuple-element.247), kind=kOutput, calls=%fused_computation.380 | convolution fusion | flops 3221225472 | bytes 16252928 | tf_op jit(solution)/shard_map/egsd,egsf->edf/dot_general | solution.py:668
  753.6 14.5 %bitcast_add_fusion = f32[2,2048,384]{2,1,0:T(8,128)} fusion(f32[2,2048,384,1]{2,1,3,0:T(8,128)} %fusion.126, bf16[2,4,256,2048]{3,2,1,0:T(8,128)(2,1)} %get-tuple-element.248, bf16[2,4,256,384]{3,2,1,0:T(8,128)(2,1)} %get-tuple-element.249), kind=kOutput, calls=%fused_computation.15 | convolution fusion | flops 3222798336 | bytes 22544384 | tf_op jit(solution)/shard_map/egsd,egsf->edf/dot_general | solution.py:668
  777.1 12.7 %attend_back.3 = (bf16[384,1024]{1,0:T(8,128)(2,1)}, bf16[384,128]{1,0:T(8,128)(2,1)}, bf16[384,128]{1,0:T(8,128)(2,1)}, f32[8,128]{1,0:T(8,128)}) custom-call(f32[384,2560]{1,0:T(8,128)} %fusion.2.q_raw.k_raw.v_raw, f32[384,2560]{1,0:T(8,128)} %fusion.2.q_raw.k_raw.v_raw, f32[384,2560]{1,0:T(8,128)} %fusion.2.q_raw.k_raw.v_raw, ...), custom_call_target="tpu_custom_call" | custom-call | tf_op jit(solution)/shard_map/attend_back/pallas_call | solution.py:143
  801.4 11.8 %collective-permute-done.67 = bf16[2,2,192,256]{3,2,1,0:T(8,128)(2,1)S(1)} collective-permute-done((bf16[2,2,192,256]{3,2,1,0:T(8,128)(2,1)S(1)}, bf16[2,2,192,256]{3,2,1,0:T(8,128)(2,1)S(1)}, u32[]{:S(2)}, u32[]{:S(2)}) %collective-permute-start.67) | collective-permute-done | bytes 393248 | tf_op jit(solution)/shard_map/ppermute | solution.py:236
  814.5 15.0 %collective-permute-done.65 = bf16[2,2,192,256]{3,2,1,0:T(8,128)(2,1)S(1)} collective-permute-done((bf16[2,2,192,256]{3,2,1,0:T(8,128)(2,1)S(1)}, bf16[2,2,192,256]{3,2,1,0:T(8,128)(2,1)S(1)}, u32[]{:S(2)}, u32[]{:S(2)}) %collective-permute-start.65) | collective-permute-done | bytes 393248 | tf_op jit(solution)/shard_map/ppermute | solution.py:236
  833.5 9.2 grad.3
  850.6 6.9 fusion
  859.3 9.3 grad.2
  875.6 9.0 collective-permute-done.72
  888.2 16.8 %collective-permute-done.77 = bf16[192,256]{1,0:T(8,128)(2,1)S(1)} collective-permute-done((bf16[192,256]{1,0:T(8,128)(2,1)S(1)}, bf16[192,256]{1,0:T(8,128)(2,1)S(1)}, u32[]{:S(2)}, u32[]{:S(2)}) %collective-permute-start.77) | collective-permute-done | bytes 98336 | tf_op jit(solution)/shard_map/ppermute | solution.py:248
  908.2 8.6 collective-permute-done.71
  929.1 11.7 %collective-permute-done.86 = bf16[2,128,1280]{2,1,0:T(8,128)(2,1)S(1)} collective-permute-done((bf16[2,128,1280]{2,1,0:T(8,128)(2,1)S(1)}, bf16[2,128,1280]{2,1,0:T(8,128)(2,1)S(1)}, u32[]{:S(2)}, u32[]{:S(2)}) %collective-permute-start.86) | collective-permute-done | bytes 655392 | tf_op jit(solution)/shard_map/ppermute | solution.py:236
  941.0 7.9 collective-permute-start.87
  953.8 11.5 %collective-permute-done.87 = bf16[2,128,1280]{2,1,0:T(8,128)(2,1)S(1)} collective-permute-done((bf16[2,128,1280]{2,1,0:T(8,128)(2,1)S(1)}, bf16[2,128,1280]{2,1,0:T(8,128)(2,1)S(1)}, u32[]{:S(2)}, u32[]{:S(2)}) %collective-permute-start.87) | collective-permute-done | bytes 655392 | tf_op jit(solution)/shard_map/ppermute | solution.py:236
  969.6 11.6 %collective-permute-done.82 = bf16[128,1408]{1,0:T(8,128)(2,1)S(1)} collective-permute-done((bf16[128,1408]{1,0:T(8,128)(2,1)S(1)}, bf16[128,1408]{1,0:T(8,128)(2,1)S(1)}, u32[]{:S(2)}, u32[]{:S(2)}) %collective-permute-start.82) | collective-permute-done | bytes 360480 | tf_op jit(solution)/shard_map/ppermute | solution.py:236
  (547 shorter events, 340.3 us)
Async XLA Ops:
  7.3 115.3 %all-gather.3.cloned.1.call-start = ((), (), s32[]{:S(2)}) async-start(), calls=%async_computation.1 | async-start | bytes 20611072 | tf_op jit(solution)/shard_map/all_gather | solution.py:177
  11.6 290.2 %all-gather.5.cloned.1.call-start = ((), (), s32[]{:S(2)}) async-start(), calls=%async_computation.2 | async-start | bytes 26738688 | tf_op jit(solution)/shard_map/all_gather | solution.py:177
  33.7 965.2 %reduce-scatter.2.cloned.1.call-start = ((), (), s32[]{:S(2)}) async-start(), calls=%async_computation.3 | async-start | bytes 8912896 | tf_op jit(solution)/shard_map/reduce_scatter | solution.py:189
  207.6 40.4 %collective-permute-start.5 = (bf16[192,768]{1,0:T(8,128)(2,1)S(1)}, bf16[192,768]{1,0:T(8,128)(2,1)S(1)}, u32[]{:S(2)}, u32[]{:S(2)}) collective-permute-start(bf16[192,768]{1,0:T(8,128)(2,1)S(1)} %get-tuple-element.385), channel_id=1, source_target_pairs={{0,8},{2,10},{4,12},{6,14},{8,16},{10,18},{12,20},{14,22},{16,24},... | collective-permute-start | bytes 884744 | tf_op jit(solution)/shard_map/ppermute | solution.py:236
  208.7 37.8 %collective-permute-start.2 = (bf16[192,768]{1,0:T(8,128)(2,1)S(1)}, bf16[192,768]{1,0:T(8,128)(2,1)S(1)}, u32[]{:S(2)}, u32[]{:S(2)}) collective-permute-start(bf16[192,768]{1,0:T(8,128)(2,1)S(1)} %get-tuple-element.386), channel_id=1, source_target_pairs={{0,8},{2,10},{4,12},{6,14},{8,16},{10,18},{12,20},{14,22},{16,24},... | collective-permute-start | bytes 884744 | tf_op jit(solution)/shard_map/ppermute | solution.py:236
  213.1 34.0 %collective-permute-start.9 = (bf16[2,192,384]{2,1,0:T(8,128)(2,1)S(1)}, bf16[2,192,384]{2,1,0:T(8,128)(2,1)S(1)}, u32[]{:S(2)}, u32[]{:S(2)}) collective-permute-start(bf16[2,192,384]{2,1,0:T(8,128)(2,1)S(1)} %get-tuple-element.390), channel_id=1, source_target_pairs={{0,1},{1,0},{2,3},{3,2},{4,5},{5,4},{6,7},{7,6},{8,9},{9,8},{10,11... | collective-permute-start | bytes 884744 | tf_op jit(solution)/shard_map/ppermute | solution.py:248
  220.7 36.5 %collective-permute-start.7 = (bf16[192,768]{1,0:T(8,128)(2,1)S(1)}, bf16[192,768]{1,0:T(8,128)(2,1)S(1)}, u32[]{:S(2)}, u32[]{:S(2)}) collective-permute-start(bf16[192,768]{1,0:T(8,128)(2,1)S(1)} %collective-permute-done.6), channel_id=1, source_target_pairs={{0,24},{2,26},{4,28},{6,30},{8,0},{10,2},{12,4},{14,6},{16,8},{18,... | collective-permute-start | bytes 884744 | tf_op jit(solution)/shard_map/ppermute | solution.py:236
  225.5 44.3 %collective-permute-start.4 = (bf16[192,768]{1,0:T(8,128)(2,1)S(1)}, bf16[192,768]{1,0:T(8,128)(2,1)S(1)}, u32[]{:S(2)}, u32[]{:S(2)}) collective-permute-start(bf16[192,768]{1,0:T(8,128)(2,1)S(1)} %get-tuple-element.386), channel_id=1, source_target_pairs={{0,24},{2,26},{4,28},{6,30},{8,0},{10,2},{12,4},{14,6},{16,8},{18,... | collective-permute-start | bytes 884744 | tf_op jit(solution)/shard_map/ppermute | solution.py:236
  246.5 37.3 %collective-permute-start.3 = (bf16[192,768]{1,0:T(8,128)(2,1)S(1)}, bf16[192,768]{1,0:T(8,128)(2,1)S(1)}, u32[]{:S(2)}, u32[]{:S(2)}) collective-permute-start(bf16[192,768]{1,0:T(8,128)(2,1)S(1)} %collective-permute-done.2), channel_id=1, source_target_pairs={{0,8},{2,10},{4,12},{6,14},{8,16},{10,18},{12,20},{14,22},{16,24},... | collective-permute-start | bytes 884744 | tf_op jit(solution)/shard_map/ppermute | solution.py:236
  285.0 44.5 %collective-permute-start.16 = (bf16[4,192,768]{2,1,0:T(8,128)(2,1)}, bf16[4,192,768]{2,1,0:T(8,128)(2,1)}, u32[]{:S(2)}, u32[]{:S(2)}) collective-permute-start(bf16[4,192,768]{2,1,0:T(8,128)(2,1)} %pad_maximum_fusion.8), channel_id=1, source_target_pairs={{0,4},{2,6},{4,0},{6,2},{8,12},{10,14},{12,8},{14,10},{16,20},{18,... | collective-permute-start | bytes 3538952 | tf_op jit(solution)/shard_map/ppermute | solution.py:240
  285.5 44.0 %collective-permute-start.17 = (bf16[4,192,768]{2,1,0:T(8,128)(2,1)}, bf16[4,192,768]{2,1,0:T(8,128)(2,1)}, u32[]{:S(2)}, u32[]{:S(2)}) collective-permute-start(bf16[4,192,768]{2,1,0:T(8,128)(2,1)} %pad_maximum_fusion.9), channel_id=1, source_target_pairs={{0,1},{1,0},{2,3},{3,2},{4,5},{5,4},{6,7},{7,6},{8,9},{9,8},{10,11... | collective-permute-start | bytes 3538952 | tf_op jit(solution)/shard_map/ppermute | solution.py:248
  287.2 42.4 %collective-permute-start.12 = (bf16[2,2,192,384]{3,2,1,0:T(8,128)(2,1)}, bf16[2,2,192,384]{3,2,1,0:T(8,128)(2,1)}, u32[]{:S(2)}, u32[]{:S(2)}) collective-permute-start(bf16[2,2,192,384]{3,2,1,0:T(8,128)(2,1)} %pad_maximum_fusion.10), channel_id=1, source_target_pairs={{0,8},{2,10},{4,12},{6,14},{8,16},{10,18},{12,20},{14,22},{16,24},... | collective-permute-start | bytes 1769480 | tf_op jit(solution)/shard_map/ppermute | solution.py:236
  287.2 42.3 %collective-permute-start.13 = (bf16[2,2,192,384]{3,2,1,0:T(8,128)(2,1)}, bf16[2,2,192,384]{3,2,1,0:T(8,128)(2,1)}, u32[]{:S(2)}, u32[]{:S(2)}) collective-permute-start(bf16[2,2,192,384]{3,2,1,0:T(8,128)(2,1)} %pad_maximum_fusion.10), channel_id=1, source_target_pairs={{0,24},{2,26},{4,28},{6,30},{8,0},{10,2},{12,4},{14,6},{16,8},{18,... | collective-permute-start | bytes 1769480 | tf_op jit(solution)/shard_map/ppermute | solution.py:236
  300.7 28.9 %collective-permute-start.15 = (bf16[2,2,192,256]{3,2,1,0:T(8,128)(2,1)S(1)}, bf16[2,2,192,256]{3,2,1,0:T(8,128)(2,1)}, u32[]{:S(2)}, u32[]{:S(2)}) collective-permute-start(bf16[2,2,192,256]{3,2,1,0:T(8,128)(2,1)S(1)} %pad_maximum_fusion.11), channel_id=1, source_target_pairs={{0,24},{2,26},{4,28},{6,30},{8,0},{10,2},{12,4},{14,6},{16,8},{18,... | collective-permute-start | bytes 1179656 | tf_op jit(solution)/shard_map/ppermute | solution.py:236
  332.9 53.6 %collective-permute-start.22 = (bf16[2,4,192,768]{3,2,1,0:T(8,128)(2,1)}, bf16[2,4,192,768]{3,2,1,0:T(8,128)(2,1)}, u32[]{:S(2)}, u32[]{:S(2)}) collective-permute-start(bf16[2,4,192,768]{3,2,1,0:T(8,128)(2,1)} %pad_maximum_fusion.2.x2a), channel_id=1, source_target_pairs={{0,4},{2,6},{4,0},{6,2},{8,12},{10,14},{12,8},{14,10},{16,20},{18,... | collective-permute-start | bytes 7077896 | tf_op jit(solution)/shard_map/ppermute | solution.py:240
  337.2 51.4 %collective-permute-start.21 = (bf16[2,4,192,768]{3,2,1,0:T(8,128)(2,1)}, bf16[2,4,192,768]{3,2,1,0:T(8,128)(2,1)}, u32[]{:S(2)}, u32[]{:S(2)}) collective-permute-start(bf16[2,4,192,768]{3,2,1,0:T(8,128)(2,1)} %pad_maximum_fusion.1.x1a), channel_id=1, source_target_pairs={{0,1},{1,0},{2,3},{3,2},{4,5},{5,4},{6,7},{7,6},{8,9},{9,8},{10,11... | collective-permute-start | bytes 7077896 | tf_op jit(solution)/shard_map/ppermute | solution.py:248
  364.1 27.4 %collective-permute-start.25 = (bf16[2,4,192,768]{3,2,1,0:T(8,128)(2,1)}, bf16[2,4,192,768]{3,2,1,0:T(8,128)(2,1)}, u32[]{:S(2)}, u32[]{:S(2)}) collective-permute-start(bf16[2,4,192,768]{3,2,1,0:T(8,128)(2,1)} %pad_maximum_fusion.2.x2a), channel_id=1, source_target_pairs={{0,2},{2,0},{4,6},{6,4},{8,10},{10,8},{12,14},{14,12},{16,18},{18,... | collective-permute-start | bytes 7077896 | tf_op jit(solution)/shard_map/ppermute | solution.py:244
  432.6 78.7 %collective-permute-start.31 = (bf16[2,2,4,192,768]{4,3,2,1,0:T(8,128)(2,1)}, bf16[2,2,4,192,768]{4,3,2,1,0:T(8,128)(2,1)}, u32[]{:S(2)}, u32[]{:S(2)}) collective-permute-start(bf16[2,2,4,192,768]{4,3,2,1,0:T(8,128)(2,1)} %get-tuple-element.196), channel_id=1, source_target_pairs={{0,2},{2,0},{4,6},{6,4},{8,10},{10,8},{12,14},{14,12},{16,18},{18,... | collective-permute-start | bytes 14155784 | tf_op jit(solution)/shard_map/ppermute | solution.py:244
  433.1 84.1 %collective-permute-start.29 = (bf16[2,2,4,192,768]{4,3,2,1,0:T(8,128)(2,1)}, bf16[2,2,4,192,768]{4,3,2,1,0:T(8,128)(2,1)}, u32[]{:S(2)}, u32[]{:S(2)}) collective-permute-start(bf16[2,2,4,192,768]{4,3,2,1,0:T(8,128)(2,1)} %get-tuple-element.194), channel_id=1, source_target_pairs={{0,2},{2,0},{4,6},{6,4},{8,10},{10,8},{12,14},{14,12},{16,18},{18,... | collective-permute-start | bytes 14155784 | tf_op jit(solution)/shard_map/ppermute | solution.py:244
  504.0 34.7 %collective-permute-start.38 = (bf16[2,2,192,256]{3,2,1,0:T(8,128)(2,1)}, bf16[2,2,192,256]{3,2,1,0:T(8,128)(2,1)S(1)}, u32[]{:S(2)}, u32[]{:S(2)}) collective-permute-start(bf16[2,2,192,256]{3,2,1,0:T(8,128)(2,1)} %get-tuple-element.364), channel_id=1, source_target_pairs={{0,24},{2,26},{4,28},{6,30},{8,0},{10,2},{12,4},{14,6},{16,8},{18,... | collective-permute-start | bytes 1179656 | tf_op jit(solution)/shard_map/ppermute | solution.py:236
  509.3 27.0 %collective-permute-start.35 = (bf16[2,2,192,384]{3,2,1,0:T(8,128)(2,1)}, bf16[2,2,192,384]{3,2,1,0:T(8,128)(2,1)}, u32[]{:S(2)}, u32[]{:S(2)}) collective-permute-start(bf16[2,2,192,384]{3,2,1,0:T(8,128)(2,1)} %get-tuple-element.355), channel_id=1, source_target_pairs={{0,24},{2,26},{4,28},{6,30},{8,0},{10,2},{12,4},{14,6},{16,8},{18,... | collective-permute-start | bytes 1769480 | tf_op jit(solution)/shard_map/ppermute | solution.py:236
  516.9 54.6 %collective-permute-start.32 = (bf16[2,4,192,768]{3,2,1,0:T(8,128)(2,1)}, bf16[2,4,192,768]{3,2,1,0:T(8,128)(2,1)}, u32[]{:S(2)}, u32[]{:S(2)}) collective-permute-start(bf16[2,4,192,768]{3,2,1,0:T(8,128)(2,1)} %slice_bitcast_fusion), channel_id=1, source_target_pairs={{0,4},{2,6},{4,0},{6,2},{8,12},{10,14},{12,8},{14,10},{16,20},{18,... | collective-permute-start | bytes 7077896 | tf_op jit(solution)/shard_map/ppermute | solution.py:240
  525.5 53.0 %collective-permute-start.30 = (bf16[2,4,192,768]{3,2,1,0:T(8,128)(2,1)}, bf16[2,4,192,768]{3,2,1,0:T(8,128)(2,1)}, u32[]{:S(2)}, u32[]{:S(2)}) collective-permute-start(bf16[2,4,192,768]{3,2,1,0:T(8,128)(2,1)} %slice_bitcast_fusion.2), channel_id=1, source_target_pairs={{0,1},{1,0},{2,3},{3,2},{4,5},{5,4},{6,7},{7,6},{8,9},{9,8},{10,11... | collective-permute-start | bytes 7077896 | tf_op jit(solution)/shard_map/ppermute | solution.py:248
  527.8 35.9 %collective-permute-start.40 = (bf16[2,2,192,256]{3,2,1,0:T(8,128)(2,1)}, bf16[2,2,192,256]{3,2,1,0:T(8,128)(2,1)}, u32[]{:S(2)}, u32[]{:S(2)}) collective-permute-start(bf16[2,2,192,256]{3,2,1,0:T(8,128)(2,1)} %fusion.41), channel_id=1, source_target_pairs={{0,8},{2,10},{4,12},{6,14},{8,16},{10,18},{12,20},{14,22},{16,24},... | collective-permute-start | bytes 1179656 | tf_op jit(solution)/shard_map/ppermute | solution.py:236
  536.3 28.6 %collective-permute-start.34 = (bf16[2,2,192,384]{3,2,1,0:T(8,128)(2,1)}, bf16[2,2,192,384]{3,2,1,0:T(8,128)(2,1)S(1)}, u32[]{:S(2)}, u32[]{:S(2)}) collective-permute-start(bf16[2,2,192,384]{3,2,1,0:T(8,128)(2,1)} %get-tuple-element.354), channel_id=1, source_target_pairs={{0,8},{2,10},{4,12},{6,14},{8,16},{10,18},{12,20},{14,22},{16,24},... | collective-permute-start | bytes 1769480 | tf_op jit(solution)/shard_map/ppermute | solution.py:236
  538.7 31.5 %collective-permute-start.36 = (bf16[2,2,192,384]{3,2,1,0:T(8,128)(2,1)S(1)}, bf16[2,2,192,384]{3,2,1,0:T(8,128)(2,1)S(1)}, u32[]{:S(2)}, u32[]{:S(2)}) collective-permute-start(bf16[2,2,192,384]{3,2,1,0:T(8,128)(2,1)S(1)} %fusion.31), channel_id=1, source_target_pairs={{0,24},{2,26},{4,28},{6,30},{8,0},{10,2},{12,4},{14,6},{16,8},{18,... | collective-permute-start | bytes 1769480 | tf_op jit(solution)/shard_map/ppermute | solution.py:236
  583.8 30.7 %collective-permute-start.42 = (bf16[4,192,768]{2,1,0:T(8,128)(2,1)}, bf16[4,192,768]{2,1,0:T(8,128)(2,1)S(1)}, u32[]{:S(2)}, u32[]{:S(2)}) collective-permute-start(bf16[4,192,768]{2,1,0:T(8,128)(2,1)} %slice_bitcast_fusion.10), channel_id=1, source_target_pairs={{0,1},{1,0},{2,3},{3,2},{4,5},{5,4},{6,7},{7,6},{8,9},{9,8},{10,11... | collective-permute-start | bytes 3538952 | tf_op jit(solution)/shard_map/ppermute | solution.py:248
  586.5 28.3 %collective-permute-start.41 = (bf16[4,192,768]{2,1,0:T(8,128)(2,1)}, bf16[4,192,768]{2,1,0:T(8,128)(2,1)S(1)}, u32[]{:S(2)}, u32[]{:S(2)}) collective-permute-start(bf16[4,192,768]{2,1,0:T(8,128)(2,1)} %slice_bitcast_fusion.11), channel_id=1, source_target_pairs={{0,4},{2,6},{4,0},{6,2},{8,12},{10,14},{12,8},{14,10},{16,20},{18,... | collective-permute-start | bytes 3538952 | tf_op jit(solution)/shard_map/ppermute | solution.py:240
  587.4 81.6 %collective-permute-start.51 = (bf16[2,2,4,192,768]{4,3,2,1,0:T(8,128)(2,1)}, bf16[2,2,4,192,768]{4,3,2,1,0:T(8,128)(2,1)}, u32[]{:S(2)}, u32[]{:S(2)}) collective-permute-start(bf16[2,2,4,192,768]{4,3,2,1,0:T(8,128)(2,1)} %get-tuple-element.222), channel_id=1, source_target_pairs={{0,2},{2,0},{4,6},{6,4},{8,10},{10,8},{12,14},{14,12},{16,18},{18,... | collective-permute-start | bytes 14155784 | tf_op jit(solution)/shard_map/ppermute | solution.py:244
  600.4 43.4 %collective-permute-start.56 = (bf16[4,2,2,192,256]{4,3,2,1,0:T(8,128)(2,1)}, bf16[4,2,2,192,256]{4,3,2,1,0:T(8,128)(2,1)S(1)}, u32[]{:S(2)}, u32[]{:S(2)}) collective-permute-start(bf16[4,2,2,192,256]{4,3,2,1,0:T(8,128)(2,1)} %get-tuple-element.232), channel_id=1, source_target_pairs={{0,2},{2,0},{4,6},{6,4},{8,10},{10,8},{12,14},{14,12},{16,18},{18,... | collective-permute-start | bytes 4718600 | tf_op jit(solution)/shard_map/ppermute | solution.py:244
  602.6 52.8 %collective-permute-start.55 = (bf16[4,2,2,192,256]{4,3,2,1,0:T(8,128)(2,1)}, bf16[4,2,2,192,256]{4,3,2,1,0:T(8,128)(2,1)S(1)}, u32[]{:S(2)}, u32[]{:S(2)}) collective-permute-start(bf16[4,2,2,192,256]{4,3,2,1,0:T(8,128)(2,1)} %get-tuple-element.230), channel_id=1, source_target_pairs={{0,2},{2,0},{4,6},{6,4},{8,10},{10,8},{12,14},{14,12},{16,18},{18,... | collective-permute-start | bytes 4718600 | tf_op jit(solution)/shard_map/ppermute | solution.py:244
  614.5 59.8 %collective-permute-start.54 = (bf16[2,2,4,192,768]{4,3,2,1,0:T(8,128)(2,1)}, bf16[2,2,4,192,768]{4,3,2,1,0:T(8,128)(2,1)}, u32[]{:S(2)}, u32[]{:S(2)}) collective-permute-start(bf16[2,2,4,192,768]{4,3,2,1,0:T(8,128)(2,1)} %get-tuple-element.228), channel_id=1, source_target_pairs={{0,2},{2,0},{4,6},{6,4},{8,10},{10,8},{12,14},{14,12},{16,18},{18,... | collective-permute-start | bytes 14155784 | tf_op jit(solution)/shard_map/ppermute | solution.py:244
  689.4 78.7 %collective-permute-start.59 = (bf16[2,4,192,768]{3,2,1,0:T(8,128)(2,1)}, bf16[2,4,192,768]{3,2,1,0:T(8,128)(2,1)}, u32[]{:S(2)}, u32[]{:S(2)}) collective-permute-start(bf16[2,4,192,768]{3,2,1,0:T(8,128)(2,1)} %slice_bitcast_fusion.4), channel_id=1, source_target_pairs={{0,4},{2,6},{4,0},{6,2},{8,12},{10,14},{12,8},{14,10},{16,20},{18,... | collective-permute-start | bytes 7077896 | tf_op jit(solution)/shard_map/ppermute | solution.py:240
  692.4 84.6 %collective-permute-start.60 = (bf16[2,2,192,256]{3,2,1,0:T(8,128)(2,1)}, bf16[2,2,192,256]{3,2,1,0:T(8,128)(2,1)}, u32[]{:S(2)}, u32[]{:S(2)}) collective-permute-start(bf16[2,2,192,256]{3,2,1,0:T(8,128)(2,1)} %get-tuple-element.361), channel_id=1, source_target_pairs={{0,24},{2,26},{4,28},{6,30},{8,0},{10,2},{12,4},{14,6},{16,8},{18,... | collective-permute-start | bytes 1179656 | tf_op jit(solution)/shard_map/ppermute | solution.py:236
  695.1 81.9 %collective-permute-start.61 = (bf16[2,2,192,256]{3,2,1,0:T(8,128)(2,1)}, bf16[2,2,192,256]{3,2,1,0:T(8,128)(2,1)}, u32[]{:S(2)}, u32[]{:S(2)}) collective-permute-start(bf16[2,2,192,256]{3,2,1,0:T(8,128)(2,1)} %get-tuple-element.359), channel_id=1, source_target_pairs={{0,8},{2,10},{4,12},{6,14},{8,16},{10,18},{12,20},{14,22},{16,24},... | collective-permute-start | bytes 1179656 | tf_op jit(solution)/shard_map/ppermute | solution.py:236
  697.4 100.2 %collective-permute-start.66 = (bf16[2,2,192,256]{3,2,1,0:T(8,128)(2,1)}, bf16[2,2,192,256]{3,2,1,0:T(8,128)(2,1)}, u32[]{:S(2)}, u32[]{:S(2)}) collective-permute-start(bf16[2,2,192,256]{3,2,1,0:T(8,128)(2,1)} %get-tuple-element.358), channel_id=1, source_target_pairs={{0,24},{2,26},{4,28},{6,30},{8,0},{10,2},{12,4},{14,6},{16,8},{18,... | collective-permute-start | bytes 1179656 | tf_op jit(solution)/shard_map/ppermute | solution.py:236
  720.8 51.9 %collective-permute-start.58 = (bf16[2,4,192,768]{3,2,1,0:T(8,128)(2,1)}, bf16[2,4,192,768]{3,2,1,0:T(8,128)(2,1)}, u32[]{:S(2)}, u32[]{:S(2)}) collective-permute-start(bf16[2,4,192,768]{3,2,1,0:T(8,128)(2,1)} %slice_bitcast_fusion.5), channel_id=1, source_target_pairs={{0,1},{1,0},{2,3},{3,2},{4,5},{5,4},{6,7},{7,6},{8,9},{9,8},{10,11... | collective-permute-start | bytes 7077896 | tf_op jit(solution)/shard_map/ppermute | solution.py:248
  768.1 46.4 %collective-permute-start.64 = (bf16[2,2,192,256]{3,2,1,0:T(8,128)(2,1)S(1)}, bf16[2,2,192,256]{3,2,1,0:T(8,128)(2,1)}, u32[]{:S(2)}, u32[]{:S(2)}) collective-permute-start(bf16[2,2,192,256]{3,2,1,0:T(8,128)(2,1)S(1)} %copy-done.56), channel_id=1, source_target_pairs={{0,8},{2,10},{4,12},{6,14},{8,16},{10,18},{12,20},{14,22},{16,24},... | collective-permute-start | bytes 1179656 | tf_op jit(solution)/shard_map/ppermute | solution.py:236
  793.9 36.9 %collective-permute-start.63 = (bf16[4,192,768]{2,1,0:T(8,128)(2,1)S(1)}, bf16[4,192,768]{2,1,0:T(8,128)(2,1)S(1)}, u32[]{:S(2)}, u32[]{:S(2)}) collective-permute-start(bf16[4,192,768]{2,1,0:T(8,128)(2,1)S(1)} %slice_bitcast_fusion.8), channel_id=1, source_target_pairs={{0,1},{1,0},{2,3},{3,2},{4,5},{5,4},{6,7},{7,6},{8,9},{9,8},{10,11... | collective-permute-start | bytes 3538952 | tf_op jit(solution)/shard_map/ppermute | solution.py:248
  794.9 37.2 %collective-permute-start.62 = (bf16[4,192,768]{2,1,0:T(8,128)(2,1)S(1)}, bf16[4,192,768]{2,1,0:T(8,128)(2,1)S(1)}, u32[]{:S(2)}, u32[]{:S(2)}) collective-permute-start(bf16[4,192,768]{2,1,0:T(8,128)(2,1)S(1)} %slice_bitcast_fusion.9), channel_id=1, source_target_pairs={{0,4},{2,6},{4,0},{6,2},{8,12},{10,14},{12,8},{14,10},{16,20},{18,... | collective-permute-start | bytes 3538952 | tf_op jit(solution)/shard_map/ppermute | solution.py:240
  797.6 31.9 %collective-permute-start.65 = (bf16[2,2,192,256]{3,2,1,0:T(8,128)(2,1)S(1)}, bf16[2,2,192,256]{3,2,1,0:T(8,128)(2,1)S(1)}, u32[]{:S(2)}, u32[]{:S(2)}) collective-permute-start(bf16[2,2,192,256]{3,2,1,0:T(8,128)(2,1)S(1)} %fusion.38), channel_id=1, source_target_pairs={{0,24},{2,26},{4,28},{6,30},{8,0},{10,2},{12,4},{14,6},{16,8},{18,... | collective-permute-start | bytes 1179656 | tf_op jit(solution)/shard_map/ppermute | solution.py:236
  842.7 82.6 %collective-permute-start.79 = (bf16[2,4,128,1408]{3,2,1,0:T(8,128)(2,1)}, bf16[2,4,128,1408]{3,2,1,0:T(8,128)(2,1)}, u32[]{:S(2)}, u32[]{:S(2)}) collective-permute-start(bf16[2,4,128,1408]{3,2,1,0:T(8,128)(2,1)} %get-tuple-element.269), channel_id=1, source_target_pairs={{0,2},{2,0},{4,6},{6,4},{8,10},{10,8},{12,14},{14,12},{16,18},{18,... | collective-permute-start | bytes 8650760 | tf_op jit(solution)/shard_map/ppermute | solution.py:244
  842.7 75.0 %collective-permute-start.84 = (bf16[4,2,128,1280]{3,2,1,0:T(8,128)(2,1)}, bf16[4,2,128,1280]{3,2,1,0:T(8,128)(2,1)}, u32[]{:S(2)}, u32[]{:S(2)}) collective-permute-start(bf16[4,2,128,1280]{3,2,1,0:T(8,128)(2,1)} %get-tuple-element.271), channel_id=1, source_target_pairs={{0,2},{2,0},{4,6},{6,4},{8,10},{10,8},{12,14},{14,12},{16,18},{18,... | collective-permute-start | bytes 7864328 | tf_op jit(solution)/shard_map/ppermute | solution.py:244
  845.1 30.1 %collective-permute-start.69 = (bf16[192,768]{1,0:T(8,128)(2,1)}, bf16[192,768]{1,0:T(8,128)(2,1)S(1)}, u32[]{:S(2)}, u32[]{:S(2)}) collective-permute-start(bf16[192,768]{1,0:T(8,128)(2,1)} %get-tuple-element.373), channel_id=1, source_target_pairs={{0,24},{2,26},{4,28},{6,30},{8,0},{10,2},{12,4},{14,6},{16,8},{18,... | collective-permute-start | bytes 884744 | tf_op jit(solution)/shard_map/ppermute | solution.py:236
  847.3 38.8 %collective-permute-start.68 = (bf16[192,768]{1,0:T(8,128)(2,1)}, bf16[192,768]{1,0:T(8,128)(2,1)}, u32[]{:S(2)}, u32[]{:S(2)}) collective-permute-start(bf16[192,768]{1,0:T(8,128)(2,1)} %get-tuple-element.372), channel_id=1, source_target_pairs={{0,8},{2,10},{4,12},{6,14},{8,16},{10,18},{12,20},{14,22},{16,24},... | collective-permute-start | bytes 884744 | tf_op jit(solution)/shard_map/ppermute | solution.py:236
  886.1 30.8 %collective-permute-start.78 = (bf16[192,2048]{1,0:T(8,128)(2,1)S(1)}, bf16[192,2048]{1,0:T(8,128)(2,1)S(1)}, u32[]{:S(2)}, u32[]{:S(2)}) collective-permute-start(bf16[192,2048]{1,0:T(8,128)(2,1)S(1)} %select_convert_fusion), channel_id=1, source_target_pairs={{0,1},{1,0},{2,3},{3,2},{4,5},{5,4},{6,7},{7,6},{8,9},{9,8},{10,11... | collective-permute-start | bytes 2359304 | tf_op jit(solution)/shard_map/ppermute | solution.py:248
  922.4 31.4 %collective-permute-start.85 = (bf16[2,128,1280]{2,1,0:T(8,128)(2,1)S(1)}, bf16[2,128,1280]{2,1,0:T(8,128)(2,1)S(1)}, u32[]{:S(2)}, u32[]{:S(2)}) collective-permute-start(bf16[2,128,1280]{2,1,0:T(8,128)(2,1)S(1)} %get-tuple-element.352), channel_id=1, source_target_pairs={{0,24},{2,26},{4,28},{6,30},{8,0},{10,2},{12,4},{14,6},{16,8},{18,... | collective-permute-start | bytes 1966088 | tf_op jit(solution)/shard_map/ppermute | solution.py:236
  927.9 37.6 %collective-permute-start.80 = (bf16[4,128,1408]{2,1,0:T(8,128)(2,1)S(1)}, bf16[4,128,1408]{2,1,0:T(8,128)(2,1)S(1)}, u32[]{:S(2)}, u32[]{:S(2)}) collective-permute-start(bf16[4,128,1408]{2,1,0:T(8,128)(2,1)S(1)} %slice_bitcast_fusion.6), channel_id=1, source_target_pairs={{0,4},{2,6},{4,0},{6,2},{8,12},{10,14},{12,8},{14,10},{16,20},{18,... | collective-permute-start | bytes 4325384 | tf_op jit(solution)/shard_map/ppermute | solution.py:240
  (133 other events, 1633.5 us)
Sparse Core Ops, SparseCore 0:
  11.7 110.8 all-gather.2
  124.1 164.6 all-gather.4
  742.1 134.1 reduce-scatter.1
where the time goes:
time: 1010 us
  waiting for transfers between devices  408 us (40%)
  Pallas kernels  184 us (18%)
  matrix products  113 us (11%)
  other arithmetic  111 us (11%)
  starting transfers between devices  105 us (10%)
  local copies, waits for them, and re-layouts  71.2 us (7%)
  between operations  16.2 us (2%)
    ppermute x42, waiting for transfers between devices, shift_z(): lax.ppermute(v, 'dp', [(at(z, x, c), at(z + k, x, c)) for z, x, c in GRID])  238 us
    ppermute x18, waiting for transfers between devices, swap_y(): return lax.ppermute(v, 'tensor', [(0, 1), (1, 0)])  83.4 us
    pallas_call x2, Pallas kernels, run_experts(): pl.pallas_call(expert_kernel, grid=(4,), in_specs=[pair(2, seq), pair(seq...  69.4 us
    all_gather x2, waiting for transfers between devices, gather_dp(): return lax.all_gather(v, 'dp', axis=0, tiled=True)  68 us
    ppermute x42, starting transfers between devices, shift_z(): lax.ppermute(v, 'dp', [(at(z, x, c), at(z + k, x, c)) for z, x, c in GRID])  64 us
    convert_element_type x38, other arithmetic, add2(): return (a.astype(F32) + b.astype(F32)).astype(BF)  58.1 us
    dot_general x10, matrix products, dot(): lax.dot_general(a, b, (((ca,), (cb,)), ((), ())), preferred_element_type=...  46.6 us
    dot_general x3, matrix products, moe_small(): jnp.einsum(spec, a[1], b[1], preferred_element_type=F32)  37.1 us
  transfers between devices with their start and end apart: 93, of which 41 were waited for; matrix products, arithmetic and copies ran while one was open for 26% of the time, Pallas kernels for 15%

commit v1 on v0

--- a/solution.py
+++ b/solution.py
@@ -262,12 +262,6 @@
     return kept.astype(F32) + other.astype(F32)
 
 
-def gather_z(v, way):
-    one, three = shift_z(v, 1), shift_z(v, -1)
-    two = shift_z(one, 1) if way > 0 else shift_z(three, -1)
-    return jnp.stack([v, one, two, three])
-
-
 def add2(a, b):
     return (a.astype(F32) + b.astype(F32)).astype(BF)
 
@@ -288,30 +282,36 @@
     return lax.optimization_barrier((v, w))
 
 
-def gather_rel(v1, v2, v5, v6, plan, aside):
-    w5 = jnp.stack([v5, swap_x(v5)])
-    w6 = jnp.stack([v6, swap_y(v6)])
-    s1 = gather_z(v1, 1)
-    s2 = gather_z(v2, -1)
-    w5 = jnp.stack([w5, swap_y(w5)])
-    w6 = jnp.stack([w6, swap_x(w6)])
-    s1, s2, w5, w6, plan = lax.optimization_barrier((s1, s2, w5, w6, plan))
+def gather_a(v1, v2, v5, v6):
+    x5, y6 = swap_x(v5), swap_y(v6)
+    one1, three1 = shift_z(v1, 1), shift_z(v1, -1)
+    one2, three2 = shift_z(v2, 1), shift_z(v2, -1)
+    w5, w6 = jnp.stack([v5, x5]), jnp.stack([v6, y6])
+    two1, two2 = shift_z(one1, 1), shift_z(three2, -1)
+    y5, x6 = swap_y(w5), swap_x(w6)
+    s1 = jnp.stack([v1, one1, two1, three1])
+    s2 = jnp.stack([v2, one2, two2, three2])
+    return lax.optimization_barrier((s1, s2, jnp.stack([w5, y5]), jnp.stack([w6, x6])))
+
+
+def gather_c(s1, s2, w5, w6):
     s1x, s2y = swap_x(s1), swap_y(s2)
-    five = [shift_z(w5, 1), shift_z(w5, -1)]
-    six = [shift_z(w6, 1), shift_z(w6, -1)]
-    far = aside(1, plan)
-    five, six, s1x, s2y, far = lax.optimization_barrier((five, six, s1x, s2y, far))
-    s1 = jnp.stack([s1, s1x])
-    s2 = jnp.stack([s2, s2y])
+    five = (shift_z(w5, 1), shift_z(w5, -1))
+    six = (shift_z(w6, 1), shift_z(w6, -1))
+    return s1x, s2y, five, six
+
+
+def gather_d(s1, s2, w5, w6, s1x, s2y, five, six):
+    s1, s2 = jnp.stack([s1, s1x]), jnp.stack([s2, s2y])
     s1y, s2x = swap_y(s1), swap_x(s2)
-    five.append(shift_z(five[0], 1))
-    six.append(shift_z(six[1], -1))
-    plan, (five, six) = tied(plan, (five, six))
-    o5 = jnp.stack([w5, five[0], five[2], five[1]])
-    o6 = jnp.stack([w6, six[0], six[2], six[1]])
-    (s1y, s2x), near = tied((s1y, s2x), aside(0, plan))
-    first = (s1, s1y, s2, s2x, o5, o6)
-    return first, tuple(swap_c(v) for v in first), plan, (near, far)
+    five2, six2 = shift_z(five[0], 1), shift_z(six[1], -1)
+    o5 = jnp.stack([w5, five[0], five2, five[1]])
+    o6 = jnp.stack([w6, six[0], six2, six[1]])
+    return s1, s1y, s2, s2x, o5, o6
+
+
+def split_columns(v):
+    return [v[:, a:b] for a, b in zip(SPLIT[:-1], SPLIT[1:])]
 
 
 def scatter_core(near, far):
@@ -371,23 +371,11 @@
     )
 
 
-def cot_kernel(where, rank, cot_a, cot_b, down, cots, d_act):
-    slots = cots.shape[2] // 2
-    for dx, cot in enumerate((cot_a, cot_b)):
-        both = nn(pick_rows(rank[dx], slots), cot[0]).astype(BF)
-        for e in range(2):
-            cots[e, 0, dx * slots : (dx + 1) * slots, :] = both[e * slots : (e + 1) * slots]
-    for e in range(2):
-        d_act[e, 0] = nt(cots[e, 0], down[e])
-
-
-def expert_kernel(
-    rank, rank_t, cols, d_act, x1a, x1b, x2a, x2b, x5, x6, weights,
-    rows, scaled, d_g, d_u, t1, t2, t5, t6, back,
-):
+def put_rows(rank, parts, rows):
+    x1a, x1b, x2a, x2b, x5, x6 = parts
     slots = rows.shape[2] // 2
     n = x1a.shape[2]
-    gates = []
+    rest = []
     for dx, x2 in enumerate((x2a, x2b)):
         pick = pick_rows(rank[dx], slots)
         low, high = pick[:, :n], pick[:, n:]
@@ -395,15 +383,33 @@
         block2 = nn(low, x2[0, 0]) + nn(high, x2[1, 0])
         block5 = nn(low, x5[0, 0, dx]) + nn(high, x5[0, 1, dx])
         block6 = nn(low, x6[0, dx, 0]) + nn(high, x6[0, dx, 1])
-        low = dx * slots
+        at = dx * slots
         for e in range(2):
             part = slice(e * slots, (e + 1) * slots)
-            rows[e, 0, low : low + slots, 0:768] = block1[part].astype(BF)
-            rows[e, 0, low : low + slots, 768:1536] = block2[part].astype(BF)
-            rows[e, 0, low : low + slots, 1536:1792] = block5[part, :256].astype(BF)
-            rows[e, 0, low : low + slots, 1792:2048] = block6[part].astype(BF)
-            both = cols[e, 0:1, :] + cols[e, 1:2, :]
-            gates.append(jnp.sum(block5[part, 256:] * both, axis=1, keepdims=True))
+            rows[e, 0, at : at + slots, 0:768] = block1[part].astype(BF)
+            rows[e, 0, at : at + slots, 768:1536] = block2[part].astype(BF)
+            rows[e, 0, at : at + slots, 1536:1792] = block5[part, :256].astype(BF)
+            rows[e, 0, at : at + slots, 1792:2048] = block6[part].astype(BF)
+            rest.append(block5[part, 256:])
+    return rest
+
+
+def cot_kernel(rank, x1a, x1b, x2a, x2b, x5, x6, down, cots, d_act):
+    put_rows(rank, (x1a, x1b, x2a, x2b, x5, x6), cots)
+    for e in range(2):
+        d_act[e, 0] = nt(cots[e, 0], down[e])
+
+
+def expert_kernel(
+    rank, rank_t, cols, d_act, x1a, x1b, x2a, x2b, x5, x6, weights,
+    rows, scaled, d_g, d_u, t1, t2, t5, t6, back,
+):
+    slots = rows.shape[2] // 2
+    rest = put_rows(rank, (x1a, x1b, x2a, x2b, x5, x6), rows)
+    gates = []
+    for i, part in enumerate(rest):
+        both = cols[i % 2, 0:1, :] + cols[i % 2, 1:2, :]
+        gates.append(jnp.sum(part * both, axis=1, keepdims=True))
     extras = []
     for e in range(2):
         gate = jnp.concatenate([gates[e], gates[2 + e]], axis=0)
@@ -545,26 +551,22 @@
 LIMIT = pltpu.CompilerParams(vmem_limit_bytes=58 * 1024 * 1024)
 
 
-def run_cots(where, rank, cot_all, down, slots):
-    seq, width = cot_all.shape[1:]
-    ff = down.shape[1]
+def part_specs(n, extra):
+    return [z_last(2)(n, 768)] * 4 + [z_first(n, 256 + extra), z_first(n, 256)]
+
+
+def run_cots(rank, parts, down, slots):
+    n = parts[0].shape[2]
+    ff, width = down.shape[1:]
     return pl.pallas_call(
         cot_kernel,
-        grid_spec=pltpu.PrefetchScalarGridSpec(
-            num_scalar_prefetch=1,
-            grid=(4,),
-            in_specs=[
-                pair(2, seq),
-                pl.BlockSpec((1, seq, width), lambda i, w: (w[2 * i], 0, 0)),
-                pl.BlockSpec((1, seq, width), lambda i, w: (w[2 * i + 1], 0, 0)),
-                fixed(2, ff, width),
-            ],
-            out_specs=[by_expert(2 * slots, width), by_expert(2 * slots, ff)],
-        ),
+        grid=(4,),
+        in_specs=[pair(2, 2 * n), *part_specs(n, 0), fixed(2, ff, width)],
+        out_specs=[by_expert(2 * slots, width), by_expert(2 * slots, ff)],
         out_shape=[shaped((2, 4, 2 * slots, width), BF), shaped((2, 4, 2 * slots, ff), F32)],
         compiler_params=LIMIT,
         name="cots",
-    )(where, rank, cot_all, cot_all, down)
+    )(rank, *parts, down)
 
 
 def run_experts(rank, rank_t, cols, d_act, parts, weights, slots):
@@ -579,12 +581,7 @@
             pair(seq, 2),
             fixed(*cols.shape),
             by_expert(2 * slots, ff),
-            z_last(2)(n, 768),
-            z_last(2)(n, 768),
-            z_last(2)(n, 768),
-            z_last(2)(n, 768),
-            z_first(n, 384),
-            z_first(n, 256),
+            *part_specs(n, 128),
             fixed(2, width, 2 * ff),
         ],
         out_specs=[
@@ -638,27 +635,32 @@
     rank = jnp.where(mask, rank, -1.0)
     d = jnp.arange(16)
     where = sequence_at(d // 8, d // 2 % 4, d % 2)
-    rank = jnp.take(rank, where, axis=0)
-    rank_rel = flip(rank, 2, y)
+    rank_rel = flip(jnp.take(rank, where, axis=0), 2, y)
     rank_t = jnp.swapaxes(rank_rel, 1, 2)
     column = jnp.arange(128)
     cols = (
         column[None, None, :] == (mine[:, None] + jnp.array([[0, experts]]))[:, :, None]
     ).astype(F32)
     halves = lambda v: (v[:8], v[8:])
-    return halves(where.astype(jnp.int32)), halves(rank), halves(rank_rel), halves(rank_t), cols
-
-
-def moe_small(plan, cot_all, ffn_in, gate_x, weights, down_weight, slots):
-
-    def cot_rows(k, plan):
-        return run_cots(plan[0][k], plan[1][k], cot_all, down_weight, slots)
-
-    v1, v2, v5, v6 = [ffn_in[:, a:b] for a, b in zip(SPLIT[:-1], SPLIT[1:])]
-    v5 = jnp.concatenate([v5, gate_x], axis=1)
-    *parts, plan, both = gather_rel(v1, v2, v5, v6, plan, cot_rows)
-    rank_rel, rank_t, cols = plan[2:]
-    cots, d_act = zip(*both)
+    return halves(where.astype(jnp.int32)), halves(rank_rel), halves(rank_t), cols
+
+
+def moe_small(plan, cot_parts, ffn_in, gate_x, weights, down_weight, slots):
+    def cot_rows(k):
+        return run_cots(plan[1][k], cot_parts[k], down_weight, slots)
+
+    v1, v2, v5, v6 = split_columns(ffn_in)
+    state = gather_a(v1, v2, jnp.concatenate([v5, gate_x], axis=1), v6)
+    state, plan = tied(state, plan)
+    further = gather_c(*state)
+    further, far = tied(further, cot_rows(1))
+    s1, s1y, s2, s2x, o5, o6 = gather_d(*state, *further)
+    o5, o6, plan = lax.optimization_barrier((o5, o6, plan))
+    (s1y, s2x), near = tied((s1y, s2x), cot_rows(0))
+    first = (s1, s1y, s2, s2x, o5, o6)
+    parts = (first, tuple(swap_c(v) for v in first))
+    cots, d_act = zip(near, far)
+    rank_rel, rank_t, cols = plan[1:]
     far, near = [
         run_experts(rank_rel[k], rank_t[k], cols, d_act[k], parts[k], weights, slots)
         for k in (1, 0)
@@ -822,7 +824,8 @@
         layer_in, weights = tied(layer_in, weights)
     o_t = all_in[:, small_end:]
     if fast:
-        cot_all = gather_dp(gather_y(cotangent)).reshape(dp, seq, width)
+        cot_own, all_in = tied(cotangent, all_in)
+        cot_state = gather_a(*split_columns(cot_own))
 
     w_qkv = all_in[:, :qkv_width]
     router = all_in[:, qkv_width : qkv_width + experts]
@@ -844,6 +847,8 @@
     if fast:
         attn_part, ids_all = tied(attn_part, ids_all)
         plan = slot_plan(ids_all, experts)
+        cot_parts = gather_d(*cot_state, *gather_c(*cot_state))
+        cot_parts = (cot_parts, tuple(swap_c(v) for v in cot_parts))
     hidden = tokens.astype(F32) + scatter_y(attn_part)
 
     ffn_in = rms(hidden, ffn_gain32).astype(BF)
@@ -855,7 +860,7 @@
     args = (gate_weight, up_weight, down_weight)
     if fast:
         d_sum, y_sum, gate_later, up_grad, down_grad = moe_small(
-            plan, cot_all, ffn_in, gate_x, weights, down_weight, slots
+            plan, cot_parts, ffn_in, gate_x, weights, down_weight, slots
         )
     else:
         d_sum, y_sum, gate_grad, up_grad, down_grad = moe_large(

time: 1010 us -> 1110 us (1.099)
  starting transfers between devices: 105 us -> 151 us
  waiting for transfers between devices: 408 us -> 447 us
  other arithmetic: 111 us -> 125 us
    ppermute x42 -> x54, waiting for transfers between devices: 238 us -> 202 us  [shift_z(): lax.ppermute(v, 'dp', [(at(z, x, c), at(z + k, x, c)) for z, x, c in GRID])]
    ppermute x18 -> x21, waiting for transfers between devices: 83.4 us -> 119 us  [swap_y(): return lax.ppermute(v, 'tensor', [(0, 1), (1, 0)])]
    ppermute x42 -> x54, starting transfers between devices: 64 us -> 99.1 us  [shift_z(): lax.ppermute(v, 'dp', [(at(z, x, c), at(z + k, x, c)) for z, x, c in GRID])]
    all_gather x2 -> x1, waiting for transfers between devices: 68 us -> 89.7 us  [gather_dp(): return lax.all_gather(v, 'dp', axis=0, tiled=True)]
    ppermute x14 -> x18, waiting for transfers between devices: 12 us -> 22.7 us  [swap_x(): lax.ppermute(v, 'dp', [(at(z, x, c), at(z, x + 1, c)) for z, x, c in GRID])]
    ppermute x14 -> x18, starting transfers between devices: 13.2 us -> 23.6 us  [swap_x(): lax.ppermute(v, 'dp', [(at(z, x, c), at(z, x + 1, c)) for z, x, c in GRID])]
    another operation x11 -> x21, other arithmetic: 14.4 us -> 22.3 us  [the longest x4 7.03 us: gather_d(): s1, s2 = (jnp.stack([s1, s1x]), jnp.stack([s2, s2y]))]
    ppermute x18 -> x21, starting transfers between devices: 23.7 us -> 23.3 us  [swap_y(): return lax.ppermute(v, 'tensor', [(0, 1), (1, 0)])]
  transfers between devices with their start and end apart: 93 -> 117, of which waited for: 41 -> 51; matrix products, arithmetic and copies ran while one was open for 26% -> 21% of each run, Pallas kernels for 15% -> 12%
where the time goes in v1:
time: 1110 us; the launch traced here: 1100 us
  waiting for transfers between devices  447 us (40%)
  Pallas kernels  181 us (16%)
  starting transfers between devices  151 us (14%)
  other arithmetic  125 us (11%)
  matrix products  114 us (10%)
  local copies, waits for them, and re-layouts  64.7 us (6%)
  between operations  16.6 us (1%)
    ppermute x54, waiting for transfers between devices, shift_z(): lax.ppermute(v, 'dp', [(at(z, x, c), at(z + k, x, c)) for z, x, c in GRID])  202 us
    ppermute x21, waiting for transfers between devices, swap_y(): return lax.ppermute(v, 'tensor', [(0, 1), (1, 0)])  119 us
    ppermute x54, starting transfers between devices, shift_z(): lax.ppermute(v, 'dp', [(at(z, x, c), at(z + k, x, c)) for z, x, c in GRID])  99.1 us
    all_gather x1, waiting for transfers between devices, gather_dp(): return lax.all_gather(v, 'dp', axis=0, tiled=True)  89.7 us
    pallas_call x2, Pallas kernels, run_experts(): pl.pallas_call(expert_kernel, grid=(4,), in_specs=[pair(2, seq), pair(seq...  69.3 us
    convert_element_type x38, other arithmetic, add2(): return (a.astype(F32) + b.astype(F32)).astype(BF)  57.9 us
    dot_general x10, matrix products, dot(): lax.dot_general(a, b, (((ca,), (cb,)), ((), ())), preferred_element_type=...  48.1 us
    dot_general x3, matrix products, moe_small(): jnp.einsum(spec, a[1], b[1], preferred_element_type=F32)  37.1 us
  transfers between devices with their start and end apart: 117, of which 51 were waited for; matrix products, arithmetic and copies ran while one was open for 21% of the time, Pallas kernels for 12%

profile of v1, /device:TPU:0, one launch (start us, length us, event | category | flops | bytes accessed | tf_op | source)
XLA Modules:
  0.0 1099.6 jit_solution(4324778721905749110)
XLA Ops:
  18.6 6.4 pad_maximum_fusion.weights
  25.1 7.2 collective-permute-done
  32.9 89.7 %all-gather.2.cloned.1.call-done = bf16[2048,4736]{0,1:T(8,128)(2,1)} async-done(((bf16[128,4736]{0,1:T(8,128)(2,1)}), bf16[2048,4736]{0,1:T(8,128)(2,1)}) %all-gather.2.cloned.1.call-update) | async-done | bytes 19398672 | tf_op jit(solution)/shard_map/all_gather | solution.py:177
  126.6 10.7 fusion.2.q_raw.k_raw.v_raw
  143.7 14.4 %attend.1 = bf16[384,2048]{1,0:T(8,128)(2,1)} custom-call(f32[384,2560]{1,0:T(8,128)} %fusion.2.q_raw.k_raw.v_raw, f32[384,2560]{1,0:T(8,128)} %fusion.2.q_raw.k_raw.v_raw, f32[384,2560]{1,0:T(8,128)} %fusion.2.q_raw.k_raw.v_raw, f32[8,128]{1,0:T(8,128)} %select_maximum_fusion.gains, f32[384,128]{1,0:T(8,128)} %get-tuple-element.423.cos, ...), custom_call_target="tpu_custom_call" | custom-call | tf_op jit(solution)/shard_map/attend/pallas_call | solution.py:120
  158.1 8.9 fusion.6
  188.5 11.5 %collective-permute-done.26 = bf16[192,256]{1,0:T(8,128)(2,1)S(1)} collective-permute-done((bf16[192,256]{1,0:T(8,128)(2,1)S(1)}, bf16[192,256]{1,0:T(8,128)(2,1)S(1)}, u32[]{:S(2)}, u32[]{:S(2)}) %collective-permute-start.26) | collective-permute-done | bytes 98336 | tf_op jit(solution)/shard_map/ppermute | solution.py:248
  213.5 12.2 %collective-permute-done.20 = bf16[192,768]{1,0:T(8,128)(2,1)S(1)} collective-permute-done((bf16[192,768]{1,0:T(8,128)(2,1)}, bf16[192,768]{1,0:T(8,128)(2,1)S(1)}, u32[]{:S(2)}, u32[]{:S(2)}) %collective-permute-start.20) | collective-permute-done | bytes 294944 | tf_op jit(solution)/shard_map/ppermute | solution.py:236
  241.1 20.1 %collective-permute-done.10 = bf16[192,256]{1,0:T(8,128)(2,1)S(1)} collective-permute-done((bf16[192,256]{1,0:T(8,128)(2,1)S(1)}, bf16[192,256]{1,0:T(8,128)(2,1)S(1)}, u32[]{:S(2)}, u32[]{:S(2)}) %collective-permute-start.10) | collective-permute-done | bytes 98336 | tf_op jit(solution)/shard_map/ppermute | solution.py:248
  280.2 17.2 %collective-permute-start.6 = (bf16[192,768]{1,0:T(8,128)(2,1)S(1)}, bf16[192,768]{1,0:T(8,128)(2,1)S(1)}, u32[]{:S(2)}, u32[]{:S(2)}) collective-permute-start(bf16[192,768]{1,0:T(8,128)(2,1)S(1)} %get-tuple-element.389), channel_id=1, source_target_pairs={{0,24},{2,26},{4,28},{6,30},{8,0},{10,2},{12,4},{14,6},{16,8},{18,... | collective-permute-start | bytes 884744 | tf_op jit(solution)/shard_map/ppermute | solution.py:236
  319.8 27.9 %collective-permute-done.9 = bf16[2,192,384]{2,1,0:T(8,128)(2,1)S(1)} collective-permute-done((bf16[2,192,384]{2,1,0:T(8,128)(2,1)S(1)}, bf16[2,192,384]{2,1,0:T(8,128)(2,1)S(1)}, u32[]{:S(2)}, u32[]{:S(2)}) %collective-permute-start.9) | collective-permute-done | bytes 294944 | tf_op jit(solution)/shard_map/ppermute | solution.py:248
  361.3 10.7 collective-permute-done.16
  375.1 7.0 collective-permute-done.39.x5
  392.6 14.7 %cots.2 = (bf16[2,4,256,2048]{3,2,1,0:T(8,128)(2,1)}, f32[2,4,256,384]{3,2,1,0:T(8,128)}) custom-call(f32[8,2,384]{2,1,0:T(2,128)} %copy.119.rank, bf16[2,4,192,768]{3,2,1,0:T(8,128)(2,1)} %copy-done.41, bf16[2,4,192,768]{3,2,1,0:T(8,128)(2,1)} %copy-done.43, bf16[2,4,192,768]{3,2,1,0:T(8,128)(2,1)} %copy-done.40, bf16[2,4,192,768]{3,2,1,0:T(8,128)(2,1)} %copy-done.42, ...), custom_call_target="tpu_custom_call" | custom-call | tf_op jit(solution)/shard_map/cots/pallas_call | solution.py:561
  407.3 13.8 %collective-permute-done.17 = bf16[2,2,192,256]{3,2,1,0:T(8,128)(2,1)} collective-permute-done((bf16[2,2,192,256]{3,2,1,0:T(8,128)(2,1)S(1)}, bf16[2,2,192,256]{3,2,1,0:T(8,128)(2,1)}, u32[]{:S(2)}, u32[]{:S(2)}) %collective-permute-start.17) | collective-permute-done | bytes 393248 | tf_op jit(solution)/shard_map/ppermute | solution.py:236
  433.0 12.5 %collective-permute-done.45 = bf16[2,2,192,256]{3,2,1,0:T(8,128)(2,1)S(1)} collective-permute-done((bf16[2,2,192,256]{3,2,1,0:T(8,128)(2,1)}, bf16[2,2,192,256]{3,2,1,0:T(8,128)(2,1)S(1)}, u32[]{:S(2)}, u32[]{:S(2)}) %collective-permute-start.45) | collective-permute-done | bytes 393248 | tf_op jit(solution)/shard_map/ppermute | solution.py:236
  454.2 14.7 %cots.3 = (bf16[2,4,256,2048]{3,2,1,0:T(8,128)(2,1)}, f32[2,4,256,384]{3,2,1,0:T(8,128)}) custom-call(f32[8,2,384]{2,1,0:T(2,128)} %copy.121.rank, bf16[2,4,192,768]{3,2,1,0:T(8,128)(2,1)} %copy-done.23, bf16[2,4,192,768]{3,2,1,0:T(8,128)(2,1)} %copy-done.39, bf16[2,4,192,768]{3,2,1,0:T(8,128)(2,1)} %copy-done.22, bf16[2,4,192,768]{3,2,1,0:T(8,128)(2,1)} %copy-done.38, ...), custom_call_target="tpu_custom_call" | custom-call | tf_op jit(solution)/shard_map/cots/pallas_call | solution.py:561
  468.9 7.8 collective-permute-done.47.x2b
  488.8 34.5 %experts.3 = (bf16[2,4,256,2048]{3,2,1,0:T(8,128)(2,1)}, bf16[2,4,256,384]{3,2,1,0:T(8,128)(2,1)}, bf16[2,4,256,384]{3,2,1,0:T(8,128)(2,1)}, bf16[2,4,256,384]{3...) custom-call(f32[8,2,384]{2,1,0:T(2,128)} %copy.122.rank, ...), custom_call_target="tpu_custom_call" | custom-call | tf_op jit(solution)/shard_map/experts/pallas_call | solution.py:576
  524.3 34.9 %experts.2 = (bf16[2,4,256,2048]{3,2,1,0:T(8,128)(2,1)}, bf16[2,4,256,384]{3,2,1,0:T(8,128)(2,1)}, bf16[2,4,256,384]{3,2,1,0:T(8,128)(2,1)}, bf16[2,4,256,384]{3...) custom-call(f32[8,2,384]{2,1,0:T(2,128)} %copy.121.rank, ...), custom_call_target="tpu_custom_call" | custom-call | tf_op jit(solution)/shard_map/experts/pallas_call | solution.py:576
  559.2 12.4 %outs.2 = (bf16[2,2,4,192,768]{4,3,2,1,0:T(8,128)(2,1)}, bf16[2,2,4,192,768]{4,3,2,1,0:T(8,128)(2,1)}, bf16[4,2,2,192,256]{4,3,2,1,0:T(8,128)(2,1)}, bf16[4,2,2,192,256]{4,3,2,1,0:T(8,128)(2,1)}) custom-call(f32[8,384,2]{2,1,0:T(8,128)} %get-tuple-element.174.rank_t, bf16[2,4,256,384]{3,2,1,0:T(8,128)(2,1)} %get-tuple-element.201.scaled, ...), custom_call_target="tpu_custom_call" | custom-call | tf_op jit(solution)/shard_map/outs/pallas_call | solution.py:611
  578.2 11.2 %fusion.126 = f32[2,2048,384,1]{2,1,3,0:T(8,128)} fusion(bf16[2,4,256,2048]{3,2,1,0:T(8,128)(2,1)} %get-tuple-element.246, bf16[2,4,256,384]{3,2,1,0:T(8,128)(2,1)} %get-tuple-element.217), kind=kOutput, calls=%fused_computation.391 | convolution fusion | flops 3221225472 | bytes 16252928 | tf_op jit(solution)/shard_map/egsd,egsf->edf/dot_general | solution.py:670
  631.6 9.6 bitcast_add_fusion.2
  641.2 12.5 %outs.3 = (bf16[2,2,4,192,768]{4,3,2,1,0:T(8,128)(2,1)}, bf16[2,2,4,192,768]{4,3,2,1,0:T(8,128)(2,1)}, bf16[4,2,2,192,256]{4,3,2,1,0:T(8,128)(2,1)}, bf16[4,2,2,192,256]{4,3,2,1,0:T(8,128)(2,1)}) custom-call(f32[8,384,2]{2,1,0:T(8,128)} %get-tuple-element.188.rank_t, bf16[2,4,256,384]{3,2,1,0:T(8,128)(2,1)} %get-tuple-element.206.scaled, ...), custom_call_target="tpu_custom_call" | custom-call | tf_op jit(solution)/shard_map/outs/pallas_call | solution.py:611
  678.4 13.0 %bitcast_add_fusion.1 = f32[2,2048,384]{2,1,0:T(8,128)} fusion(f32[2,2048,384,1]{2,1,3,0:T(8,128)} %fusion.126, bf16[2,4,256,2048]{3,2,1,0:T(8,128)(2,1)} %get-tuple-element.248, bf16[2,4,256,384]{3,2,1,0:T(8,128)(2,1)} %get-tuple-element.218), kind=kOutput, calls=%fused_computation.16 | convolution fusion | flops 3222798336 | bytes 22544384 | tf_op jit(solution)/shard_map/egsd,egsf->edf/dot_general | solution.py:670
  692.2 13.0 %collective-permute-done.67 = bf16[4,192,768]{2,1,0:T(8,128)(2,1)} collective-permute-done((bf16[4,192,768]{2,1,0:T(8,128)(2,1)}, bf16[4,192,768]{2,1,0:T(8,128)(2,1)}, u32[]{:S(2)}, u32[]{:S(2)}) %collective-permute-start.67) | collective-permute-done | bytes 1179680 | tf_op jit(solution)/shard_map/ppermute | solution.py:248
  718.2 10.4 collective-permute-done.74
  728.8 6.6 collective-permute-done.71
  739.9 7.3 collective-permute-done.70
  751.9 8.7 collective-permute-done.72
  766.4 7.6 add_convert_fusion
  801.4 6.9 convolution_convert_fusion
  813.6 8.0 fusion.16.d_context
  821.6 12.6 %attend_back.2 = (bf16[384,1024]{1,0:T(8,128)(2,1)}, bf16[384,128]{1,0:T(8,128)(2,1)}, bf16[384,128]{1,0:T(8,128)(2,1)}, f32[8,128]{1,0:T(8,128)}) custom-call(f32[384,2560]{1,0:T(8,128)} %fusion.2.q_raw.k_raw.v_raw, f32[384,2560]{1,0:T(8,128)} %fusion.2.q_raw.k_raw.v_raw, f32[384,2560]{1,0:T(8,128)} %fusion.2.q_raw.k_raw.v_raw, ...), custom_call_target="tpu_custom_call" | custom-call | tf_op jit(solution)/shard_map/attend_back/pallas_call | solution.py:143
  834.2 11.6 %fusion.127 = f32[2,2048,384,1]{2,1,3,0:T(8,128)} fusion(bf16[2,4,256,2048]{3,2,1,0:T(8,128)(2,1)} %get-tuple-element.246, bf16[2,4,256,384]{3,2,1,0:T(8,128)(2,1)} %get-tuple-element.247), kind=kOutput, calls=%fused_computation.392 | convolution fusion | flops 3221225472 | bytes 16252928 | tf_op jit(solution)/shard_map/egsd,egsf->edf/dot_general | solution.py:670
  845.9 14.5 %bitcast_add_fusion = f32[2,2048,384]{2,1,0:T(8,128)} fusion(f32[2,2048,384,1]{2,1,3,0:T(8,128)} %fusion.127, bf16[2,4,256,2048]{3,2,1,0:T(8,128)(2,1)} %get-tuple-element.248, bf16[2,4,256,384]{3,2,1,0:T(8,128)(2,1)} %get-tuple-element.249), kind=kOutput, calls=%fused_computation.15 | convolution fusion | flops 3222798336 | bytes 22544384 | tf_op jit(solution)/shard_map/egsd,egsf->edf/dot_general | solution.py:670
  869.5 12.7 %attend_back.3 = (bf16[384,1024]{1,0:T(8,128)(2,1)}, bf16[384,128]{1,0:T(8,128)(2,1)}, bf16[384,128]{1,0:T(8,128)(2,1)}, f32[8,128]{1,0:T(8,128)}) custom-call(f32[384,2560]{1,0:T(8,128)} %fusion.2.q_raw.k_raw.v_raw, f32[384,2560]{1,0:T(8,128)} %fusion.2.q_raw.k_raw.v_raw, f32[384,2560]{1,0:T(8,128)} %fusion.2.q_raw.k_raw.v_raw, ...), custom_call_target="tpu_custom_call" | custom-call | tf_op jit(solution)/shard_map/attend_back/pallas_call | solution.py:143
  894.9 10.8 collective-permute-done.92
  907.0 15.0 %collective-permute-done.90 = bf16[2,2,192,256]{3,2,1,0:T(8,128)(2,1)S(1)} collective-permute-done((bf16[2,2,192,256]{3,2,1,0:T(8,128)(2,1)S(1)}, bf16[2,2,192,256]{3,2,1,0:T(8,128)(2,1)S(1)}, u32[]{:S(2)}, u32[]{:S(2)}) %collective-permute-start.90) | collective-permute-done | bytes 393248 | tf_op jit(solution)/shard_map/ppermute | solution.py:236
  924.7 8.7 fusion
  933.4 9.1 grad.3
  951.2 9.1 grad.2
  969.8 6.3 collective-permute-done.97
  978.5 17.1 %collective-permute-done.102 = bf16[192,256]{1,0:T(8,128)(2,1)S(1)} collective-permute-done((bf16[192,256]{1,0:T(8,128)(2,1)S(1)}, bf16[192,256]{1,0:T(8,128)(2,1)S(1)}, u32[]{:S(2)}, u32[]{:S(2)}) %collective-permute-start.102) | collective-permute-done | bytes 98336 | tf_op jit(solution)/shard_map/ppermute | solution.py:248
  1021.8 11.0 %collective-permute-done.111 = bf16[2,128,1280]{2,1,0:T(8,128)(2,1)S(1)} collective-permute-done((bf16[2,128,1280]{2,1,0:T(8,128)(2,1)S(1)}, bf16[2,128,1280]{2,1,0:T(8,128)(2,1)S(1)}, u32[]{:S(2)}, u32[]{:S(2)}) %collective-permute-start.111) | collective-permute-done | bytes 655392 | tf_op jit(solution)/shard_map/ppermute | solution.py:236
  1033.0 7.0 collective-permute-start.112
  1046.3 10.9 collective-permute-done.112
  1062.5 10.5 collective-permute-done.107
  (623 shorter events, 412.3 us)
Async XLA Ops:
  7.3 115.3 %all-gather.2.cloned.1.call-start = ((), (), s32[]{:S(2)}) async-start(), calls=%async_computation.1 | async-start | bytes 20611072 | tf_op jit(solution)/shard_map/all_gather | solution.py:177
  11.6 1078.2 %reduce-scatter.2.cloned.1.call-start = ((), (), s32[]{:S(2)}) async-start(), calls=%async_computation.2 | async-start | bytes 8912896 | tf_op jit(solution)/shard_map/reduce_scatter | solution.py:189
  177.2 59.2 %collective-permute-start.1 = (bf16[192,2048]{1,0:T(8,128)(2,1)}, bf16[192,2048]{1,0:T(8,128)(2,1)}, u32[]{:S(2)}, u32[]{:S(2)}) collective-permute-start(bf16[192,2048]{1,0:T(8,128)(2,1)} %select_convert_fusion.1), channel_id=1, source_target_pairs={{0,1},{1,0},{2,3},{3,2},{4,5},{5,4},{6,7},{7,6},{8,9},{9,8},{10,11... | collective-permute-start | bytes 2359304 | tf_op jit(solution)/shard_map/ppermute | solution.py:248
  231.0 35.4 %collective-permute-start.41 = (bf16[2,2,192,256]{3,2,1,0:T(8,128)(2,1)S(1)}, bf16[2,2,192,256]{3,2,1,0:T(8,128)(2,1)S(1)}, u32[]{:S(2)}, u32[]{:S(2)}) collective-permute-start(bf16[2,2,192,256]{3,2,1,0:T(8,128)(2,1)S(1)} %pad_maximum_fusion.18), channel_id=1, source_target_pairs={{0,24},{2,26},{4,28},{6,30},{8,0},{10,2},{12,4},{14,6},{16,8},{18,... | collective-permute-start | bytes 1179656 | tf_op jit(solution)/shard_map/ppermute | solution.py:236
  233.9 36.4 %collective-permute-start.40 = (bf16[2,2,192,256]{3,2,1,0:T(8,128)(2,1)S(1)}, bf16[2,2,192,256]{3,2,1,0:T(8,128)(2,1)S(1)}, u32[]{:S(2)}, u32[]{:S(2)}) collective-permute-start(bf16[2,2,192,256]{3,2,1,0:T(8,128)(2,1)S(1)} %pad_maximum_fusion.18), channel_id=1, source_target_pairs={{0,8},{2,10},{4,12},{6,14},{8,16},{10,18},{12,20},{14,22},{16,24},... | collective-permute-start | bytes 1179656 | tf_op jit(solution)/shard_map/ppermute | solution.py:236
  233.9 38.5 %collective-permute-start.32 = (bf16[4,192,768]{2,1,0:T(8,128)(2,1)S(1)}, bf16[4,192,768]{2,1,0:T(8,128)(2,1)S(1)}, u32[]{:S(2)}, u32[]{:S(2)}) collective-permute-start(bf16[4,192,768]{2,1,0:T(8,128)(2,1)S(1)} %pad_maximum_fusion.14), channel_id=1, source_target_pairs={{0,1},{1,0},{2,3},{3,2},{4,5},{5,4},{6,7},{7,6},{8,9},{9,8},{10,11... | collective-permute-start | bytes 3538952 | tf_op jit(solution)/shard_map/ppermute | solution.py:248
  235.3 38.4 %collective-permute-start.28 = (bf16[4,192,768]{2,1,0:T(8,128)(2,1)S(1)}, bf16[4,192,768]{2,1,0:T(8,128)(2,1)S(1)}, u32[]{:S(2)}, u32[]{:S(2)}) collective-permute-start(bf16[4,192,768]{2,1,0:T(8,128)(2,1)S(1)} %pad_maximum_fusion.13), channel_id=1, source_target_pairs={{0,4},{2,6},{4,0},{6,2},{8,12},{10,14},{12,8},{14,10},{16,20},{18,... | collective-permute-start | bytes 3538952 | tf_op jit(solution)/shard_map/ppermute | solution.py:240
  266.5 31.0 %collective-permute-start.38 = (bf16[2,2,192,256]{3,2,1,0:T(8,128)(2,1)S(1)}, bf16[2,2,192,256]{3,2,1,0:T(8,128)(2,1)S(1)}, u32[]{:S(2)}, u32[]{:S(2)}) collective-permute-start(bf16[2,2,192,256]{3,2,1,0:T(8,128)(2,1)S(1)} %pad_maximum_fusion.17), channel_id=1, source_target_pairs={{0,24},{2,26},{4,28},{6,30},{8,0},{10,2},{12,4},{14,6},{16,8},{18,... | collective-permute-start | bytes 1179656 | tf_op jit(solution)/shard_map/ppermute | solution.py:236
  273.8 98.2 %collective-permute-start.34 = (bf16[2,4,192,768]{3,2,1,0:T(8,128)(2,1)S(1)}, bf16[2,4,192,768]{3,2,1,0:T(8,128)(2,1)S(1)}, u32[]{:S(2)}, u32[]{:S(2)}) collective-permute-start(bf16[2,4,192,768]{3,2,1,0:T(8,128)(2,1)S(1)} %pad_maximum_fusion.2.x2a), channel_id=1, source_target_pairs={{0,4},{2,6},{4,0},{6,2},{8,12},{10,14},{12,8},{14,10},{16,20},{18,... | collective-permute-start | bytes 7077896 | tf_op jit(solution)/shard_map/ppermute | solution.py:240
  297.5 77.2 %collective-permute-start.30 = (bf16[2,4,192,768]{3,2,1,0:T(8,128)(2,1)S(1)}, bf16[2,4,192,768]{3,2,1,0:T(8,128)(2,1)S(1)}, u32[]{:S(2)}, u32[]{:S(2)}) collective-permute-start(bf16[2,4,192,768]{3,2,1,0:T(8,128)(2,1)S(1)} %pad_maximum_fusion.1.x1a), channel_id=1, source_target_pairs={{0,1},{1,0},{2,3},{3,2},{4,5},{5,4},{6,7},{7,6},{8,9},{9,8},{10,11... | collective-permute-start | bytes 7077896 | tf_op jit(solution)/shard_map/ppermute | solution.py:248
  310.4 37.3 %collective-permute-start.9 = (bf16[2,192,384]{2,1,0:T(8,128)(2,1)S(1)}, bf16[2,192,384]{2,1,0:T(8,128)(2,1)S(1)}, u32[]{:S(2)}, u32[]{:S(2)}) collective-permute-start(bf16[2,192,384]{2,1,0:T(8,128)(2,1)S(1)} %get-tuple-element.394), channel_id=1, source_target_pairs={{0,1},{1,0},{2,3},{3,2},{4,5},{5,4},{6,7},{7,6},{8,9},{9,8},{10,11... | collective-permute-start | bytes 884744 | tf_op jit(solution)/shard_map/ppermute | solution.py:248
  313.6 59.9 %collective-permute-start.43 = (bf16[4,2,2,192,256]{4,3,2,1,0:T(8,128)(2,1)S(1)}, bf16[4,2,2,192,256]{4,3,2,1,0:T(8,128)(2,1)S(1)}, u32[]{:S(2)}, u32[]{:S(2)}) collective-permute-start(bf16[4,2,2,192,256]{4,3,2,1,0:T(8,128)(2,1)S(1)} %pad_maximum_fusion.8.x6), channel_id=1, source_target_pairs={{0,2},{2,0},{4,6},{6,4},{8,10},{10,8},{12,14},{14,12},{16,18},{18,... | collective-permute-start | bytes 4718600 | tf_op jit(solution)/shard_map/ppermute | solution.py:244
  316.7 34.9 %collective-permute-start.7 = (bf16[192,768]{1,0:T(8,128)(2,1)S(1)}, bf16[192,768]{1,0:T(8,128)(2,1)S(1)}, u32[]{:S(2)}, u32[]{:S(2)}) collective-permute-start(bf16[192,768]{1,0:T(8,128)(2,1)S(1)} %collective-permute-done.6), channel_id=1, source_target_pairs={{0,24},{2,26},{4,28},{6,30},{8,0},{10,2},{12,4},{14,6},{16,8},{18,... | collective-permute-start | bytes 884744 | tf_op jit(solution)/shard_map/ppermute | solution.py:236
  382.1 39.0 %collective-permute-start.12 = (bf16[4,192,768]{2,1,0:T(8,128)(2,1)}, bf16[4,192,768]{2,1,0:T(8,128)(2,1)}, u32[]{:S(2)}, u32[]{:S(2)}) collective-permute-start(bf16[4,192,768]{2,1,0:T(8,128)(2,1)} %pad_maximum_fusion.11), channel_id=1, source_target_pairs={{0,4},{2,6},{4,0},{6,2},{8,12},{10,14},{12,8},{14,10},{16,20},{18,... | collective-permute-start | bytes 3538952 | tf_op jit(solution)/shard_map/ppermute | solution.py:240
  383.2 37.9 %collective-permute-start.13 = (bf16[4,192,768]{2,1,0:T(8,128)(2,1)}, bf16[4,192,768]{2,1,0:T(8,128)(2,1)}, u32[]{:S(2)}, u32[]{:S(2)}) collective-permute-start(bf16[4,192,768]{2,1,0:T(8,128)(2,1)} %pad_maximum_fusion.12), channel_id=1, source_target_pairs={{0,1},{1,0},{2,3},{3,2},{4,5},{5,4},{6,7},{7,6},{8,9},{9,8},{10,11... | collective-permute-start | bytes 3538952 | tf_op jit(solution)/shard_map/ppermute | solution.py:248
  384.7 36.3 %collective-permute-start.14 = (bf16[2,2,192,384]{3,2,1,0:T(8,128)(2,1)}, bf16[2,2,192,384]{3,2,1,0:T(8,128)(2,1)}, u32[]{:S(2)}, u32[]{:S(2)}) collective-permute-start(bf16[2,2,192,384]{3,2,1,0:T(8,128)(2,1)} %pad_maximum_fusion.15), channel_id=1, source_target_pairs={{0,8},{2,10},{4,12},{6,14},{8,16},{10,18},{12,20},{14,22},{16,24},... | collective-permute-start | bytes 1769480 | tf_op jit(solution)/shard_map/ppermute | solution.py:236
  384.8 36.3 %collective-permute-start.15 = (bf16[2,2,192,384]{3,2,1,0:T(8,128)(2,1)}, bf16[2,2,192,384]{3,2,1,0:T(8,128)(2,1)}, u32[]{:S(2)}, u32[]{:S(2)}) collective-permute-start(bf16[2,2,192,384]{3,2,1,0:T(8,128)(2,1)} %pad_maximum_fusion.15), channel_id=1, source_target_pairs={{0,24},{2,26},{4,28},{6,30},{8,0},{10,2},{12,4},{14,6},{16,8},{18,... | collective-permute-start | bytes 1769480 | tf_op jit(solution)/shard_map/ppermute | solution.py:236
  390.1 31.0 %collective-permute-start.17 = (bf16[2,2,192,256]{3,2,1,0:T(8,128)(2,1)S(1)}, bf16[2,2,192,256]{3,2,1,0:T(8,128)(2,1)}, u32[]{:S(2)}, u32[]{:S(2)}) collective-permute-start(bf16[2,2,192,256]{3,2,1,0:T(8,128)(2,1)S(1)} %pad_maximum_fusion.16), channel_id=1, source_target_pairs={{0,24},{2,26},{4,28},{6,30},{8,0},{10,2},{12,4},{14,6},{16,8},{18,... | collective-permute-start | bytes 1179656 | tf_op jit(solution)/shard_map/ppermute | solution.py:236
  424.4 52.2 %collective-permute-start.47 = (bf16[2,4,192,768]{3,2,1,0:T(8,128)(2,1)}, bf16[2,4,192,768]{3,2,1,0:T(8,128)(2,1)}, u32[]{:S(2)}, u32[]{:S(2)}) collective-permute-start(bf16[2,4,192,768]{3,2,1,0:T(8,128)(2,1)} %pad_maximum_fusion.5.x2a), channel_id=1, source_target_pairs={{0,4},{2,6},{4,0},{6,2},{8,12},{10,14},{12,8},{14,10},{16,20},{18,... | collective-permute-start | bytes 7077896 | tf_op jit(solution)/shard_map/ppermute | solution.py:240
  428.6 51.9 %collective-permute-start.46 = (bf16[2,4,192,768]{3,2,1,0:T(8,128)(2,1)}, bf16[2,4,192,768]{3,2,1,0:T(8,128)(2,1)}, u32[]{:S(2)}, u32[]{:S(2)}) collective-permute-start(bf16[2,4,192,768]{3,2,1,0:T(8,128)(2,1)} %pad_maximum_fusion.4.x1a), channel_id=1, source_target_pairs={{0,1},{1,0},{2,3},{3,2},{4,5},{5,4},{6,7},{7,6},{8,9},{9,8},{10,11... | collective-permute-start | bytes 7077896 | tf_op jit(solution)/shard_map/ppermute | solution.py:248
  451.2 30.9 %collective-permute-start.50 = (bf16[2,4,192,768]{3,2,1,0:T(8,128)(2,1)}, bf16[2,4,192,768]{3,2,1,0:T(8,128)(2,1)}, u32[]{:S(2)}, u32[]{:S(2)}) collective-permute-start(bf16[2,4,192,768]{3,2,1,0:T(8,128)(2,1)} %pad_maximum_fusion.5.x2a), channel_id=1, source_target_pairs={{0,2},{2,0},{4,6},{6,4},{8,10},{10,8},{12,14},{14,12},{16,18},{18,... | collective-permute-start | bytes 7077896 | tf_op jit(solution)/shard_map/ppermute | solution.py:244
  451.6 30.5 %collective-permute-start.48 = (bf16[2,4,192,768]{3,2,1,0:T(8,128)(2,1)}, bf16[2,4,192,768]{3,2,1,0:T(8,128)(2,1)}, u32[]{:S(2)}, u32[]{:S(2)}) collective-permute-start(bf16[2,4,192,768]{3,2,1,0:T(8,128)(2,1)} %pad_maximum_fusion.4.x1a), channel_id=1, source_target_pairs={{0,2},{2,0},{4,6},{6,4},{8,10},{10,8},{12,14},{14,12},{16,18},{18,... | collective-permute-start | bytes 7077896 | tf_op jit(solution)/shard_map/ppermute | solution.py:244
  523.2 76.6 %collective-permute-start.56 = (bf16[2,2,4,192,768]{4,3,2,1,0:T(8,128)(2,1)}, bf16[2,2,4,192,768]{4,3,2,1,0:T(8,128)(2,1)}, u32[]{:S(2)}, u32[]{:S(2)}) collective-permute-start(bf16[2,2,4,192,768]{4,3,2,1,0:T(8,128)(2,1)} %get-tuple-element.196), channel_id=1, source_target_pairs={{0,2},{2,0},{4,6},{6,4},{8,10},{10,8},{12,14},{14,12},{16,18},{18,... | collective-permute-start | bytes 14155784 | tf_op jit(solution)/shard_map/ppermute | solution.py:244
  523.5 85.7 %collective-permute-start.54 = (bf16[2,2,4,192,768]{4,3,2,1,0:T(8,128)(2,1)}, bf16[2,2,4,192,768]{4,3,2,1,0:T(8,128)(2,1)}, u32[]{:S(2)}, u32[]{:S(2)}) collective-permute-start(bf16[2,2,4,192,768]{4,3,2,1,0:T(8,128)(2,1)} %get-tuple-element.194), channel_id=1, source_target_pairs={{0,2},{2,0},{4,6},{6,4},{8,10},{10,8},{12,14},{14,12},{16,18},{18,... | collective-permute-start | bytes 14155784 | tf_op jit(solution)/shard_map/ppermute | solution.py:244
  593.3 35.1 %collective-permute-start.63 = (bf16[2,2,192,256]{3,2,1,0:T(8,128)(2,1)S(1)}, bf16[2,2,192,256]{3,2,1,0:T(8,128)(2,1)S(1)}, u32[]{:S(2)}, u32[]{:S(2)}) collective-permute-start(bf16[2,2,192,256]{3,2,1,0:T(8,128)(2,1)S(1)} %get-tuple-element.362), channel_id=1, source_target_pairs={{0,24},{2,26},{4,28},{6,30},{8,0},{10,2},{12,4},{14,6},{16,8},{18,... | collective-permute-start | bytes 1179656 | tf_op jit(solution)/shard_map/ppermute | solution.py:236
  607.9 52.8 %collective-permute-start.57 = (bf16[2,4,192,768]{3,2,1,0:T(8,128)(2,1)}, bf16[2,4,192,768]{3,2,1,0:T(8,128)(2,1)}, u32[]{:S(2)}, u32[]{:S(2)}) collective-permute-start(bf16[2,4,192,768]{3,2,1,0:T(8,128)(2,1)} %slice_bitcast_fusion), channel_id=1, source_target_pairs={{0,4},{2,6},{4,0},{6,2},{8,12},{10,14},{12,8},{14,10},{16,20},{18,... | collective-permute-start | bytes 7077896 | tf_op jit(solution)/shard_map/ppermute | solution.py:240
  617.2 52.5 %collective-permute-start.55 = (bf16[2,4,192,768]{3,2,1,0:T(8,128)(2,1)}, bf16[2,4,192,768]{3,2,1,0:T(8,128)(2,1)}, u32[]{:S(2)}, u32[]{:S(2)}) collective-permute-start(bf16[2,4,192,768]{3,2,1,0:T(8,128)(2,1)} %slice_bitcast_fusion.2), channel_id=1, source_target_pairs={{0,1},{1,0},{2,3},{3,2},{4,5},{5,4},{6,7},{7,6},{8,9},{9,8},{10,11... | collective-permute-start | bytes 7077896 | tf_op jit(solution)/shard_map/ppermute | solution.py:248
  619.5 34.2 %collective-permute-start.65 = (bf16[2,2,192,256]{3,2,1,0:T(8,128)(2,1)}, bf16[2,2,192,256]{3,2,1,0:T(8,128)(2,1)}, u32[]{:S(2)}, u32[]{:S(2)}) collective-permute-start(bf16[2,2,192,256]{3,2,1,0:T(8,128)(2,1)} %fusion.41), channel_id=1, source_target_pairs={{0,8},{2,10},{4,12},{6,14},{8,16},{10,18},{12,20},{14,22},{16,24},... | collective-permute-start | bytes 1179656 | tf_op jit(solution)/shard_map/ppermute | solution.py:236
  674.7 30.5 %collective-permute-start.67 = (bf16[4,192,768]{2,1,0:T(8,128)(2,1)}, bf16[4,192,768]{2,1,0:T(8,128)(2,1)}, u32[]{:S(2)}, u32[]{:S(2)}) collective-permute-start(bf16[4,192,768]{2,1,0:T(8,128)(2,1)} %slice_bitcast_fusion.10), channel_id=1, source_target_pairs={{0,1},{1,0},{2,3},{3,2},{4,5},{5,4},{6,7},{7,6},{8,9},{9,8},{10,11... | collective-permute-start | bytes 3538952 | tf_op jit(solution)/shard_map/ppermute | solution.py:248
  678.4 82.5 %collective-permute-start.76 = (bf16[2,2,4,192,768]{4,3,2,1,0:T(8,128)(2,1)}, bf16[2,2,4,192,768]{4,3,2,1,0:T(8,128)(2,1)}, u32[]{:S(2)}, u32[]{:S(2)}) collective-permute-start(bf16[2,2,4,192,768]{4,3,2,1,0:T(8,128)(2,1)} %get-tuple-element.222), channel_id=1, source_target_pairs={{0,2},{2,0},{4,6},{6,4},{8,10},{10,8},{12,14},{14,12},{16,18},{18,... | collective-permute-start | bytes 14155784 | tf_op jit(solution)/shard_map/ppermute | solution.py:244
  691.5 44.0 %collective-permute-start.81 = (bf16[4,2,2,192,256]{4,3,2,1,0:T(8,128)(2,1)}, bf16[4,2,2,192,256]{4,3,2,1,0:T(8,128)(2,1)S(1)}, u32[]{:S(2)}, u32[]{:S(2)}) collective-permute-start(bf16[4,2,2,192,256]{4,3,2,1,0:T(8,128)(2,1)} %get-tuple-element.232), channel_id=1, source_target_pairs={{0,2},{2,0},{4,6},{6,4},{8,10},{10,8},{12,14},{14,12},{16,18},{18,... | collective-permute-start | bytes 4718600 | tf_op jit(solution)/shard_map/ppermute | solution.py:244
  692.0 55.2 %collective-permute-start.80 = (bf16[4,2,2,192,256]{4,3,2,1,0:T(8,128)(2,1)}, bf16[4,2,2,192,256]{4,3,2,1,0:T(8,128)(2,1)S(1)}, u32[]{:S(2)}, u32[]{:S(2)}) collective-permute-start(bf16[4,2,2,192,256]{4,3,2,1,0:T(8,128)(2,1)} %get-tuple-element.230), channel_id=1, source_target_pairs={{0,2},{2,0},{4,6},{6,4},{8,10},{10,8},{12,14},{14,12},{16,18},{18,... | collective-permute-start | bytes 4718600 | tf_op jit(solution)/shard_map/ppermute | solution.py:244
  705.2 61.1 %collective-permute-start.79 = (bf16[2,2,4,192,768]{4,3,2,1,0:T(8,128)(2,1)}, bf16[2,2,4,192,768]{4,3,2,1,0:T(8,128)(2,1)}, u32[]{:S(2)}, u32[]{:S(2)}) collective-permute-start(bf16[2,2,4,192,768]{4,3,2,1,0:T(8,128)(2,1)} %get-tuple-element.228), channel_id=1, source_target_pairs={{0,2},{2,0},{4,6},{6,4},{8,10},{10,8},{12,14},{14,12},{16,18},{18,... | collective-permute-start | bytes 14155784 | tf_op jit(solution)/shard_map/ppermute | solution.py:244
  781.6 78.7 %collective-permute-start.84 = (bf16[2,4,192,768]{3,2,1,0:T(8,128)(2,1)}, bf16[2,4,192,768]{3,2,1,0:T(8,128)(2,1)}, u32[]{:S(2)}, u32[]{:S(2)}) collective-permute-start(bf16[2,4,192,768]{3,2,1,0:T(8,128)(2,1)} %slice_bitcast_fusion.4), channel_id=1, source_target_pairs={{0,4},{2,6},{4,0},{6,2},{8,12},{10,14},{12,8},{14,10},{16,20},{18,... | collective-permute-start | bytes 7077896 | tf_op jit(solution)/shard_map/ppermute | solution.py:240
  783.7 85.8 %collective-permute-start.85 = (bf16[2,2,192,256]{3,2,1,0:T(8,128)(2,1)}, bf16[2,2,192,256]{3,2,1,0:T(8,128)(2,1)}, u32[]{:S(2)}, u32[]{:S(2)}) collective-permute-start(bf16[2,2,192,256]{3,2,1,0:T(8,128)(2,1)} %get-tuple-element.359), channel_id=1, source_target_pairs={{0,24},{2,26},{4,28},{6,30},{8,0},{10,2},{12,4},{14,6},{16,8},{18,... | collective-permute-start | bytes 1179656 | tf_op jit(solution)/shard_map/ppermute | solution.py:236
  786.5 83.0 %collective-permute-start.86 = (bf16[2,2,192,256]{3,2,1,0:T(8,128)(2,1)}, bf16[2,2,192,256]{3,2,1,0:T(8,128)(2,1)}, u32[]{:S(2)}, u32[]{:S(2)}) collective-permute-start(bf16[2,2,192,256]{3,2,1,0:T(8,128)(2,1)} %get-tuple-element.357), channel_id=1, source_target_pairs={{0,8},{2,10},{4,12},{6,14},{8,16},{10,18},{12,20},{14,22},{16,24},... | collective-permute-start | bytes 1179656 | tf_op jit(solution)/shard_map/ppermute | solution.py:236
  788.7 102.2 %collective-permute-start.91 = (bf16[2,2,192,256]{3,2,1,0:T(8,128)(2,1)}, bf16[2,2,192,256]{3,2,1,0:T(8,128)(2,1)S(1)}, u32[]{:S(2)}, u32[]{:S(2)}) collective-permute-start(bf16[2,2,192,256]{3,2,1,0:T(8,128)(2,1)} %get-tuple-element.356), channel_id=1, source_target_pairs={{0,24},{2,26},{4,28},{6,30},{8,0},{10,2},{12,4},{14,6},{16,8},{18,... | collective-permute-start | bytes 1179656 | tf_op jit(solution)/shard_map/ppermute | solution.py:236
  813.0 52.1 %collective-permute-start.83 = (bf16[2,4,192,768]{3,2,1,0:T(8,128)(2,1)}, bf16[2,4,192,768]{3,2,1,0:T(8,128)(2,1)}, u32[]{:S(2)}, u32[]{:S(2)}) collective-permute-start(bf16[2,4,192,768]{3,2,1,0:T(8,128)(2,1)} %slice_bitcast_fusion.5), channel_id=1, source_target_pairs={{0,1},{1,0},{2,3},{3,2},{4,5},{5,4},{6,7},{7,6},{8,9},{9,8},{10,11... | collective-permute-start | bytes 7077896 | tf_op jit(solution)/shard_map/ppermute | solution.py:248
  860.4 46.7 %collective-permute-start.89 = (bf16[2,2,192,256]{3,2,1,0:T(8,128)(2,1)}, bf16[2,2,192,256]{3,2,1,0:T(8,128)(2,1)}, u32[]{:S(2)}, u32[]{:S(2)}) collective-permute-start(bf16[2,2,192,256]{3,2,1,0:T(8,128)(2,1)} %get-tuple-element.358), channel_id=1, source_target_pairs={{0,8},{2,10},{4,12},{6,14},{8,16},{10,18},{12,20},{14,22},{16,24},... | collective-permute-start | bytes 1179656 | tf_op jit(solution)/shard_map/ppermute | solution.py:236
  886.3 37.7 %collective-permute-start.88 = (bf16[4,192,768]{2,1,0:T(8,128)(2,1)S(1)}, bf16[4,192,768]{2,1,0:T(8,128)(2,1)S(1)}, u32[]{:S(2)}, u32[]{:S(2)}) collective-permute-start(bf16[4,192,768]{2,1,0:T(8,128)(2,1)S(1)} %slice_bitcast_fusion.8), channel_id=1, source_target_pairs={{0,1},{1,0},{2,3},{3,2},{4,5},{5,4},{6,7},{7,6},{8,9},{9,8},{10,11... | collective-permute-start | bytes 3538952 | tf_op jit(solution)/shard_map/ppermute | solution.py:248
  887.1 37.2 %collective-permute-start.87 = (bf16[4,192,768]{2,1,0:T(8,128)(2,1)S(1)}, bf16[4,192,768]{2,1,0:T(8,128)(2,1)S(1)}, u32[]{:S(2)}, u32[]{:S(2)}) collective-permute-start(bf16[4,192,768]{2,1,0:T(8,128)(2,1)S(1)} %slice_bitcast_fusion.9), channel_id=1, source_target_pairs={{0,4},{2,6},{4,0},{6,2},{8,12},{10,14},{12,8},{14,10},{16,20},{18,... | collective-permute-start | bytes 3538952 | tf_op jit(solution)/shard_map/ppermute | solution.py:240
  890.9 31.1 %collective-permute-start.90 = (bf16[2,2,192,256]{3,2,1,0:T(8,128)(2,1)S(1)}, bf16[2,2,192,256]{3,2,1,0:T(8,128)(2,1)S(1)}, u32[]{:S(2)}, u32[]{:S(2)}) collective-permute-start(bf16[2,2,192,256]{3,2,1,0:T(8,128)(2,1)S(1)} %fusion.38), channel_id=1, source_target_pairs={{0,24},{2,26},{4,28},{6,30},{8,0},{10,2},{12,4},{14,6},{16,8},{18,... | collective-permute-start | bytes 1179656 | tf_op jit(solution)/shard_map/ppermute | solution.py:236
  942.5 74.8 %collective-permute-start.104 = (bf16[2,4,128,1408]{3,2,1,0:T(8,128)(2,1)}, bf16[2,4,128,1408]{3,2,1,0:T(8,128)(2,1)}, u32[]{:S(2)}, u32[]{:S(2)}) collective-permute-start(bf16[2,4,128,1408]{3,2,1,0:T(8,128)(2,1)} %get-tuple-element.269), channel_id=1, source_target_pairs={{0,2},{2,0},{4,6},{6,4},{8,10},{10,8},{12,14},{14,12},{16,18},{18,... | collective-permute-start | bytes 8650760 | tf_op jit(solution)/shard_map/ppermute | solution.py:244
  942.5 67.2 %collective-permute-start.109 = (bf16[4,2,128,1280]{3,2,1,0:T(8,128)(2,1)}, bf16[4,2,128,1280]{3,2,1,0:T(8,128)(2,1)}, u32[]{:S(2)}, u32[]{:S(2)}) collective-permute-start(bf16[4,2,128,1280]{3,2,1,0:T(8,128)(2,1)} %get-tuple-element.271), channel_id=1, source_target_pairs={{0,2},{2,0},{4,6},{6,4},{8,10},{10,8},{12,14},{14,12},{16,18},{18,... | collective-permute-start | bytes 7864328 | tf_op jit(solution)/shard_map/ppermute | solution.py:244
  945.1 31.2 %collective-permute-start.93 = (bf16[192,768]{1,0:T(8,128)(2,1)}, bf16[192,768]{1,0:T(8,128)(2,1)}, u32[]{:S(2)}, u32[]{:S(2)}) collective-permute-start(bf16[192,768]{1,0:T(8,128)(2,1)} %get-tuple-element.368), channel_id=1, source_target_pairs={{0,8},{2,10},{4,12},{6,14},{8,16},{10,18},{12,20},{14,22},{16,24},... | collective-permute-start | bytes 884744 | tf_op jit(solution)/shard_map/ppermute | solution.py:236
  976.3 32.6 %collective-permute-start.103 = (bf16[192,2048]{1,0:T(8,128)(2,1)S(1)}, bf16[192,2048]{1,0:T(8,128)(2,1)S(1)}, u32[]{:S(2)}, u32[]{:S(2)}) collective-permute-start(bf16[192,2048]{1,0:T(8,128)(2,1)S(1)} %copy-done.56), channel_id=1, source_target_pairs={{0,1},{1,0},{2,3},{3,2},{4,5},{5,4},{6,7},{7,6},{8,9},{9,8},{10,11... | collective-permute-start | bytes 2359304 | tf_op jit(solution)/shard_map/ppermute | solution.py:248
  1015.2 31.2 %collective-permute-start.110 = (bf16[2,128,1280]{2,1,0:T(8,128)(2,1)S(1)}, bf16[2,128,1280]{2,1,0:T(8,128)(2,1)S(1)}, u32[]{:S(2)}, u32[]{:S(2)}) collective-permute-start(bf16[2,128,1280]{2,1,0:T(8,128)(2,1)S(1)} %get-tuple-element.350), channel_id=1, source_target_pairs={{0,24},{2,26},{4,28},{6,30},{8,0},{10,2},{12,4},{14,6},{16,8},{18,... | collective-permute-start | bytes 1966088 | tf_op jit(solution)/shard_map/ppermute | solution.py:236
  1019.9 37.5 %collective-permute-start.105 = (bf16[4,128,1408]{2,1,0:T(8,128)(2,1)S(1)}, bf16[4,128,1408]{2,1,0:T(8,128)(2,1)S(1)}, u32[]{:S(2)}, u32[]{:S(2)}) collective-permute-start(bf16[4,128,1408]{2,1,0:T(8,128)(2,1)S(1)} %slice_bitcast_fusion.6), channel_id=1, source_target_pairs={{0,4},{2,6},{4,0},{6,2},{8,12},{10,14},{12,8},{14,10},{16,20},{18,... | collective-permute-start | bytes 4325384 | tf_op jit(solution)/shard_map/ppermute | solution.py:240
  (168 other events, 2539.6 us)
Sparse Core Ops, SparseCore 0:
  11.7 110.8 all-gather.1
  834.3 126.8 reduce-scatter.1

commit v2 on v0

--- a/solution.py
+++ b/solution.py
@@ -296,20 +296,19 @@
     w5 = jnp.stack([w5, swap_y(w5)])
     w6 = jnp.stack([w6, swap_x(w6)])
     s1, s2, w5, w6, plan = lax.optimization_barrier((s1, s2, w5, w6, plan))
-    s1x, s2y = swap_x(s1), swap_y(s2)
     five = [shift_z(w5, 1), shift_z(w5, -1)]
     six = [shift_z(w6, 1), shift_z(w6, -1)]
-    far = aside(1, plan)
-    five, six, s1x, s2y, far = lax.optimization_barrier((five, six, s1x, s2y, far))
+    s1x, s2y = swap_x(s1), swap_y(s2)
     s1 = jnp.stack([s1, s1x])
     s2 = jnp.stack([s2, s2y])
     s1y, s2x = swap_y(s1), swap_x(s2)
     five.append(shift_z(five[0], 1))
     six.append(shift_z(six[1], -1))
-    plan, (five, six) = tied(plan, (five, six))
     o5 = jnp.stack([w5, five[0], five[2], five[1]])
     o6 = jnp.stack([w6, six[0], six[2], six[1]])
-    (s1y, s2x), near = tied((s1y, s2x), aside(0, plan))
+    far = aside(1, plan)
+    near = aside(0, plan)
+    (s1y, s2x), (near, far) = tied((s1y, s2x), (near, far))
     first = (s1, s1y, s2, s2x, o5, o6)
     return first, tuple(swap_c(v) for v in first), plan, (near, far)
 

time: 1010 us -> 1040 us (1.030)
  starting transfers between devices: 105 us -> 124 us
    ppermute x18, waiting for transfers between devices: 83.4 us -> 106 us  [swap_y(): return lax.ppermute(v, 'tensor', [(0, 1), (1, 0)])]
    ppermute x42, starting transfers between devices: 64 us -> 81.8 us  [shift_z(): lax.ppermute(v, 'dp', [(at(z, x, c), at(z + k, x, c)) for z, x, c in GRID])]
    ppermute x42, waiting for transfers between devices: 238 us -> 225 us  [shift_z(): lax.ppermute(v, 'dp', [(at(z, x, c), at(z + k, x, c)) for z, x, c in GRID])]
  transfers between devices with their start and end apart: 93 -> 93, of which waited for: 41 -> 41; matrix products, arithmetic and copies ran while one was open for 26% -> 25% of each run, Pallas kernels for 15% -> 15%
where the time goes in v2:
time: 1040 us; the launch traced here: 1030 us
  waiting for transfers between devices  418 us (40%)
  Pallas kernels  184 us (18%)
  starting transfers between devices  124 us (12%)
  matrix products  113 us (11%)
  other arithmetic  105 us (10%)
  local copies, waits for them, and re-layouts  70.4 us (7%)
  between operations  16.1 us (2%)
    ppermute x42, waiting for transfers between devices, shift_z(): lax.ppermute(v, 'dp', [(at(z, x, c), at(z + k, x, c)) for z, x, c in GRID])  225 us
    ppermute x18, waiting for transfers between devices, swap_y(): return lax.ppermute(v, 'tensor', [(0, 1), (1, 0)])  106 us
    ppermute x42, starting transfers between devices, shift_z(): lax.ppermute(v, 'dp', [(at(z, x, c), at(z + k, x, c)) for z, x, c in GRID])  81.8 us
    pallas_call x2, Pallas kernels, run_experts(): pl.pallas_call(expert_kernel, grid=(4,), in_specs=[pair(2, seq), pair(seq...  69.4 us
    all_gather x2, waiting for transfers between devices, gather_dp(): return lax.all_gather(v, 'dp', axis=0, tiled=True)  67.9 us
    convert_element_type x38, other arithmetic, add2(): return (a.astype(F32) + b.astype(F32)).astype(BF)  57.6 us
    dot_general x10, matrix products, dot(): lax.dot_general(a, b, (((ca,), (cb,)), ((), ())), preferred_element_type=...  46.7 us
    dot_general x3, matrix products, moe_small(): jnp.einsum(spec, a[1], b[1], preferred_element_type=F32)  37.1 us
  transfers between devices with their start and end apart: 93, of which 41 were waited for; matrix products, arithmetic and copies ran while one was open for 25% of the time, Pallas kernels for 15%

profile of v2, /device:TPU:0, one launch (start us, length us, event | category | flops | bytes accessed | tf_op | source)
XLA Modules:
  0.0 1030.4 jit_solution(12944403802435803148)
XLA Ops:
  14.7 17.5 %collective-permute-done.16 = bf16[192,2048]{1,0:T(8,128)(2,1)S(1)} collective-permute-done((bf16[192,2048]{1,0:T(8,128)(2,1)S(1)}, bf16[192,2048]{1,0:T(8,128)(2,1)S(1)}, u32[]{:S(2)}, u32[]{:S(2)}) %collective-permute-start.16) | collective-permute-done | bytes 786464 | tf_op jit(solution)/shard_map/ppermute | solution.py:248
  45.1 7.7 collective-permute-done
  54.6 67.9 %all-gather.3.cloned.1.call-done = bf16[2048,4736]{0,1:T(8,128)(2,1)} async-done(((bf16[128,4736]{0,1:T(8,128)(2,1)}), bf16[2048,4736]{0,1:T(8,128)(2,1)}) %all-gather.3.cloned.1.call-update) | async-done | bytes 19398672 | tf_op jit(solution)/shard_map/all_gather | solution.py:177
  128.5 11.1 %fusion.2.q_raw.k_raw.v_raw = f32[384,2560]{1,0:T(8,128)} fusion(bf16[384,2048]{1,0:T(8,128)(2,1)S(1)} %fusion.14.left, bf16[2048,4736]{0,1:T(8,128)(2,1)} %all-gather.3.cloned.1.call-done), kind=kOutput, calls=%fused_computation.7 | convolution fusion | flops 4026531840 | bytes 15990784 | tf_op jit(solution)/shard_map/dot_general | solution.py:17
  139.6 14.4 %attend.1 = bf16[384,2048]{1,0:T(8,128)(2,1)} custom-call(f32[384,2560]{1,0:T(8,128)} %fusion.2.q_raw.k_raw.v_raw, f32[384,2560]{1,0:T(8,128)} %fusion.2.q_raw.k_raw.v_raw, f32[384,2560]{1,0:T(8,128)} %fusion.2.q_raw.k_raw.v_raw, f32[8,128]{1,0:T(8,128)} %select_maximum_fusion.gains, f32[384,128]{1,0:T(8,128)} %get-tuple-element.377.cos, ...), custom_call_target="tpu_custom_call" | custom-call | tf_op jit(solution)/shard_map/attend/pallas_call | solution.py:120
  154.0 9.2 fusion.6
  185.6 13.6 %collective-permute-done.1 = bf16[192,2048]{1,0:T(8,128)(2,1)S(1)} collective-permute-done((bf16[192,2048]{1,0:T(8,128)(2,1)S(1)}, bf16[192,2048]{1,0:T(8,128)(2,1)S(1)}, u32[]{:S(2)}, u32[]{:S(2)}) %collective-permute-start.1) | collective-permute-done | bytes 786464 | tf_op jit(solution)/shard_map/ppermute | solution.py:248
  213.7 7.0 collective-permute-done.6
  225.8 20.9 %collective-permute-done.2 = bf16[192,768]{1,0:T(8,128)(2,1)S(1)} collective-permute-done((bf16[192,768]{1,0:T(8,128)(2,1)S(1)}, bf16[192,768]{1,0:T(8,128)(2,1)S(1)}, u32[]{:S(2)}, u32[]{:S(2)}) %collective-permute-start.2) | collective-permute-done | bytes 294944 | tf_op jit(solution)/shard_map/ppermute | solution.py:236
  248.2 9.2 collective-permute-done.7
  257.6 12.5 %collective-permute-done.4 = bf16[192,768]{1,0:T(8,128)(2,1)S(1)} collective-permute-done((bf16[192,768]{1,0:T(8,128)(2,1)S(1)}, bf16[192,768]{1,0:T(8,128)(2,1)S(1)}, u32[]{:S(2)}, u32[]{:S(2)}) %collective-permute-start.4) | collective-permute-done | bytes 294944 | tf_op jit(solution)/shard_map/ppermute | solution.py:236
  270.1 14.3 %collective-permute-done.3 = bf16[192,768]{1,0:T(8,128)(2,1)S(1)} collective-permute-done((bf16[192,768]{1,0:T(8,128)(2,1)S(1)}, bf16[192,768]{1,0:T(8,128)(2,1)S(1)}, u32[]{:S(2)}, u32[]{:S(2)}) %collective-permute-start.3) | collective-permute-done | bytes 294944 | tf_op jit(solution)/shard_map/ppermute | solution.py:236
  285.3 25.2 %collective-permute-done.14 = bf16[4,192,768]{2,1,0:T(8,128)(2,1)S(1)} collective-permute-done((bf16[4,192,768]{2,1,0:T(8,128)(2,1)S(1)}, bf16[4,192,768]{2,1,0:T(8,128)(2,1)S(1)}, u32[]{:S(2)}, u32[]{:S(2)}) %collective-permute-start.14) | collective-permute-done | bytes 1179680 | tf_op jit(solution)/shard_map/ppermute | solution.py:248
  318.3 10.0 collective-permute-done.20
  335.4 14.5 %collective-permute-done.17 = bf16[2,2,192,384]{3,2,1,0:T(8,128)(2,1)} collective-permute-done((bf16[2,2,192,384]{3,2,1,0:T(8,128)(2,1)}, bf16[2,2,192,384]{3,2,1,0:T(8,128)(2,1)}, u32[]{:S(2)}, u32[]{:S(2)}) %collective-permute-start.17) | collective-permute-done | bytes 589856 | tf_op jit(solution)/shard_map/ppermute | solution.py:236
  350.0 10.5 %collective-permute-start.18 = (bf16[2,2,192,384]{3,2,1,0:T(8,128)(2,1)}, bf16[2,2,192,384]{3,2,1,0:T(8,128)(2,1)}, u32[]{:S(2)}, u32[]{:S(2)}) collective-permute-start(bf16[2,2,192,384]{3,2,1,0:T(8,128)(2,1)} %collective-permute-done.17), channel_id=1, source_target_pairs={{0,8},{2,10},{4,12},{6,14},{8,16},{10,18},{12,20},{14,22},{16,24},... | collective-permute-start | bytes 1769480 | tf_op jit(solution)/shard_map/ppermute | solution.py:236
  365.5 9.2 collective-permute-done.18
  378.2 16.0 %cots.3 = (bf16[2,4,256,2048]{3,2,1,0:T(8,128)(2,1)}, f32[2,4,256,384]{3,2,1,0:T(8,128)}) custom-call(s32[8]{0:T(128)} %get-tuple-element.138.where, f32[8,2,384]{2,1,0:T(2,128)} %copy.120.rank, bf16[16,384,2048]{2,1,0:T(8,128)(2,1)} %bitcast.320, bf16[16,384,2048]{2,1,0:T(8,128)(2,1)} %bitcast.321, bf16[2,384,2048]{2,1,0:T(8,128)(2,1)} %down.7), custom_call_target="tpu_custom_call" | custom-call | tf_op jit(solution)/shard_map/cots/pallas_call | solution.py:550
  394.2 15.7 %cots.2 = (bf16[2,4,256,2048]{3,2,1,0:T(8,128)(2,1)}, f32[2,4,256,384]{3,2,1,0:T(8,128)}) custom-call(s32[8]{0:T(128)} %get-tuple-element.134.where, f32[8,2,384]{2,1,0:T(2,128)} %copy.119.rank, bf16[16,384,2048]{2,1,0:T(8,128)(2,1)} %bitcast.322, bf16[16,384,2048]{2,1,0:T(8,128)(2,1)} %bitcast.323, bf16[2,384,2048]{2,1,0:T(8,128)(2,1)} %down.7), custom_call_target="tpu_custom_call" | custom-call | tf_op jit(solution)/shard_map/cots/pallas_call | solution.py:550
  421.7 34.5 %experts.3 = (bf16[2,4,256,2048]{3,2,1,0:T(8,128)(2,1)}, bf16[2,4,256,384]{3,2,1,0:T(8,128)(2,1)}, bf16[2,4,256,384]{3,2,1,0:T(8,128)(2,1)}, bf16[2,4,256,384]{3...) custom-call(f32[8,2,384]{2,1,0:T(2,128)} %copy.122.rank, ...), custom_call_target="tpu_custom_call" | custom-call | tf_op jit(solution)/shard_map/experts/pallas_call | solution.py:573
  458.4 34.9 %experts.2 = (bf16[2,4,256,2048]{3,2,1,0:T(8,128)(2,1)}, bf16[2,4,256,384]{3,2,1,0:T(8,128)(2,1)}, bf16[2,4,256,384]{3,2,1,0:T(8,128)(2,1)}, bf16[2,4,256,384]{3...) custom-call(f32[8,2,384]{2,1,0:T(2,128)} %copy.121.rank, ...), custom_call_target="tpu_custom_call" | custom-call | tf_op jit(solution)/shard_map/experts/pallas_call | solution.py:573
  493.3 12.4 %outs.2 = (bf16[2,2,4,192,768]{4,3,2,1,0:T(8,128)(2,1)}, bf16[2,2,4,192,768]{4,3,2,1,0:T(8,128)(2,1)}, bf16[4,2,2,192,256]{4,3,2,1,0:T(8,128)(2,1)}, bf16[4,2,2,192,256]{4,3,2,1,0:T(8,128)(2,1)}) custom-call(f32[8,384,2]{2,1,0:T(8,128)} %get-tuple-element.130.rank_t, bf16[2,4,256,384]{3,2,1,0:T(8,128)(2,1)} %get-tuple-element.163.scaled, ...), custom_call_target="tpu_custom_call" | custom-call | tf_op jit(solution)/shard_map/outs/pallas_call | solution.py:613
  512.3 11.2 %fusion.125 = f32[2,2048,384,1]{2,1,3,0:T(8,128)} fusion(bf16[2,4,256,2048]{3,2,1,0:T(8,128)(2,1)} %get-tuple-element.208, bf16[2,4,256,384]{3,2,1,0:T(8,128)(2,1)} %get-tuple-element.179), kind=kOutput, calls=%fused_computation.379 | convolution fusion | flops 3221225472 | bytes 16252928 | tf_op jit(solution)/shard_map/egsd,egsf->edf/dot_general | solution.py:667
  551.6 8.9 collective-permute-start.40
  565.8 9.6 bitcast_add_fusion.2
  575.4 12.6 %outs.3 = (bf16[2,2,4,192,768]{4,3,2,1,0:T(8,128)(2,1)}, bf16[2,2,4,192,768]{4,3,2,1,0:T(8,128)(2,1)}, bf16[4,2,2,192,256]{4,3,2,1,0:T(8,128)(2,1)}, bf16[4,2,2,192,256]{4,3,2,1,0:T(8,128)(2,1)}) custom-call(f32[8,384,2]{2,1,0:T(8,128)} %get-tuple-element.150.rank_t, bf16[2,4,256,384]{3,2,1,0:T(8,128)(2,1)} %get-tuple-element.168.scaled, ...), custom_call_target="tpu_custom_call" | custom-call | tf_op jit(solution)/shard_map/outs/pallas_call | solution.py:613
  610.2 13.0 %bitcast_add_fusion.1 = f32[2,2048,384]{2,1,0:T(8,128)} fusion(f32[2,2048,384,1]{2,1,3,0:T(8,128)} %fusion.125, bf16[2,4,256,2048]{3,2,1,0:T(8,128)(2,1)} %get-tuple-element.210, bf16[2,4,256,384]{3,2,1,0:T(8,128)(2,1)} %get-tuple-element.180), kind=kOutput, calls=%fused_computation.16 | convolution fusion | flops 3222798336 | bytes 22544384 | tf_op jit(solution)/shard_map/egsd,egsf->edf/dot_general | solution.py:667
  626.4 11.0 %collective-permute-done.42 = bf16[4,192,768]{2,1,0:T(8,128)(2,1)S(1)} collective-permute-done((bf16[4,192,768]{2,1,0:T(8,128)(2,1)}, bf16[4,192,768]{2,1,0:T(8,128)(2,1)S(1)}, u32[]{:S(2)}, u32[]{:S(2)}) %collective-permute-start.42) | collective-permute-done | bytes 1179680 | tf_op jit(solution)/shard_map/ppermute | solution.py:248
  649.9 8.5 collective-permute-done.49
  669.6 7.2 collective-permute-done.45
  682.4 8.4 collective-permute-done.47
  696.5 7.6 add_convert_fusion
  743.7 8.0 fusion.16.d_context
  751.6 12.6 %attend_back.2 = (bf16[384,1024]{1,0:T(8,128)(2,1)}, bf16[384,128]{1,0:T(8,128)(2,1)}, bf16[384,128]{1,0:T(8,128)(2,1)}, f32[8,128]{1,0:T(8,128)}) custom-call(f32[384,2560]{1,0:T(8,128)} %fusion.2.q_raw.k_raw.v_raw, f32[384,2560]{1,0:T(8,128)} %fusion.2.q_raw.k_raw.v_raw, f32[384,2560]{1,0:T(8,128)} %fusion.2.q_raw.k_raw.v_raw, ...), custom_call_target="tpu_custom_call" | custom-call | tf_op jit(solution)/shard_map/attend_back/pallas_call | solution.py:143
  764.3 11.7 %fusion.126 = f32[2,2048,384,1]{2,1,3,0:T(8,128)} fusion(bf16[2,4,256,2048]{3,2,1,0:T(8,128)(2,1)} %get-tuple-element.208, bf16[2,4,256,384]{3,2,1,0:T(8,128)(2,1)} %get-tuple-element.209), kind=kOutput, calls=%fused_computation.380 | convolution fusion | flops 3221225472 | bytes 16252928 | tf_op jit(solution)/shard_map/egsd,egsf->edf/dot_general | solution.py:667
  776.0 14.6 %bitcast_add_fusion = f32[2,2048,384]{2,1,0:T(8,128)} fusion(f32[2,2048,384,1]{2,1,3,0:T(8,128)} %fusion.126, bf16[2,4,256,2048]{3,2,1,0:T(8,128)(2,1)} %get-tuple-element.210, bf16[2,4,256,384]{3,2,1,0:T(8,128)(2,1)} %get-tuple-element.211), kind=kOutput, calls=%fused_computation.15 | convolution fusion | flops 3222798336 | bytes 22544384 | tf_op jit(solution)/shard_map/egsd,egsf->edf/dot_general | solution.py:667
  798.7 12.7 %attend_back.3 = (bf16[384,1024]{1,0:T(8,128)(2,1)}, bf16[384,128]{1,0:T(8,128)(2,1)}, bf16[384,128]{1,0:T(8,128)(2,1)}, f32[8,128]{1,0:T(8,128)}) custom-call(f32[384,2560]{1,0:T(8,128)} %fusion.2.q_raw.k_raw.v_raw, f32[384,2560]{1,0:T(8,128)} %fusion.2.q_raw.k_raw.v_raw, f32[384,2560]{1,0:T(8,128)} %fusion.2.q_raw.k_raw.v_raw, ...), custom_call_target="tpu_custom_call" | custom-call | tf_op jit(solution)/shard_map/attend_back/pallas_call | solution.py:143
  823.9 11.1 %collective-permute-done.67 = bf16[2,2,192,256]{3,2,1,0:T(8,128)(2,1)S(1)} collective-permute-done((bf16[2,2,192,256]{3,2,1,0:T(8,128)(2,1)S(1)}, bf16[2,2,192,256]{3,2,1,0:T(8,128)(2,1)S(1)}, u32[]{:S(2)}, u32[]{:S(2)}) %collective-permute-start.67) | collective-permute-done | bytes 393248 | tf_op jit(solution)/shard_map/ppermute | solution.py:236
  836.2 15.6 %collective-permute-done.65 = bf16[2,2,192,256]{3,2,1,0:T(8,128)(2,1)S(1)} collective-permute-done((bf16[2,2,192,256]{3,2,1,0:T(8,128)(2,1)S(1)}, bf16[2,2,192,256]{3,2,1,0:T(8,128)(2,1)S(1)}, u32[]{:S(2)}, u32[]{:S(2)}) %collective-permute-start.65) | collective-permute-done | bytes 393248 | tf_op jit(solution)/shard_map/ppermute | solution.py:236
  855.7 9.2 grad.3
  880.1 9.2 grad.2
  898.2 7.8 collective-permute-done.72
  909.6 17.1 %collective-permute-done.77 = bf16[192,256]{1,0:T(8,128)(2,1)S(1)} collective-permute-done((bf16[192,256]{1,0:T(8,128)(2,1)S(1)}, bf16[192,256]{1,0:T(8,128)(2,1)S(1)}, u32[]{:S(2)}, u32[]{:S(2)}) %collective-permute-start.77) | collective-permute-done | bytes 98336 | tf_op jit(solution)/shard_map/ppermute | solution.py:248
  929.8 8.8 collective-permute-done.71
  950.7 12.0 %collective-permute-done.86 = bf16[2,128,1280]{2,1,0:T(8,128)(2,1)S(1)} collective-permute-done((bf16[2,128,1280]{2,1,0:T(8,128)(2,1)S(1)}, bf16[2,128,1280]{2,1,0:T(8,128)(2,1)S(1)}, u32[]{:S(2)}, u32[]{:S(2)}) %collective-permute-start.86) | collective-permute-done | bytes 655392 | tf_op jit(solution)/shard_map/ppermute | solution.py:236
  962.8 8.3 collective-permute-start.87
  975.4 12.0 %collective-permute-done.87 = bf16[2,128,1280]{2,1,0:T(8,128)(2,1)S(1)} collective-permute-done((bf16[2,128,1280]{2,1,0:T(8,128)(2,1)S(1)}, bf16[2,128,1280]{2,1,0:T(8,128)(2,1)S(1)}, u32[]{:S(2)}, u32[]{:S(2)}) %collective-permute-start.87) | collective-permute-done | bytes 655392 | tf_op jit(solution)/shard_map/ppermute | solution.py:236
  990.9 13.5 %collective-permute-done.82 = bf16[128,1408]{1,0:T(8,128)(2,1)S(1)} collective-permute-done((bf16[128,1408]{1,0:T(8,128)(2,1)S(1)}, bf16[128,1408]{1,0:T(8,128)(2,1)S(1)}, u32[]{:S(2)}, u32[]{:S(2)}) %collective-permute-start.82) | collective-permute-done | bytes 360480 | tf_op jit(solution)/shard_map/ppermute | solution.py:236
  (529 shorter events, 343.9 us)
Async XLA Ops:
  7.3 115.2 %all-gather.3.cloned.1.call-start = ((), (), s32[]{:S(2)}) async-start(), calls=%async_computation.1 | async-start | bytes 20611072 | tf_op jit(solution)/shard_map/all_gather | solution.py:177
  11.6 366.7 %all-gather.5.cloned.1.call-start = ((), (), s32[]{:S(2)}) async-start(), calls=%async_computation.2 | async-start | bytes 26738688 | tf_op jit(solution)/shard_map/all_gather | solution.py:177
  33.7 987.2 %reduce-scatter.2.cloned.1.call-start = ((), (), s32[]{:S(2)}) async-start(), calls=%async_computation.3 | async-start | bytes 8912896 | tf_op jit(solution)/shard_map/reduce_scatter | solution.py:189
  207.8 40.4 %collective-permute-start.5 = (bf16[192,768]{1,0:T(8,128)(2,1)S(1)}, bf16[192,768]{1,0:T(8,128)(2,1)S(1)}, u32[]{:S(2)}, u32[]{:S(2)}) collective-permute-start(bf16[192,768]{1,0:T(8,128)(2,1)S(1)} %get-tuple-element.347), channel_id=1, source_target_pairs={{0,8},{2,10},{4,12},{6,14},{8,16},{10,18},{12,20},{14,22},{16,24},... | collective-permute-start | bytes 884744 | tf_op jit(solution)/shard_map/ppermute | solution.py:236
  208.8 37.9 %collective-permute-start.2 = (bf16[192,768]{1,0:T(8,128)(2,1)S(1)}, bf16[192,768]{1,0:T(8,128)(2,1)S(1)}, u32[]{:S(2)}, u32[]{:S(2)}) collective-permute-start(bf16[192,768]{1,0:T(8,128)(2,1)S(1)} %get-tuple-element.348), channel_id=1, source_target_pairs={{0,8},{2,10},{4,12},{6,14},{8,16},{10,18},{12,20},{14,22},{16,24},... | collective-permute-start | bytes 884744 | tf_op jit(solution)/shard_map/ppermute | solution.py:236
  213.2 34.2 %collective-permute-start.9 = (bf16[2,192,384]{2,1,0:T(8,128)(2,1)S(1)}, bf16[2,192,384]{2,1,0:T(8,128)(2,1)S(1)}, u32[]{:S(2)}, u32[]{:S(2)}) collective-permute-start(bf16[2,192,384]{2,1,0:T(8,128)(2,1)S(1)} %get-tuple-element.352), channel_id=1, source_target_pairs={{0,1},{1,0},{2,3},{3,2},{4,5},{5,4},{6,7},{7,6},{8,9},{9,8},{10,11... | collective-permute-start | bytes 884744 | tf_op jit(solution)/shard_map/ppermute | solution.py:248
  220.7 36.7 %collective-permute-start.7 = (bf16[192,768]{1,0:T(8,128)(2,1)S(1)}, bf16[192,768]{1,0:T(8,128)(2,1)S(1)}, u32[]{:S(2)}, u32[]{:S(2)}) collective-permute-start(bf16[192,768]{1,0:T(8,128)(2,1)S(1)} %collective-permute-done.6), channel_id=1, source_target_pairs={{0,24},{2,26},{4,28},{6,30},{8,0},{10,2},{12,4},{14,6},{16,8},{18,... | collective-permute-start | bytes 884744 | tf_op jit(solution)/shard_map/ppermute | solution.py:236
  225.8 44.3 %collective-permute-start.4 = (bf16[192,768]{1,0:T(8,128)(2,1)S(1)}, bf16[192,768]{1,0:T(8,128)(2,1)S(1)}, u32[]{:S(2)}, u32[]{:S(2)}) collective-permute-start(bf16[192,768]{1,0:T(8,128)(2,1)S(1)} %get-tuple-element.348), channel_id=1, source_target_pairs={{0,24},{2,26},{4,28},{6,30},{8,0},{10,2},{12,4},{14,6},{16,8},{18,... | collective-permute-start | bytes 884744 | tf_op jit(solution)/shard_map/ppermute | solution.py:236
  246.7 37.6 %collective-permute-start.3 = (bf16[192,768]{1,0:T(8,128)(2,1)S(1)}, bf16[192,768]{1,0:T(8,128)(2,1)S(1)}, u32[]{:S(2)}, u32[]{:S(2)}) collective-permute-start(bf16[192,768]{1,0:T(8,128)(2,1)S(1)} %collective-permute-done.2), channel_id=1, source_target_pairs={{0,8},{2,10},{4,12},{6,14},{8,16},{10,18},{12,20},{14,22},{16,24},... | collective-permute-start | bytes 884744 | tf_op jit(solution)/shard_map/ppermute | solution.py:236
  284.7 27.7 %collective-permute-start.12 = (bf16[4,192,768]{2,1,0:T(8,128)(2,1)S(1)}, bf16[4,192,768]{2,1,0:T(8,128)(2,1)S(1)}, u32[]{:S(2)}, u32[]{:S(2)}) collective-permute-start(bf16[4,192,768]{2,1,0:T(8,128)(2,1)S(1)} %pad_maximum_fusion.8), channel_id=1, source_target_pairs={{0,4},{2,6},{4,0},{6,2},{8,12},{10,14},{12,8},{14,10},{16,20},{18,... | collective-permute-start | bytes 3538952 | tf_op jit(solution)/shard_map/ppermute | solution.py:240
  285.3 30.2 %collective-permute-start.21 = (bf16[2,2,192,256]{3,2,1,0:T(8,128)(2,1)S(1)}, bf16[2,2,192,256]{3,2,1,0:T(8,128)(2,1)S(1)}, u32[]{:S(2)}, u32[]{:S(2)}) collective-permute-start(bf16[2,2,192,256]{3,2,1,0:T(8,128)(2,1)S(1)} %pad_maximum_fusion.11), channel_id=1, source_target_pairs={{0,24},{2,26},{4,28},{6,30},{8,0},{10,2},{12,4},{14,6},{16,8},{18,... | collective-permute-start | bytes 1179656 | tf_op jit(solution)/shard_map/ppermute | solution.py:236
  312.1 97.8 %collective-permute-start.15 = (bf16[2,4,192,768]{3,2,1,0:T(8,128)(2,1)}, bf16[2,4,192,768]{3,2,1,0:T(8,128)(2,1)}, u32[]{:S(2)}, u32[]{:S(2)}) collective-permute-start(bf16[2,4,192,768]{3,2,1,0:T(8,128)(2,1)} %pad_maximum_fusion.2.x2a), channel_id=1, source_target_pairs={{0,4},{2,6},{4,0},{6,2},{8,12},{10,14},{12,8},{14,10},{16,20},{18,... | collective-permute-start | bytes 7077896 | tf_op jit(solution)/shard_map/ppermute | solution.py:240
  314.0 96.4 %collective-permute-start.13 = (bf16[2,4,192,768]{3,2,1,0:T(8,128)(2,1)}, bf16[2,4,192,768]{3,2,1,0:T(8,128)(2,1)}, u32[]{:S(2)}, u32[]{:S(2)}) collective-permute-start(bf16[2,4,192,768]{3,2,1,0:T(8,128)(2,1)} %pad_maximum_fusion.1.x1a), channel_id=1, source_target_pairs={{0,1},{1,0},{2,3},{3,2},{4,5},{5,4},{6,7},{7,6},{8,9},{9,8},{10,11... | collective-permute-start | bytes 7077896 | tf_op jit(solution)/shard_map/ppermute | solution.py:248
  331.5 79.1 %collective-permute-start.28 = (bf16[4,2,2,192,256]{4,3,2,1,0:T(8,128)(2,1)S(1)}, bf16[4,2,2,192,256]{4,3,2,1,0:T(8,128)(2,1)}, u32[]{:S(2)}, u32[]{:S(2)}) collective-permute-start(bf16[4,2,2,192,256]{4,3,2,1,0:T(8,128)(2,1)S(1)} %pad_maximum_fusion.6.x6), channel_id=1, source_target_pairs={{0,2},{2,0},{4,6},{6,4},{8,10},{10,8},{12,14},{14,12},{16,18},{18,... | collective-permute-start | bytes 4718600 | tf_op jit(solution)/shard_map/ppermute | solution.py:244
  331.9 33.6 %collective-permute-start.19 = (bf16[2,2,192,384]{3,2,1,0:T(8,128)(2,1)}, bf16[2,2,192,384]{3,2,1,0:T(8,128)(2,1)}, u32[]{:S(2)}, u32[]{:S(2)}) collective-permute-start(bf16[2,2,192,384]{3,2,1,0:T(8,128)(2,1)} %pad_maximum_fusion.10), channel_id=1, source_target_pairs={{0,24},{2,26},{4,28},{6,30},{8,0},{10,2},{12,4},{14,6},{16,8},{18,... | collective-permute-start | bytes 1769480 | tf_op jit(solution)/shard_map/ppermute | solution.py:236
  365.5 49.5 %collective-permute-start.25 = (bf16[2,4,192,768]{3,2,1,0:T(8,128)(2,1)}, bf16[2,4,192,768]{3,2,1,0:T(8,128)(2,1)}, u32[]{:S(2)}, u32[]{:S(2)}) collective-permute-start(bf16[2,4,192,768]{3,2,1,0:T(8,128)(2,1)} %pad_maximum_fusion.2.x2a), channel_id=1, source_target_pairs={{0,2},{2,0},{4,6},{6,4},{8,10},{10,8},{12,14},{14,12},{16,18},{18,... | collective-permute-start | bytes 7077896 | tf_op jit(solution)/shard_map/ppermute | solution.py:244
  374.7 40.2 %collective-permute-start.23 = (bf16[2,4,192,768]{3,2,1,0:T(8,128)(2,1)}, bf16[2,4,192,768]{3,2,1,0:T(8,128)(2,1)}, u32[]{:S(2)}, u32[]{:S(2)}) collective-permute-start(bf16[2,4,192,768]{3,2,1,0:T(8,128)(2,1)} %pad_maximum_fusion.1.x1a), channel_id=1, source_target_pairs={{0,2},{2,0},{4,6},{6,4},{8,10},{10,8},{12,14},{14,12},{16,18},{18,... | collective-permute-start | bytes 7077896 | tf_op jit(solution)/shard_map/ppermute | solution.py:244
  456.2 77.2 %collective-permute-start.31 = (bf16[2,2,4,192,768]{4,3,2,1,0:T(8,128)(2,1)}, bf16[2,2,4,192,768]{4,3,2,1,0:T(8,128)(2,1)}, u32[]{:S(2)}, u32[]{:S(2)}) collective-permute-start(bf16[2,2,4,192,768]{4,3,2,1,0:T(8,128)(2,1)} %get-tuple-element.158), channel_id=1, source_target_pairs={{0,2},{2,0},{4,6},{6,4},{8,10},{10,8},{12,14},{14,12},{16,18},{18,... | collective-permute-start | bytes 14155784 | tf_op jit(solution)/shard_map/ppermute | solution.py:244
  456.6 84.1 %collective-permute-start.29 = (bf16[2,2,4,192,768]{4,3,2,1,0:T(8,128)(2,1)}, bf16[2,2,4,192,768]{4,3,2,1,0:T(8,128)(2,1)}, u32[]{:S(2)}, u32[]{:S(2)}) collective-permute-start(bf16[2,2,4,192,768]{4,3,2,1,0:T(8,128)(2,1)} %get-tuple-element.156), channel_id=1, source_target_pairs={{0,2},{2,0},{4,6},{6,4},{8,10},{10,8},{12,14},{14,12},{16,18},{18,... | collective-permute-start | bytes 14155784 | tf_op jit(solution)/shard_map/ppermute | solution.py:244
  525.9 38.5 %collective-permute-start.38 = (bf16[2,2,192,256]{3,2,1,0:T(8,128)(2,1)}, bf16[2,2,192,256]{3,2,1,0:T(8,128)(2,1)}, u32[]{:S(2)}, u32[]{:S(2)}) collective-permute-start(bf16[2,2,192,256]{3,2,1,0:T(8,128)(2,1)} %get-tuple-element.326), channel_id=1, source_target_pairs={{0,24},{2,26},{4,28},{6,30},{8,0},{10,2},{12,4},{14,6},{16,8},{18,... | collective-permute-start | bytes 1179656 | tf_op jit(solution)/shard_map/ppermute | solution.py:236
  532.6 27.9 %collective-permute-start.35 = (bf16[2,2,192,384]{3,2,1,0:T(8,128)(2,1)}, bf16[2,2,192,384]{3,2,1,0:T(8,128)(2,1)}, u32[]{:S(2)}, u32[]{:S(2)}) collective-permute-start(bf16[2,2,192,384]{3,2,1,0:T(8,128)(2,1)} %get-tuple-element.317), channel_id=1, source_target_pairs={{0,24},{2,26},{4,28},{6,30},{8,0},{10,2},{12,4},{14,6},{16,8},{18,... | collective-permute-start | bytes 1769480 | tf_op jit(solution)/shard_map/ppermute | solution.py:236
  538.9 55.5 %collective-permute-start.32 = (bf16[2,4,192,768]{3,2,1,0:T(8,128)(2,1)}, bf16[2,4,192,768]{3,2,1,0:T(8,128)(2,1)}, u32[]{:S(2)}, u32[]{:S(2)}) collective-permute-start(bf16[2,4,192,768]{3,2,1,0:T(8,128)(2,1)} %slice_bitcast_fusion), channel_id=1, source_target_pairs={{0,4},{2,6},{4,0},{6,2},{8,12},{10,14},{12,8},{14,10},{16,20},{18,... | collective-permute-start | bytes 7077896 | tf_op jit(solution)/shard_map/ppermute | solution.py:240
  548.8 52.7 %collective-permute-start.30 = (bf16[2,4,192,768]{3,2,1,0:T(8,128)(2,1)}, bf16[2,4,192,768]{3,2,1,0:T(8,128)(2,1)}, u32[]{:S(2)}, u32[]{:S(2)}) collective-permute-start(bf16[2,4,192,768]{3,2,1,0:T(8,128)(2,1)} %slice_bitcast_fusion.2), channel_id=1, source_target_pairs={{0,1},{1,0},{2,3},{3,2},{4,5},{5,4},{6,7},{7,6},{8,9},{9,8},{10,11... | collective-permute-start | bytes 7077896 | tf_op jit(solution)/shard_map/ppermute | solution.py:248
  551.6 36.4 %collective-permute-start.40 = (bf16[2,2,192,256]{3,2,1,0:T(8,128)(2,1)}, bf16[2,2,192,256]{3,2,1,0:T(8,128)(2,1)S(1)}, u32[]{:S(2)}, u32[]{:S(2)}) collective-permute-start(bf16[2,2,192,256]{3,2,1,0:T(8,128)(2,1)} %fusion.41), channel_id=1, source_target_pairs={{0,8},{2,10},{4,12},{6,14},{8,16},{10,18},{12,20},{14,22},{16,24},... | collective-permute-start | bytes 1179656 | tf_op jit(solution)/shard_map/ppermute | solution.py:236
  560.5 28.6 %collective-permute-start.34 = (bf16[2,2,192,384]{3,2,1,0:T(8,128)(2,1)}, bf16[2,2,192,384]{3,2,1,0:T(8,128)(2,1)S(1)}, u32[]{:S(2)}, u32[]{:S(2)}) collective-permute-start(bf16[2,2,192,384]{3,2,1,0:T(8,128)(2,1)} %get-tuple-element.316), channel_id=1, source_target_pairs={{0,8},{2,10},{4,12},{6,14},{8,16},{10,18},{12,20},{14,22},{16,24},... | collective-permute-start | bytes 1769480 | tf_op jit(solution)/shard_map/ppermute | solution.py:236
  564.4 28.8 %collective-permute-start.36 = (bf16[2,2,192,384]{3,2,1,0:T(8,128)(2,1)S(1)}, bf16[2,2,192,384]{3,2,1,0:T(8,128)(2,1)S(1)}, u32[]{:S(2)}, u32[]{:S(2)}) collective-permute-start(bf16[2,2,192,384]{3,2,1,0:T(8,128)(2,1)S(1)} %fusion.31), channel_id=1, source_target_pairs={{0,24},{2,26},{4,28},{6,30},{8,0},{10,2},{12,4},{14,6},{16,8},{18,... | collective-permute-start | bytes 1769480 | tf_op jit(solution)/shard_map/ppermute | solution.py:236
  607.1 30.3 %collective-permute-start.42 = (bf16[4,192,768]{2,1,0:T(8,128)(2,1)}, bf16[4,192,768]{2,1,0:T(8,128)(2,1)S(1)}, u32[]{:S(2)}, u32[]{:S(2)}) collective-permute-start(bf16[4,192,768]{2,1,0:T(8,128)(2,1)} %slice_bitcast_fusion.10), channel_id=1, source_target_pairs={{0,1},{1,0},{2,3},{3,2},{4,5},{5,4},{6,7},{7,6},{8,9},{9,8},{10,11... | collective-permute-start | bytes 3538952 | tf_op jit(solution)/shard_map/ppermute | solution.py:248
  609.0 28.7 %collective-permute-start.41 = (bf16[4,192,768]{2,1,0:T(8,128)(2,1)}, bf16[4,192,768]{2,1,0:T(8,128)(2,1)S(1)}, u32[]{:S(2)}, u32[]{:S(2)}) collective-permute-start(bf16[4,192,768]{2,1,0:T(8,128)(2,1)} %slice_bitcast_fusion.11), channel_id=1, source_target_pairs={{0,4},{2,6},{4,0},{6,2},{8,12},{10,14},{12,8},{14,10},{16,20},{18,... | collective-permute-start | bytes 3538952 | tf_op jit(solution)/shard_map/ppermute | solution.py:240
  610.2 80.8 %collective-permute-start.51 = (bf16[2,2,4,192,768]{4,3,2,1,0:T(8,128)(2,1)}, bf16[2,2,4,192,768]{4,3,2,1,0:T(8,128)(2,1)}, u32[]{:S(2)}, u32[]{:S(2)}) collective-permute-start(bf16[2,2,4,192,768]{4,3,2,1,0:T(8,128)(2,1)} %get-tuple-element.184), channel_id=1, source_target_pairs={{0,2},{2,0},{4,6},{6,4},{8,10},{10,8},{12,14},{14,12},{16,18},{18,... | collective-permute-start | bytes 14155784 | tf_op jit(solution)/shard_map/ppermute | solution.py:244
  623.2 42.1 %collective-permute-start.56 = (bf16[4,2,2,192,256]{4,3,2,1,0:T(8,128)(2,1)}, bf16[4,2,2,192,256]{4,3,2,1,0:T(8,128)(2,1)S(1)}, u32[]{:S(2)}, u32[]{:S(2)}) collective-permute-start(bf16[4,2,2,192,256]{4,3,2,1,0:T(8,128)(2,1)} %get-tuple-element.194), channel_id=1, source_target_pairs={{0,2},{2,0},{4,6},{6,4},{8,10},{10,8},{12,14},{14,12},{16,18},{18,... | collective-permute-start | bytes 4718600 | tf_op jit(solution)/shard_map/ppermute | solution.py:244
  625.4 51.5 %collective-permute-start.55 = (bf16[4,2,2,192,256]{4,3,2,1,0:T(8,128)(2,1)}, bf16[4,2,2,192,256]{4,3,2,1,0:T(8,128)(2,1)S(1)}, u32[]{:S(2)}, u32[]{:S(2)}) collective-permute-start(bf16[4,2,2,192,256]{4,3,2,1,0:T(8,128)(2,1)} %get-tuple-element.192), channel_id=1, source_target_pairs={{0,2},{2,0},{4,6},{6,4},{8,10},{10,8},{12,14},{14,12},{16,18},{18,... | collective-permute-start | bytes 4718600 | tf_op jit(solution)/shard_map/ppermute | solution.py:244
  637.4 59.1 %collective-permute-start.54 = (bf16[2,2,4,192,768]{4,3,2,1,0:T(8,128)(2,1)}, bf16[2,2,4,192,768]{4,3,2,1,0:T(8,128)(2,1)}, u32[]{:S(2)}, u32[]{:S(2)}) collective-permute-start(bf16[2,2,4,192,768]{4,3,2,1,0:T(8,128)(2,1)} %get-tuple-element.190), channel_id=1, source_target_pairs={{0,2},{2,0},{4,6},{6,4},{8,10},{10,8},{12,14},{14,12},{16,18},{18,... | collective-permute-start | bytes 14155784 | tf_op jit(solution)/shard_map/ppermute | solution.py:244
  711.9 78.6 %collective-permute-start.59 = (bf16[2,4,192,768]{3,2,1,0:T(8,128)(2,1)}, bf16[2,4,192,768]{3,2,1,0:T(8,128)(2,1)}, u32[]{:S(2)}, u32[]{:S(2)}) collective-permute-start(bf16[2,4,192,768]{3,2,1,0:T(8,128)(2,1)} %slice_bitcast_fusion.4), channel_id=1, source_target_pairs={{0,4},{2,6},{4,0},{6,2},{8,12},{10,14},{12,8},{14,10},{16,20},{18,... | collective-permute-start | bytes 7077896 | tf_op jit(solution)/shard_map/ppermute | solution.py:240
  714.3 84.4 %collective-permute-start.60 = (bf16[2,2,192,256]{3,2,1,0:T(8,128)(2,1)}, bf16[2,2,192,256]{3,2,1,0:T(8,128)(2,1)}, u32[]{:S(2)}, u32[]{:S(2)}) collective-permute-start(bf16[2,2,192,256]{3,2,1,0:T(8,128)(2,1)} %get-tuple-element.323), channel_id=1, source_target_pairs={{0,24},{2,26},{4,28},{6,30},{8,0},{10,2},{12,4},{14,6},{16,8},{18,... | collective-permute-start | bytes 1179656 | tf_op jit(solution)/shard_map/ppermute | solution.py:236
  717.2 81.5 %collective-permute-start.61 = (bf16[2,2,192,256]{3,2,1,0:T(8,128)(2,1)}, bf16[2,2,192,256]{3,2,1,0:T(8,128)(2,1)}, u32[]{:S(2)}, u32[]{:S(2)}) collective-permute-start(bf16[2,2,192,256]{3,2,1,0:T(8,128)(2,1)} %get-tuple-element.321), channel_id=1, source_target_pairs={{0,8},{2,10},{4,12},{6,14},{8,16},{10,18},{12,20},{14,22},{16,24},... | collective-permute-start | bytes 1179656 | tf_op jit(solution)/shard_map/ppermute | solution.py:236
  719.3 100.8 %collective-permute-start.66 = (bf16[2,2,192,256]{3,2,1,0:T(8,128)(2,1)}, bf16[2,2,192,256]{3,2,1,0:T(8,128)(2,1)}, u32[]{:S(2)}, u32[]{:S(2)}) collective-permute-start(bf16[2,2,192,256]{3,2,1,0:T(8,128)(2,1)} %get-tuple-element.320), channel_id=1, source_target_pairs={{0,24},{2,26},{4,28},{6,30},{8,0},{10,2},{12,4},{14,6},{16,8},{18,... | collective-permute-start | bytes 1179656 | tf_op jit(solution)/shard_map/ppermute | solution.py:236
  741.9 52.4 %collective-permute-start.58 = (bf16[2,4,192,768]{3,2,1,0:T(8,128)(2,1)}, bf16[2,4,192,768]{3,2,1,0:T(8,128)(2,1)}, u32[]{:S(2)}, u32[]{:S(2)}) collective-permute-start(bf16[2,4,192,768]{3,2,1,0:T(8,128)(2,1)} %slice_bitcast_fusion.5), channel_id=1, source_target_pairs={{0,1},{1,0},{2,3},{3,2},{4,5},{5,4},{6,7},{7,6},{8,9},{9,8},{10,11... | collective-permute-start | bytes 7077896 | tf_op jit(solution)/shard_map/ppermute | solution.py:248
  790.5 45.7 %collective-permute-start.64 = (bf16[2,2,192,256]{3,2,1,0:T(8,128)(2,1)S(1)}, bf16[2,2,192,256]{3,2,1,0:T(8,128)(2,1)}, u32[]{:S(2)}, u32[]{:S(2)}) collective-permute-start(bf16[2,2,192,256]{3,2,1,0:T(8,128)(2,1)S(1)} %copy-done.49), channel_id=1, source_target_pairs={{0,8},{2,10},{4,12},{6,14},{8,16},{10,18},{12,20},{14,22},{16,24},... | collective-permute-start | bytes 1179656 | tf_op jit(solution)/shard_map/ppermute | solution.py:236
  815.6 37.5 %collective-permute-start.63 = (bf16[4,192,768]{2,1,0:T(8,128)(2,1)S(1)}, bf16[4,192,768]{2,1,0:T(8,128)(2,1)S(1)}, u32[]{:S(2)}, u32[]{:S(2)}) collective-permute-start(bf16[4,192,768]{2,1,0:T(8,128)(2,1)S(1)} %slice_bitcast_fusion.8), channel_id=1, source_target_pairs={{0,1},{1,0},{2,3},{3,2},{4,5},{5,4},{6,7},{7,6},{8,9},{9,8},{10,11... | collective-permute-start | bytes 3538952 | tf_op jit(solution)/shard_map/ppermute | solution.py:248
  817.2 37.2 %collective-permute-start.62 = (bf16[4,192,768]{2,1,0:T(8,128)(2,1)S(1)}, bf16[4,192,768]{2,1,0:T(8,128)(2,1)S(1)}, u32[]{:S(2)}, u32[]{:S(2)}) collective-permute-start(bf16[4,192,768]{2,1,0:T(8,128)(2,1)S(1)} %slice_bitcast_fusion.9), channel_id=1, source_target_pairs={{0,4},{2,6},{4,0},{6,2},{8,12},{10,14},{12,8},{14,10},{16,20},{18,... | collective-permute-start | bytes 3538952 | tf_op jit(solution)/shard_map/ppermute | solution.py:240
  820.1 31.7 %collective-permute-start.65 = (bf16[2,2,192,256]{3,2,1,0:T(8,128)(2,1)S(1)}, bf16[2,2,192,256]{3,2,1,0:T(8,128)(2,1)S(1)}, u32[]{:S(2)}, u32[]{:S(2)}) collective-permute-start(bf16[2,2,192,256]{3,2,1,0:T(8,128)(2,1)S(1)} %fusion.38), channel_id=1, source_target_pairs={{0,24},{2,26},{4,28},{6,30},{8,0},{10,2},{12,4},{14,6},{16,8},{18,... | collective-permute-start | bytes 1179656 | tf_op jit(solution)/shard_map/ppermute | solution.py:236
  864.9 82.2 %collective-permute-start.79 = (bf16[2,4,128,1408]{3,2,1,0:T(8,128)(2,1)}, bf16[2,4,128,1408]{3,2,1,0:T(8,128)(2,1)}, u32[]{:S(2)}, u32[]{:S(2)}) collective-permute-start(bf16[2,4,128,1408]{3,2,1,0:T(8,128)(2,1)} %get-tuple-element.231), channel_id=1, source_target_pairs={{0,2},{2,0},{4,6},{6,4},{8,10},{10,8},{12,14},{14,12},{16,18},{18,... | collective-permute-start | bytes 8650760 | tf_op jit(solution)/shard_map/ppermute | solution.py:244
  864.9 74.6 %collective-permute-start.84 = (bf16[4,2,128,1280]{3,2,1,0:T(8,128)(2,1)}, bf16[4,2,128,1280]{3,2,1,0:T(8,128)(2,1)}, u32[]{:S(2)}, u32[]{:S(2)}) collective-permute-start(bf16[4,2,128,1280]{3,2,1,0:T(8,128)(2,1)} %get-tuple-element.233), channel_id=1, source_target_pairs={{0,2},{2,0},{4,6},{6,4},{8,10},{10,8},{12,14},{14,12},{16,18},{18,... | collective-permute-start | bytes 7864328 | tf_op jit(solution)/shard_map/ppermute | solution.py:244
  867.3 28.9 %collective-permute-start.69 = (bf16[192,768]{1,0:T(8,128)(2,1)}, bf16[192,768]{1,0:T(8,128)(2,1)S(1)}, u32[]{:S(2)}, u32[]{:S(2)}) collective-permute-start(bf16[192,768]{1,0:T(8,128)(2,1)} %get-tuple-element.335), channel_id=1, source_target_pairs={{0,24},{2,26},{4,28},{6,30},{8,0},{10,2},{12,4},{14,6},{16,8},{18,... | collective-permute-start | bytes 884744 | tf_op jit(solution)/shard_map/ppermute | solution.py:236
  868.5 39.0 %collective-permute-start.68 = (bf16[192,768]{1,0:T(8,128)(2,1)}, bf16[192,768]{1,0:T(8,128)(2,1)}, u32[]{:S(2)}, u32[]{:S(2)}) collective-permute-start(bf16[192,768]{1,0:T(8,128)(2,1)} %get-tuple-element.334), channel_id=1, source_target_pairs={{0,8},{2,10},{4,12},{6,14},{8,16},{10,18},{12,20},{14,22},{16,24},... | collective-permute-start | bytes 884744 | tf_op jit(solution)/shard_map/ppermute | solution.py:236
  907.5 31.3 %collective-permute-start.78 = (bf16[192,2048]{1,0:T(8,128)(2,1)S(1)}, bf16[192,2048]{1,0:T(8,128)(2,1)S(1)}, u32[]{:S(2)}, u32[]{:S(2)}) collective-permute-start(bf16[192,2048]{1,0:T(8,128)(2,1)S(1)} %select_convert_fusion), channel_id=1, source_target_pairs={{0,1},{1,0},{2,3},{3,2},{4,5},{5,4},{6,7},{7,6},{8,9},{9,8},{10,11... | collective-permute-start | bytes 2359304 | tf_op jit(solution)/shard_map/ppermute | solution.py:248
  944.3 31.2 %collective-permute-start.85 = (bf16[2,128,1280]{2,1,0:T(8,128)(2,1)S(1)}, bf16[2,128,1280]{2,1,0:T(8,128)(2,1)S(1)}, u32[]{:S(2)}, u32[]{:S(2)}) collective-permute-start(bf16[2,128,1280]{2,1,0:T(8,128)(2,1)S(1)} %get-tuple-element.314), channel_id=1, source_target_pairs={{0,24},{2,26},{4,28},{6,30},{8,0},{10,2},{12,4},{14,6},{16,8},{18,... | collective-permute-start | bytes 1966088 | tf_op jit(solution)/shard_map/ppermute | solution.py:236
  949.8 38.0 %collective-permute-start.80 = (bf16[4,128,1408]{2,1,0:T(8,128)(2,1)S(1)}, bf16[4,128,1408]{2,1,0:T(8,128)(2,1)S(1)}, u32[]{:S(2)}, u32[]{:S(2)}) collective-permute-start(bf16[4,128,1408]{2,1,0:T(8,128)(2,1)S(1)} %slice_bitcast_fusion.6), channel_id=1, source_target_pairs={{0,4},{2,6},{4,0},{6,2},{8,12},{10,14},{12,8},{14,10},{16,20},{18,... | collective-permute-start | bytes 4325384 | tf_op jit(solution)/shard_map/ppermute | solution.py:240
  (124 other events, 1553.5 us)
Sparse Core Ops, SparseCore 0:
  11.7 110.7 all-gather.2
  124.1 165.4 all-gather.4
  764.4 133.7 reduce-scatter.1

commit v3 on v2

--- a/solution.py
+++ b/solution.py
@@ -868,17 +868,22 @@
     d_hidden, ffn_gain_rows = rms_back(hidden, ffn_gain32, d_ffn)
     ffn_gain_part = jnp.sum(ffn_gain_rows, axis=0)
     d_hidden = d_hidden + cotangent.astype(F32)
-    d_attn = gather_y(d_hidden.astype(BF))
-
+    d_attn = d_hidden.astype(BF)
+    if fast:
+        gate_grad, d_attn = gate_later(d_attn)
+    d_attn = gather_y(d_attn)
+    if fast:
+        d_attn, gate_grad = tied(d_attn, gate_grad)
+
+    if fast:
+        p1, p2, p5, p6 = y_sum
+        d_attn, p1 = tied(d_attn, p1)
+        p1 = step_y(p1)
     o_part = dot(d_attn, context, 0, 0).astype(BF)
     d_attn, o_part = tied(d_attn, o_part)
     o_sum = scatter_dp(o_part).astype(F32)
     if fast:
-        p1, p2, p5, p6 = y_sum
-        d_attn, p1 = tied(d_attn, p1)
-        p1 = step_y(p1)
         two5, two6 = first_hop(p5, 1), first_hop(p6, -1)
-        gate_grad, d_attn = gate_later(d_attn)
     d_context = dot(d_attn, o_t, 1, 0).astype(BF)
     heads = []
     for head in range(hk):

time: 1040 us -> 1020 us (0.981)
  starting transfers between devices: 124 us -> 109 us
    ppermute x18, waiting for transfers between devices: 106 us -> 39.6 us  [swap_y(): return lax.ppermute(v, 'tensor', [(0, 1), (1, 0)])]
    ppermute x14, waiting for transfers between devices: 10.5 us -> 54.3 us  [swap_x(): lax.ppermute(v, 'dp', [(at(z, x, c), at(z, x + 1, c)) for z, x, c in GRID])]
    ppermute x42, waiting for transfers between devices: 225 us -> 254 us  [shift_z(): lax.ppermute(v, 'dp', [(at(z, x, c), at(z + k, x, c)) for z, x, c in GRID])]
    ppermute x42, starting transfers between devices: 81.8 us -> 68.6 us  [shift_z(): lax.ppermute(v, 'dp', [(at(z, x, c), at(z + k, x, c)) for z, x, c in GRID])]
    unnamed x176 -> x174, local copies, waits for them, and re-layouts: 16.7 us -> 20.8 us
  transfers between devices with their start and end apart: 93 -> 93, of which waited for: 41 -> 45; matrix products, arithmetic and copies ran while one was open for 25% -> 24% of each run, Pallas kernels for 15% -> 15%
where the time goes in v3:
time: 1020 us; the launch traced here: 1010 us
  waiting for transfers between devices  426 us (42%)
  Pallas kernels  184 us (18%)
  matrix products  111 us (11%)
  starting transfers between devices  109 us (11%)
  other arithmetic  96.1 us (9%)
  local copies, waits for them, and re-layouts  71.6 us (7%)
  between operations  15.9 us (2%)
    ppermute x42, waiting for transfers between devices, shift_z(): lax.ppermute(v, 'dp', [(at(z, x, c), at(z + k, x, c)) for z, x, c in GRID])  254 us
    all_gather x2, waiting for transfers between devices, gather_dp(): return lax.all_gather(v, 'dp', axis=0, tiled=True)  69.4 us
    pallas_call x2, Pallas kernels, run_experts(): pl.pallas_call(expert_kernel, grid=(4,), in_specs=[pair(2, seq), pair(seq...  69.2 us
    ppermute x42, starting transfers between devices, shift_z(): lax.ppermute(v, 'dp', [(at(z, x, c), at(z + k, x, c)) for z, x, c in GRID])  68.6 us
    ppermute x14, waiting for transfers between devices, swap_x(): lax.ppermute(v, 'dp', [(at(z, x, c), at(z, x + 1, c)) for z, x, c in GRID])  54.3 us
    convert_element_type x38, other arithmetic, add2(): return (a.astype(F32) + b.astype(F32)).astype(BF)  52.9 us
    dot_general x10, matrix products, dot(): lax.dot_general(a, b, (((ca,), (cb,)), ((), ())), preferred_element_type=...  46.7 us
    ppermute x18, waiting for transfers between devices, swap_y(): return lax.ppermute(v, 'tensor', [(0, 1), (1, 0)])  39.6 us
  transfers between devices with their start and end apart: 93, of which 45 were waited for; matrix products, arithmetic and copies ran while one was open for 24% of the time, Pallas kernels for 15%

profile of v3, /device:TPU:0, one launch (start us, length us, event | category | flops | bytes accessed | tf_op | source)
XLA Modules:
  0.0 1013.5 jit_solution(7278045081526940704)
XLA Ops:
  14.0 17.5 %collective-permute-done.16 = bf16[192,2048]{1,0:T(8,128)(2,1)S(1)} collective-permute-done((bf16[192,2048]{1,0:T(8,128)(2,1)S(1)}, bf16[192,2048]{1,0:T(8,128)(2,1)S(1)}, u32[]{:S(2)}, u32[]{:S(2)}) %collective-permute-start.16) | collective-permute-done | bytes 786464 | tf_op jit(solution)/shard_map/ppermute | solution.py:248
  38.2 6.2 pad_maximum_fusion.weights
  44.3 7.6 collective-permute-done
  52.5 69.3 %all-gather.3.cloned.1.call-done = bf16[2048,4736]{0,1:T(8,128)(2,1)} async-done(((bf16[128,4736]{0,1:T(8,128)(2,1)}), bf16[2048,4736]{0,1:T(8,128)(2,1)}) %all-gather.3.cloned.1.call-update) | async-done | bytes 19398672 | tf_op jit(solution)/shard_map/all_gather | solution.py:177
  127.7 11.3 %fusion.2.q_raw.k_raw.v_raw = f32[384,2560]{1,0:T(8,128)} fusion(bf16[384,2048]{1,0:T(8,128)(2,1)S(1)} %fusion.14.left, bf16[2048,4736]{0,1:T(8,128)(2,1)} %all-gather.3.cloned.1.call-done), kind=kOutput, calls=%fused_computation.7 | convolution fusion | flops 4026531840 | bytes 15990784 | tf_op jit(solution)/shard_map/dot_general | solution.py:17
  139.0 14.4 %attend.1 = bf16[384,2048]{1,0:T(8,128)(2,1)} custom-call(f32[384,2560]{1,0:T(8,128)} %fusion.2.q_raw.k_raw.v_raw, f32[384,2560]{1,0:T(8,128)} %fusion.2.q_raw.k_raw.v_raw, f32[384,2560]{1,0:T(8,128)} %fusion.2.q_raw.k_raw.v_raw, f32[8,128]{1,0:T(8,128)} %select_maximum_fusion.gains, f32[384,128]{1,0:T(8,128)} %get-tuple-element.381.cos, ...), custom_call_target="tpu_custom_call" | custom-call | tf_op jit(solution)/shard_map/attend/pallas_call | solution.py:120
  153.4 6.5 fusion.6
  206.4 20.0 %collective-permute-done.6 = bf16[192,768]{1,0:T(8,128)(2,1)S(1)} collective-permute-done((bf16[192,768]{1,0:T(8,128)(2,1)S(1)}, bf16[192,768]{1,0:T(8,128)(2,1)S(1)}, u32[]{:S(2)}, u32[]{:S(2)}) %collective-permute-start.6) | collective-permute-done | bytes 294944 | tf_op jit(solution)/shard_map/ppermute | solution.py:236
  230.8 11.5 %collective-permute-done.3 = bf16[192,768]{1,0:T(8,128)(2,1)S(1)} collective-permute-done((bf16[192,768]{1,0:T(8,128)(2,1)S(1)}, bf16[192,768]{1,0:T(8,128)(2,1)S(1)}, u32[]{:S(2)}, u32[]{:S(2)}) %collective-permute-start.3) | collective-permute-done | bytes 294944 | tf_op jit(solution)/shard_map/ppermute | solution.py:236
  242.4 12.5 %collective-permute-done.5 = bf16[192,768]{1,0:T(8,128)(2,1)S(1)} collective-permute-done((bf16[192,768]{1,0:T(8,128)(2,1)S(1)}, bf16[192,768]{1,0:T(8,128)(2,1)S(1)}, u32[]{:S(2)}, u32[]{:S(2)}) %collective-permute-start.5) | collective-permute-done | bytes 294944 | tf_op jit(solution)/shard_map/ppermute | solution.py:236
  254.9 9.0 collective-permute-done.7
  270.0 31.3 %collective-permute-done.12 = bf16[4,192,768]{2,1,0:T(8,128)(2,1)S(1)} collective-permute-done((bf16[4,192,768]{2,1,0:T(8,128)(2,1)S(1)}, bf16[4,192,768]{2,1,0:T(8,128)(2,1)S(1)}, u32[]{:S(2)}, u32[]{:S(2)}) %collective-permute-start.12) | collective-permute-done | bytes 1179680 | tf_op jit(solution)/shard_map/ppermute | solution.py:240
  310.4 10.0 collective-permute-done.20
  330.1 14.2 %collective-permute-done.17 = bf16[2,2,192,384]{3,2,1,0:T(8,128)(2,1)S(1)} collective-permute-done((bf16[2,2,192,384]{3,2,1,0:T(8,128)(2,1)S(1)}, bf16[2,2,192,384]{3,2,1,0:T(8,128)(2,1)S(1)}, u32[]{:S(2)}, u32[]{:S(2)}) %collective-permute-start.17) | collective-permute-done | bytes 589856 | tf_op jit(solution)/shard_map/ppermute | solution.py:236
  349.5 6.5 collective-permute-done.19
  356.0 13.3 %collective-permute-done.18 = bf16[2,2,192,384]{3,2,1,0:T(8,128)(2,1)} collective-permute-done((bf16[2,2,192,384]{3,2,1,0:T(8,128)(2,1)S(1)}, bf16[2,2,192,384]{3,2,1,0:T(8,128)(2,1)}, u32[]{:S(2)}, u32[]{:S(2)}) %collective-permute-start.18) | collective-permute-done | bytes 589856 | tf_op jit(solution)/shard_map/ppermute | solution.py:236
  372.4 15.8 %cots.2 = (bf16[2,4,256,2048]{3,2,1,0:T(8,128)(2,1)}, f32[2,4,256,384]{3,2,1,0:T(8,128)}) custom-call(s32[8]{0:T(128)} %get-tuple-element.136.where, f32[8,2,384]{2,1,0:T(2,128)} %copy.119.rank, bf16[16,384,2048]{2,1,0:T(8,128)(2,1)} %bitcast.321, bf16[16,384,2048]{2,1,0:T(8,128)(2,1)} %bitcast.322, bf16[2,384,2048]{2,1,0:T(8,128)(2,1)} %down.7), custom_call_target="tpu_custom_call" | custom-call | tf_op jit(solution)/shard_map/cots/pallas_call | solution.py:550
  388.1 15.7 %cots.3 = (bf16[2,4,256,2048]{3,2,1,0:T(8,128)(2,1)}, f32[2,4,256,384]{3,2,1,0:T(8,128)}) custom-call(s32[8]{0:T(128)} %get-tuple-element.140.where, f32[8,2,384]{2,1,0:T(2,128)} %copy.120.rank, bf16[16,384,2048]{2,1,0:T(8,128)(2,1)} %bitcast.323, bf16[16,384,2048]{2,1,0:T(8,128)(2,1)} %bitcast.324, bf16[2,384,2048]{2,1,0:T(8,128)(2,1)} %down.7), custom_call_target="tpu_custom_call" | custom-call | tf_op jit(solution)/shard_map/cots/pallas_call | solution.py:550
  415.7 34.5 %experts.3 = (bf16[2,4,256,2048]{3,2,1,0:T(8,128)(2,1)}, bf16[2,4,256,384]{3,2,1,0:T(8,128)(2,1)}, bf16[2,4,256,384]{3,2,1,0:T(8,128)(2,1)}, bf16[2,4,256,384]{3...) custom-call(f32[8,2,384]{2,1,0:T(2,128)} %copy.122.rank, ...), custom_call_target="tpu_custom_call" | custom-call | tf_op jit(solution)/shard_map/experts/pallas_call | solution.py:573
  453.7 34.7 %experts.2 = (bf16[2,4,256,2048]{3,2,1,0:T(8,128)(2,1)}, bf16[2,4,256,384]{3,2,1,0:T(8,128)(2,1)}, bf16[2,4,256,384]{3,2,1,0:T(8,128)(2,1)}, bf16[2,4,256,384]{3...) custom-call(f32[8,2,384]{2,1,0:T(2,128)} %copy.121.rank, ...), custom_call_target="tpu_custom_call" | custom-call | tf_op jit(solution)/shard_map/experts/pallas_call | solution.py:573
  488.5 12.4 %outs.2 = (bf16[2,2,4,192,768]{4,3,2,1,0:T(8,128)(2,1)}, bf16[2,2,4,192,768]{4,3,2,1,0:T(8,128)(2,1)}, bf16[4,2,2,192,256]{4,3,2,1,0:T(8,128)(2,1)}, bf16[4,2,2,192,256]{4,3,2,1,0:T(8,128)(2,1)}) custom-call(f32[8,384,2]{2,1,0:T(8,128)} %get-tuple-element.132.rank_t, bf16[2,4,256,384]{3,2,1,0:T(8,128)(2,1)} %get-tuple-element.165.scaled, ...), custom_call_target="tpu_custom_call" | custom-call | tf_op jit(solution)/shard_map/outs/pallas_call | solution.py:613
  501.4 6.3 fusion.124
  507.7 11.0 %fusion.125 = f32[2,2048,384,1]{2,1,3,0:T(8,128)} fusion(bf16[2,4,256,2048]{3,2,1,0:T(8,128)(2,1)} %get-tuple-element.199, bf16[2,4,256,384]{3,2,1,0:T(8,128)(2,1)} %get-tuple-element.181), kind=kOutput, calls=%fused_computation.379 | convolution fusion | flops 3221225472 | bytes 16252928 | tf_op jit(solution)/shard_map/egsd,egsf->edf/dot_general | solution.py:667
  561.2 9.6 bitcast_add_fusion.2
  570.8 12.6 %outs.3 = (bf16[2,2,4,192,768]{4,3,2,1,0:T(8,128)(2,1)}, bf16[2,2,4,192,768]{4,3,2,1,0:T(8,128)(2,1)}, bf16[4,2,2,192,256]{4,3,2,1,0:T(8,128)(2,1)}, bf16[4,2,2,192,256]{4,3,2,1,0:T(8,128)(2,1)}) custom-call(f32[8,384,2]{2,1,0:T(8,128)} %get-tuple-element.152.rank_t, bf16[2,4,256,384]{3,2,1,0:T(8,128)(2,1)} %get-tuple-element.170.scaled, ...), custom_call_target="tpu_custom_call" | custom-call | tf_op jit(solution)/shard_map/outs/pallas_call | solution.py:613
  584.7 7.0 collective-permute-done.36
  608.8 13.2 %bitcast_add_fusion.1 = f32[2,2048,384]{2,1,0:T(8,128)} fusion(f32[2,2048,384,1]{2,1,3,0:T(8,128)} %fusion.125, bf16[2,4,256,2048]{3,2,1,0:T(8,128)(2,1)} %get-tuple-element.201, bf16[2,4,256,384]{3,2,1,0:T(8,128)(2,1)} %get-tuple-element.182), kind=kOutput, calls=%fused_computation.16 | convolution fusion | flops 3222798336 | bytes 22544384 | tf_op jit(solution)/shard_map/egsd,egsf->edf/dot_general | solution.py:667
  622.0 12.7 %collective-permute-done.44 = bf16[2,192,256]{2,1,0:T(8,128)(2,1)S(1)} collective-permute-done((bf16[2,192,256]{2,1,0:T(8,128)(2,1)S(1)}, bf16[2,192,256]{2,1,0:T(8,128)(2,1)S(1)}, u32[]{:S(2)}, u32[]{:S(2)}) %collective-permute-start.44) | collective-permute-done | bytes 196640 | tf_op jit(solution)/shard_map/ppermute | solution.py:240
  660.5 7.2 collective-permute-done.49
  672.2 5.8 collective-permute-done.45
  678.0 8.1 collective-permute-start.47
  699.1 6.8 add_convert_fusion
  720.4 11.5 %fusion.126 = f32[2,2048,384,1]{2,1,3,0:T(8,128)} fusion(bf16[2,4,256,2048]{3,2,1,0:T(8,128)(2,1)} %get-tuple-element.199, bf16[2,4,256,384]{3,2,1,0:T(8,128)(2,1)S(1)} %copy-done.73), kind=kOutput, calls=%fused_computation.380 | convolution fusion | flops 3221225472 | bytes 16252928 | tf_op jit(solution)/shard_map/egsd,egsf->edf/dot_general | solution.py:667
  731.9 12.9 %bitcast_add_fusion = f32[2,2048,384]{2,1,0:T(8,128)} fusion(f32[2,2048,384,1]{2,1,3,0:T(8,128)} %fusion.126, bf16[2,4,256,2048]{3,2,1,0:T(8,128)(2,1)} %get-tuple-element.201, bf16[2,4,256,384]{3,2,1,0:T(8,128)(2,1)} %get-tuple-element.202), kind=kOutput, calls=%fused_computation.15 | convolution fusion | flops 3222798336 | bytes 22544384 | tf_op jit(solution)/shard_map/egsd,egsf->edf/dot_general | solution.py:667
  754.4 8.3 convolution_convert_fusion
  762.7 8.5 fusion.16.d_context
  771.2 12.4 %attend_back.2 = (bf16[384,1024]{1,0:T(8,128)(2,1)}, bf16[384,128]{1,0:T(8,128)(2,1)}, bf16[384,128]{1,0:T(8,128)(2,1)}, f32[8,128]{1,0:T(8,128)}) custom-call(f32[384,2560]{1,0:T(8,128)} %fusion.2.q_raw.k_raw.v_raw, f32[384,2560]{1,0:T(8,128)} %fusion.2.q_raw.k_raw.v_raw, f32[384,2560]{1,0:T(8,128)} %fusion.2.q_raw.k_raw.v_raw, ...), custom_call_target="tpu_custom_call" | custom-call | tf_op jit(solution)/shard_map/attend_back/pallas_call | solution.py:143
  797.0 12.6 %attend_back.3 = (bf16[384,1024]{1,0:T(8,128)(2,1)}, bf16[384,128]{1,0:T(8,128)(2,1)}, bf16[384,128]{1,0:T(8,128)(2,1)}, f32[8,128]{1,0:T(8,128)}) custom-call(f32[384,2560]{1,0:T(8,128)} %fusion.2.q_raw.k_raw.v_raw, f32[384,2560]{1,0:T(8,128)} %fusion.2.q_raw.k_raw.v_raw, f32[384,2560]{1,0:T(8,128)} %fusion.2.q_raw.k_raw.v_raw, ...), custom_call_target="tpu_custom_call" | custom-call | tf_op jit(solution)/shard_map/attend_back/pallas_call | solution.py:143
  821.6 21.4 %collective-permute-done.65 = bf16[2,2,192,256]{3,2,1,0:T(8,128)(2,1)S(1)} collective-permute-done((bf16[2,2,192,256]{3,2,1,0:T(8,128)(2,1)S(1)}, bf16[2,2,192,256]{3,2,1,0:T(8,128)(2,1)S(1)}, u32[]{:S(2)}, u32[]{:S(2)}) %collective-permute-start.65) | collective-permute-done | bytes 393248 | tf_op jit(solution)/shard_map/ppermute | solution.py:236
  850.3 9.3 grad.3
  859.6 9.1 grad.2
  876.2 7.3 fusion
  893.3 15.4 %collective-permute-done.69 = bf16[192,768]{1,0:T(8,128)(2,1)S(1)} collective-permute-done((bf16[192,768]{1,0:T(8,128)(2,1)S(1)}, bf16[192,768]{1,0:T(8,128)(2,1)S(1)}, u32[]{:S(2)}, u32[]{:S(2)}) %collective-permute-start.69) | collective-permute-done | bytes 294944 | tf_op jit(solution)/shard_map/ppermute | solution.py:236
  910.2 9.8 collective-permute-done.73
  923.2 12.5 %collective-permute-done.70 = bf16[192,768]{1,0:T(8,128)(2,1)S(1)} collective-permute-done((bf16[192,768]{1,0:T(8,128)(2,1)S(1)}, bf16[192,768]{1,0:T(8,128)(2,1)S(1)}, u32[]{:S(2)}, u32[]{:S(2)}) %collective-permute-start.70) | collective-permute-done | bytes 294944 | tf_op jit(solution)/shard_map/ppermute | solution.py:236
  944.5 11.8 %collective-permute-done.86 = bf16[2,128,1280]{2,1,0:T(8,128)(2,1)S(1)} collective-permute-done((bf16[2,128,1280]{2,1,0:T(8,128)(2,1)S(1)}, bf16[2,128,1280]{2,1,0:T(8,128)(2,1)S(1)}, u32[]{:S(2)}, u32[]{:S(2)}) %collective-permute-start.86) | collective-permute-done | bytes 655392 | tf_op jit(solution)/shard_map/ppermute | solution.py:236
  963.6 13.3 %collective-permute-done.87 = bf16[2,128,1280]{2,1,0:T(8,128)(2,1)S(1)} collective-permute-done((bf16[2,128,1280]{2,1,0:T(8,128)(2,1)S(1)}, bf16[2,128,1280]{2,1,0:T(8,128)(2,1)S(1)}, u32[]{:S(2)}, u32[]{:S(2)}) %collective-permute-start.87) | collective-permute-done | bytes 655392 | tf_op jit(solution)/shard_map/ppermute | solution.py:236
  981.0 6.7 collective-permute-done.82
  (525 shorter events, 340.3 us)
Async XLA Ops:
  7.3 114.6 %all-gather.3.cloned.1.call-start = ((), (), s32[]{:S(2)}) async-start(), calls=%async_computation.1 | async-start | bytes 20611072 | tf_op jit(solution)/shard_map/all_gather | solution.py:177
  10.9 361.5 %all-gather.5.cloned.1.call-start = ((), (), s32[]{:S(2)}) async-start(), calls=%async_computation.2 | async-start | bytes 26738688 | tf_op jit(solution)/shard_map/all_gather | solution.py:177
  33.0 971.3 %reduce-scatter.2.cloned.1.call-start = ((), (), s32[]{:S(2)}) async-start(), calls=%async_computation.3 | async-start | bytes 8912896 | tf_op jit(solution)/shard_map/reduce_scatter | solution.py:189
  192.5 38.2 %collective-permute-start.4 = (bf16[192,768]{1,0:T(8,128)(2,1)S(1)}, bf16[192,768]{1,0:T(8,128)(2,1)S(1)}, u32[]{:S(2)}, u32[]{:S(2)}) collective-permute-start(bf16[192,768]{1,0:T(8,128)(2,1)S(1)} %get-tuple-element.352), channel_id=1, source_target_pairs={{0,24},{2,26},{4,28},{6,30},{8,0},{10,2},{12,4},{14,6},{16,8},{18,... | collective-permute-start | bytes 884744 | tf_op jit(solution)/shard_map/ppermute | solution.py:236
  196.3 30.0 %collective-permute-start.6 = (bf16[192,768]{1,0:T(8,128)(2,1)S(1)}, bf16[192,768]{1,0:T(8,128)(2,1)S(1)}, u32[]{:S(2)}, u32[]{:S(2)}) collective-permute-start(bf16[192,768]{1,0:T(8,128)(2,1)S(1)} %get-tuple-element.351), channel_id=1, source_target_pairs={{0,24},{2,26},{4,28},{6,30},{8,0},{10,2},{12,4},{14,6},{16,8},{18,... | collective-permute-start | bytes 884744 | tf_op jit(solution)/shard_map/ppermute | solution.py:236
  196.4 29.9 %collective-permute-start.11 = (bf16[2,192,256]{2,1,0:T(8,128)(2,1)S(1)}, bf16[2,192,256]{2,1,0:T(8,128)(2,1)S(1)}, u32[]{:S(2)}, u32[]{:S(2)}) collective-permute-start(bf16[2,192,256]{2,1,0:T(8,128)(2,1)S(1)} %get-tuple-element.358), channel_id=1, source_target_pairs={{0,4},{2,6},{4,0},{6,2},{8,12},{10,14},{12,8},{14,10},{16,20},{18,... | collective-permute-start | bytes 589832 | tf_op jit(solution)/shard_map/ppermute | solution.py:240
  198.7 32.0 %collective-permute-start.9 = (bf16[2,192,384]{2,1,0:T(8,128)(2,1)S(1)}, bf16[2,192,384]{2,1,0:T(8,128)(2,1)S(1)}, u32[]{:S(2)}, u32[]{:S(2)}) collective-permute-start(bf16[2,192,384]{2,1,0:T(8,128)(2,1)S(1)} %get-tuple-element.356), channel_id=1, source_target_pairs={{0,1},{1,0},{2,3},{3,2},{4,5},{5,4},{6,7},{7,6},{8,9},{9,8},{10,11... | collective-permute-start | bytes 884744 | tf_op jit(solution)/shard_map/ppermute | solution.py:248
  204.4 37.9 %collective-permute-start.3 = (bf16[192,768]{1,0:T(8,128)(2,1)S(1)}, bf16[192,768]{1,0:T(8,128)(2,1)S(1)}, u32[]{:S(2)}, u32[]{:S(2)}) collective-permute-start(bf16[192,768]{1,0:T(8,128)(2,1)S(1)} %collective-permute-done.2), channel_id=1, source_target_pairs={{0,8},{2,10},{4,12},{6,14},{8,16},{10,18},{12,20},{14,22},{16,24},... | collective-permute-start | bytes 884744 | tf_op jit(solution)/shard_map/ppermute | solution.py:236
  226.3 28.6 %collective-permute-start.5 = (bf16[192,768]{1,0:T(8,128)(2,1)S(1)}, bf16[192,768]{1,0:T(8,128)(2,1)S(1)}, u32[]{:S(2)}, u32[]{:S(2)}) collective-permute-start(bf16[192,768]{1,0:T(8,128)(2,1)S(1)} %get-tuple-element.351), channel_id=1, source_target_pairs={{0,8},{2,10},{4,12},{6,14},{8,16},{10,18},{12,20},{14,22},{16,24},... | collective-permute-start | bytes 884744 | tf_op jit(solution)/shard_map/ppermute | solution.py:236
  226.3 37.6 %collective-permute-start.7 = (bf16[192,768]{1,0:T(8,128)(2,1)S(1)}, bf16[192,768]{1,0:T(8,128)(2,1)S(1)}, u32[]{:S(2)}, u32[]{:S(2)}) collective-permute-start(bf16[192,768]{1,0:T(8,128)(2,1)S(1)} %collective-permute-done.6), channel_id=1, source_target_pairs={{0,24},{2,26},{4,28},{6,30},{8,0},{10,2},{12,4},{14,6},{16,8},{18,... | collective-permute-start | bytes 884744 | tf_op jit(solution)/shard_map/ppermute | solution.py:236
  264.1 37.2 %collective-permute-start.12 = (bf16[4,192,768]{2,1,0:T(8,128)(2,1)S(1)}, bf16[4,192,768]{2,1,0:T(8,128)(2,1)S(1)}, u32[]{:S(2)}, u32[]{:S(2)}) collective-permute-start(bf16[4,192,768]{2,1,0:T(8,128)(2,1)S(1)} %pad_maximum_fusion.8), channel_id=1, source_target_pairs={{0,4},{2,6},{4,0},{6,2},{8,12},{10,14},{12,8},{14,10},{16,20},{18,... | collective-permute-start | bytes 3538952 | tf_op jit(solution)/shard_map/ppermute | solution.py:240
  265.2 39.1 %collective-permute-start.14 = (bf16[4,192,768]{2,1,0:T(8,128)(2,1)S(1)}, bf16[4,192,768]{2,1,0:T(8,128)(2,1)S(1)}, u32[]{:S(2)}, u32[]{:S(2)}) collective-permute-start(bf16[4,192,768]{2,1,0:T(8,128)(2,1)S(1)} %pad_maximum_fusion.9), channel_id=1, source_target_pairs={{0,1},{1,0},{2,3},{3,2},{4,5},{5,4},{6,7},{7,6},{8,9},{9,8},{10,11... | collective-permute-start | bytes 3538952 | tf_op jit(solution)/shard_map/ppermute | solution.py:248
  265.7 40.9 %collective-permute-start.21 = (bf16[2,2,192,256]{3,2,1,0:T(8,128)(2,1)S(1)}, bf16[2,2,192,256]{3,2,1,0:T(8,128)(2,1)S(1)}, u32[]{:S(2)}, u32[]{:S(2)}) collective-permute-start(bf16[2,2,192,256]{3,2,1,0:T(8,128)(2,1)S(1)} %pad_maximum_fusion.11), channel_id=1, source_target_pairs={{0,24},{2,26},{4,28},{6,30},{8,0},{10,2},{12,4},{14,6},{16,8},{18,... | collective-permute-start | bytes 1179656 | tf_op jit(solution)/shard_map/ppermute | solution.py:236
  302.9 101.0 %collective-permute-start.13 = (bf16[2,4,192,768]{3,2,1,0:T(8,128)(2,1)}, bf16[2,4,192,768]{3,2,1,0:T(8,128)(2,1)}, u32[]{:S(2)}, u32[]{:S(2)}) collective-permute-start(bf16[2,4,192,768]{3,2,1,0:T(8,128)(2,1)} %pad_maximum_fusion.1.x1a), channel_id=1, source_target_pairs={{0,1},{1,0},{2,3},{3,2},{4,5},{5,4},{6,7},{7,6},{8,9},{9,8},{10,11... | collective-permute-start | bytes 7077896 | tf_op jit(solution)/shard_map/ppermute | solution.py:248
  306.0 98.4 %collective-permute-start.15 = (bf16[2,4,192,768]{3,2,1,0:T(8,128)(2,1)}, bf16[2,4,192,768]{3,2,1,0:T(8,128)(2,1)}, u32[]{:S(2)}, u32[]{:S(2)}) collective-permute-start(bf16[2,4,192,768]{3,2,1,0:T(8,128)(2,1)} %pad_maximum_fusion.2.x2a), channel_id=1, source_target_pairs={{0,4},{2,6},{4,0},{6,2},{8,12},{10,14},{12,8},{14,10},{16,20},{18,... | collective-permute-start | bytes 7077896 | tf_op jit(solution)/shard_map/ppermute | solution.py:240
  326.3 78.2 %collective-permute-start.28 = (bf16[4,2,2,192,256]{4,3,2,1,0:T(8,128)(2,1)}, bf16[4,2,2,192,256]{4,3,2,1,0:T(8,128)(2,1)}, u32[]{:S(2)}, u32[]{:S(2)}) collective-permute-start(bf16[4,2,2,192,256]{4,3,2,1,0:T(8,128)(2,1)} %pad_maximum_fusion.6.x6), channel_id=1, source_target_pairs={{0,2},{2,0},{4,6},{6,4},{8,10},{10,8},{12,14},{14,12},{16,18},{18,... | collective-permute-start | bytes 4718600 | tf_op jit(solution)/shard_map/ppermute | solution.py:244
  327.8 28.2 %collective-permute-start.19 = (bf16[2,2,192,384]{3,2,1,0:T(8,128)(2,1)S(1)}, bf16[2,2,192,384]{3,2,1,0:T(8,128)(2,1)}, u32[]{:S(2)}, u32[]{:S(2)}) collective-permute-start(bf16[2,2,192,384]{3,2,1,0:T(8,128)(2,1)S(1)} %pad_maximum_fusion.10), channel_id=1, source_target_pairs={{0,24},{2,26},{4,28},{6,30},{8,0},{10,2},{12,4},{14,6},{16,8},{18,... | collective-permute-start | bytes 1769480 | tf_op jit(solution)/shard_map/ppermute | solution.py:236
  356.0 51.4 %collective-permute-start.23 = (bf16[2,4,192,768]{3,2,1,0:T(8,128)(2,1)}, bf16[2,4,192,768]{3,2,1,0:T(8,128)(2,1)}, u32[]{:S(2)}, u32[]{:S(2)}) collective-permute-start(bf16[2,4,192,768]{3,2,1,0:T(8,128)(2,1)} %pad_maximum_fusion.1.x1a), channel_id=1, source_target_pairs={{0,2},{2,0},{4,6},{6,4},{8,10},{10,8},{12,14},{14,12},{16,18},{18,... | collective-permute-start | bytes 7077896 | tf_op jit(solution)/shard_map/ppermute | solution.py:244
  369.3 38.1 %collective-permute-start.25 = (bf16[2,4,192,768]{3,2,1,0:T(8,128)(2,1)}, bf16[2,4,192,768]{3,2,1,0:T(8,128)(2,1)}, u32[]{:S(2)}, u32[]{:S(2)}) collective-permute-start(bf16[2,4,192,768]{3,2,1,0:T(8,128)(2,1)} %pad_maximum_fusion.2.x2a), channel_id=1, source_target_pairs={{0,2},{2,0},{4,6},{6,4},{8,10},{10,8},{12,14},{14,12},{16,18},{18,... | collective-permute-start | bytes 7077896 | tf_op jit(solution)/shard_map/ppermute | solution.py:244
  450.2 80.6 %collective-permute-start.29 = (bf16[2,2,4,192,768]{4,3,2,1,0:T(8,128)(2,1)}, bf16[2,2,4,192,768]{4,3,2,1,0:T(8,128)(2,1)}, u32[]{:S(2)}, u32[]{:S(2)}) collective-permute-start(bf16[2,2,4,192,768]{4,3,2,1,0:T(8,128)(2,1)} %get-tuple-element.158), channel_id=1, source_target_pairs={{0,2},{2,0},{4,6},{6,4},{8,10},{10,8},{12,14},{14,12},{16,18},{18,... | collective-permute-start | bytes 14155784 | tf_op jit(solution)/shard_map/ppermute | solution.py:244
  450.6 87.6 %collective-permute-start.31 = (bf16[2,2,4,192,768]{4,3,2,1,0:T(8,128)(2,1)}, bf16[2,2,4,192,768]{4,3,2,1,0:T(8,128)(2,1)}, u32[]{:S(2)}, u32[]{:S(2)}) collective-permute-start(bf16[2,2,4,192,768]{4,3,2,1,0:T(8,128)(2,1)} %get-tuple-element.160), channel_id=1, source_target_pairs={{0,2},{2,0},{4,6},{6,4},{8,10},{10,8},{12,14},{14,12},{16,18},{18,... | collective-permute-start | bytes 14155784 | tf_op jit(solution)/shard_map/ppermute | solution.py:244
  523.5 34.7 %collective-permute-start.38 = (bf16[2,2,192,256]{3,2,1,0:T(8,128)(2,1)}, bf16[2,2,192,256]{3,2,1,0:T(8,128)(2,1)}, u32[]{:S(2)}, u32[]{:S(2)}) collective-permute-start(bf16[2,2,192,256]{3,2,1,0:T(8,128)(2,1)} %get-tuple-element.330), channel_id=1, source_target_pairs={{0,24},{2,26},{4,28},{6,30},{8,0},{10,2},{12,4},{14,6},{16,8},{18,... | collective-permute-start | bytes 1179656 | tf_op jit(solution)/shard_map/ppermute | solution.py:236
  537.7 55.3 %collective-permute-start.30 = (bf16[2,4,192,768]{3,2,1,0:T(8,128)(2,1)}, bf16[2,4,192,768]{3,2,1,0:T(8,128)(2,1)}, u32[]{:S(2)}, u32[]{:S(2)}) collective-permute-start(bf16[2,4,192,768]{3,2,1,0:T(8,128)(2,1)} %slice_bitcast_fusion.2), channel_id=1, source_target_pairs={{0,1},{1,0},{2,3},{3,2},{4,5},{5,4},{6,7},{7,6},{8,9},{9,8},{10,11... | collective-permute-start | bytes 7077896 | tf_op jit(solution)/shard_map/ppermute | solution.py:248
  546.3 53.6 %collective-permute-start.32 = (bf16[2,4,192,768]{3,2,1,0:T(8,128)(2,1)}, bf16[2,4,192,768]{3,2,1,0:T(8,128)(2,1)}, u32[]{:S(2)}, u32[]{:S(2)}) collective-permute-start(bf16[2,4,192,768]{3,2,1,0:T(8,128)(2,1)} %slice_bitcast_fusion), channel_id=1, source_target_pairs={{0,4},{2,6},{4,0},{6,2},{8,12},{10,14},{12,8},{14,10},{16,20},{18,... | collective-permute-start | bytes 7077896 | tf_op jit(solution)/shard_map/ppermute | solution.py:240
  549.9 33.5 %collective-permute-start.40 = (bf16[2,2,192,256]{3,2,1,0:T(8,128)(2,1)S(1)}, bf16[2,2,192,256]{3,2,1,0:T(8,128)(2,1)S(1)}, u32[]{:S(2)}, u32[]{:S(2)}) collective-permute-start(bf16[2,2,192,256]{3,2,1,0:T(8,128)(2,1)S(1)} %fusion.41), channel_id=1, source_target_pairs={{0,8},{2,10},{4,12},{6,14},{8,16},{10,18},{12,20},{14,22},{16,24},... | collective-permute-start | bytes 1179656 | tf_op jit(solution)/shard_map/ppermute | solution.py:236
  556.1 28.6 %collective-permute-start.34 = (bf16[2,2,192,384]{3,2,1,0:T(8,128)(2,1)S(1)}, bf16[2,2,192,384]{3,2,1,0:T(8,128)(2,1)S(1)}, u32[]{:S(2)}, u32[]{:S(2)}) collective-permute-start(bf16[2,2,192,384]{3,2,1,0:T(8,128)(2,1)S(1)} %get-tuple-element.320), channel_id=1, source_target_pairs={{0,8},{2,10},{4,12},{6,14},{8,16},{10,18},{12,20},{14,22},{16,24},... | collective-permute-start | bytes 1769480 | tf_op jit(solution)/shard_map/ppermute | solution.py:236
  558.2 33.5 %collective-permute-start.36 = (bf16[2,2,192,384]{3,2,1,0:T(8,128)(2,1)S(1)}, bf16[2,2,192,384]{3,2,1,0:T(8,128)(2,1)S(1)}, u32[]{:S(2)}, u32[]{:S(2)}) collective-permute-start(bf16[2,2,192,384]{3,2,1,0:T(8,128)(2,1)S(1)} %fusion.31), channel_id=1, source_target_pairs={{0,24},{2,26},{4,28},{6,30},{8,0},{10,2},{12,4},{14,6},{16,8},{18,... | collective-permute-start | bytes 1769480 | tf_op jit(solution)/shard_map/ppermute | solution.py:236
  603.4 35.8 %collective-permute-start.41 = (bf16[4,192,768]{2,1,0:T(8,128)(2,1)}, bf16[4,192,768]{2,1,0:T(8,128)(2,1)}, u32[]{:S(2)}, u32[]{:S(2)}) collective-permute-start(bf16[4,192,768]{2,1,0:T(8,128)(2,1)} %slice_bitcast_fusion.11), channel_id=1, source_target_pairs={{0,4},{2,6},{4,0},{6,2},{8,12},{10,14},{12,8},{14,10},{16,20},{18,... | collective-permute-start | bytes 3538952 | tf_op jit(solution)/shard_map/ppermute | solution.py:240
  606.3 35.2 %collective-permute-start.42 = (bf16[4,192,768]{2,1,0:T(8,128)(2,1)}, bf16[4,192,768]{2,1,0:T(8,128)(2,1)S(1)}, u32[]{:S(2)}, u32[]{:S(2)}) collective-permute-start(bf16[4,192,768]{2,1,0:T(8,128)(2,1)} %slice_bitcast_fusion.10), channel_id=1, source_target_pairs={{0,1},{1,0},{2,3},{3,2},{4,5},{5,4},{6,7},{7,6},{8,9},{9,8},{10,11... | collective-permute-start | bytes 3538952 | tf_op jit(solution)/shard_map/ppermute | solution.py:248
  607.4 31.7 %collective-permute-start.43 = (bf16[2,192,384]{2,1,0:T(8,128)(2,1)S(1)}, bf16[2,192,384]{2,1,0:T(8,128)(2,1)S(1)}, u32[]{:S(2)}, u32[]{:S(2)}) collective-permute-start(bf16[2,192,384]{2,1,0:T(8,128)(2,1)S(1)} %slice_bitcast_fusion.42), channel_id=1, source_target_pairs={{0,1},{1,0},{2,3},{3,2},{4,5},{5,4},{6,7},{7,6},{8,9},{9,8},{10,11... | collective-permute-start | bytes 884744 | tf_op jit(solution)/shard_map/ppermute | solution.py:248
  608.8 86.4 %collective-permute-start.51 = (bf16[2,2,4,192,768]{4,3,2,1,0:T(8,128)(2,1)}, bf16[2,2,4,192,768]{4,3,2,1,0:T(8,128)(2,1)}, u32[]{:S(2)}, u32[]{:S(2)}) collective-permute-start(bf16[2,2,4,192,768]{4,3,2,1,0:T(8,128)(2,1)} %get-tuple-element.186), channel_id=1, source_target_pairs={{0,2},{2,0},{4,6},{6,4},{8,10},{10,8},{12,14},{14,12},{16,18},{18,... | collective-permute-start | bytes 14155784 | tf_op jit(solution)/shard_map/ppermute | solution.py:244
  634.7 64.4 %collective-permute-start.54 = (bf16[2,2,4,192,768]{4,3,2,1,0:T(8,128)(2,1)}, bf16[2,2,4,192,768]{4,3,2,1,0:T(8,128)(2,1)}, u32[]{:S(2)}, u32[]{:S(2)}) collective-permute-start(bf16[2,2,4,192,768]{4,3,2,1,0:T(8,128)(2,1)} %get-tuple-element.192), channel_id=1, source_target_pairs={{0,2},{2,0},{4,6},{6,4},{8,10},{10,8},{12,14},{14,12},{16,18},{18,... | collective-permute-start | bytes 14155784 | tf_op jit(solution)/shard_map/ppermute | solution.py:244
  639.1 28.7 %collective-permute-start.55 = (bf16[4,2,2,192,256]{4,3,2,1,0:T(8,128)(2,1)}, bf16[4,2,2,192,256]{4,3,2,1,0:T(8,128)(2,1)S(1)}, u32[]{:S(2)}, u32[]{:S(2)}) collective-permute-start(bf16[4,2,2,192,256]{4,3,2,1,0:T(8,128)(2,1)} %get-tuple-element.194), channel_id=1, source_target_pairs={{0,2},{2,0},{4,6},{6,4},{8,10},{10,8},{12,14},{14,12},{16,18},{18,... | collective-permute-start | bytes 4718600 | tf_op jit(solution)/shard_map/ppermute | solution.py:244
  639.2 46.9 %collective-permute-start.56 = (bf16[4,2,2,192,256]{4,3,2,1,0:T(8,128)(2,1)}, bf16[4,2,2,192,256]{4,3,2,1,0:T(8,128)(2,1)S(1)}, u32[]{:S(2)}, u32[]{:S(2)}) collective-permute-start(bf16[4,2,2,192,256]{4,3,2,1,0:T(8,128)(2,1)} %get-tuple-element.196), channel_id=1, source_target_pairs={{0,2},{2,0},{4,6},{6,4},{8,10},{10,8},{12,14},{14,12},{16,18},{18,... | collective-permute-start | bytes 4718600 | tf_op jit(solution)/shard_map/ppermute | solution.py:244
  711.9 32.9 %collective-permute-start.57 = (bf16[192,2048]{1,0:T(8,128)(2,1)}, bf16[192,2048]{1,0:T(8,128)(2,1)}, u32[]{:S(2)}, u32[]{:S(2)}) collective-permute-start(bf16[192,2048]{1,0:T(8,128)(2,1)} %fusion.115), channel_id=1, source_target_pairs={{0,1},{1,0},{2,3},{3,2},{4,5},{5,4},{6,7},{7,6},{8,9},{9,8},{10,11... | collective-permute-start | bytes 2359304 | tf_op jit(solution)/shard_map/ppermute | solution.py:248
  714.4 69.2 %collective-permute-start.59 = (bf16[2,4,192,768]{3,2,1,0:T(8,128)(2,1)}, bf16[2,4,192,768]{3,2,1,0:T(8,128)(2,1)}, u32[]{:S(2)}, u32[]{:S(2)}) collective-permute-start(bf16[2,4,192,768]{3,2,1,0:T(8,128)(2,1)} %slice_bitcast_fusion.4), channel_id=1, source_target_pairs={{0,4},{2,6},{4,0},{6,2},{8,12},{10,14},{12,8},{14,10},{16,20},{18,... | collective-permute-start | bytes 7077896 | tf_op jit(solution)/shard_map/ppermute | solution.py:240
  716.4 80.6 %collective-permute-start.60 = (bf16[2,2,192,256]{3,2,1,0:T(8,128)(2,1)}, bf16[2,2,192,256]{3,2,1,0:T(8,128)(2,1)}, u32[]{:S(2)}, u32[]{:S(2)}) collective-permute-start(bf16[2,2,192,256]{3,2,1,0:T(8,128)(2,1)} %get-tuple-element.327), channel_id=1, source_target_pairs={{0,24},{2,26},{4,28},{6,30},{8,0},{10,2},{12,4},{14,6},{16,8},{18,... | collective-permute-start | bytes 1179656 | tf_op jit(solution)/shard_map/ppermute | solution.py:236
  719.0 78.0 %collective-permute-start.61 = (bf16[2,2,192,256]{3,2,1,0:T(8,128)(2,1)}, bf16[2,2,192,256]{3,2,1,0:T(8,128)(2,1)}, u32[]{:S(2)}, u32[]{:S(2)}) collective-permute-start(bf16[2,2,192,256]{3,2,1,0:T(8,128)(2,1)} %get-tuple-element.325), channel_id=1, source_target_pairs={{0,8},{2,10},{4,12},{6,14},{8,16},{10,18},{12,20},{14,22},{16,24},... | collective-permute-start | bytes 1179656 | tf_op jit(solution)/shard_map/ppermute | solution.py:236
  719.4 102.1 %collective-permute-start.64 = (bf16[2,2,192,256]{3,2,1,0:T(8,128)(2,1)}, bf16[2,2,192,256]{3,2,1,0:T(8,128)(2,1)}, u32[]{:S(2)}, u32[]{:S(2)}) collective-permute-start(bf16[2,2,192,256]{3,2,1,0:T(8,128)(2,1)} %get-tuple-element.326), channel_id=1, source_target_pairs={{0,8},{2,10},{4,12},{6,14},{8,16},{10,18},{12,20},{14,22},{16,24},... | collective-permute-start | bytes 1179656 | tf_op jit(solution)/shard_map/ppermute | solution.py:236
  749.1 43.1 %collective-permute-start.58 = (bf16[2,4,192,768]{3,2,1,0:T(8,128)(2,1)}, bf16[2,4,192,768]{3,2,1,0:T(8,128)(2,1)}, u32[]{:S(2)}, u32[]{:S(2)}) collective-permute-start(bf16[2,4,192,768]{3,2,1,0:T(8,128)(2,1)} %slice_bitcast_fusion.5), channel_id=1, source_target_pairs={{0,1},{1,0},{2,3},{3,2},{4,5},{5,4},{6,7},{7,6},{8,9},{9,8},{10,11... | collective-permute-start | bytes 7077896 | tf_op jit(solution)/shard_map/ppermute | solution.py:248
  784.6 59.6 %collective-permute-start.66 = (bf16[2,2,192,256]{3,2,1,0:T(8,128)(2,1)S(1)}, bf16[2,2,192,256]{3,2,1,0:T(8,128)(2,1)}, u32[]{:S(2)}, u32[]{:S(2)}) collective-permute-start(bf16[2,2,192,256]{3,2,1,0:T(8,128)(2,1)S(1)} %copy-done.49), channel_id=1, source_target_pairs={{0,24},{2,26},{4,28},{6,30},{8,0},{10,2},{12,4},{14,6},{16,8},{18,... | collective-permute-start | bytes 1179656 | tf_op jit(solution)/shard_map/ppermute | solution.py:236
  811.2 37.5 %collective-permute-start.62 = (bf16[4,192,768]{2,1,0:T(8,128)(2,1)S(1)}, bf16[4,192,768]{2,1,0:T(8,128)(2,1)S(1)}, u32[]{:S(2)}, u32[]{:S(2)}) collective-permute-start(bf16[4,192,768]{2,1,0:T(8,128)(2,1)S(1)} %slice_bitcast_fusion.9), channel_id=1, source_target_pairs={{0,4},{2,6},{4,0},{6,2},{8,12},{10,14},{12,8},{14,10},{16,20},{18,... | collective-permute-start | bytes 3538952 | tf_op jit(solution)/shard_map/ppermute | solution.py:240
  812.6 37.4 %collective-permute-start.63 = (bf16[4,192,768]{2,1,0:T(8,128)(2,1)S(1)}, bf16[4,192,768]{2,1,0:T(8,128)(2,1)S(1)}, u32[]{:S(2)}, u32[]{:S(2)}) collective-permute-start(bf16[4,192,768]{2,1,0:T(8,128)(2,1)S(1)} %slice_bitcast_fusion.8), channel_id=1, source_target_pairs={{0,1},{1,0},{2,3},{3,2},{4,5},{5,4},{6,7},{7,6},{8,9},{9,8},{10,11... | collective-permute-start | bytes 3538952 | tf_op jit(solution)/shard_map/ppermute | solution.py:248
  815.0 27.9 %collective-permute-start.65 = (bf16[2,2,192,256]{3,2,1,0:T(8,128)(2,1)S(1)}, bf16[2,2,192,256]{3,2,1,0:T(8,128)(2,1)S(1)}, u32[]{:S(2)}, u32[]{:S(2)}) collective-permute-start(bf16[2,2,192,256]{3,2,1,0:T(8,128)(2,1)S(1)} %fusion.38), channel_id=1, source_target_pairs={{0,24},{2,26},{4,28},{6,30},{8,0},{10,2},{12,4},{14,6},{16,8},{18,... | collective-permute-start | bytes 1179656 | tf_op jit(solution)/shard_map/ppermute | solution.py:236
  871.0 39.2 %collective-permute-start.71 = (bf16[192,768]{1,0:T(8,128)(2,1)S(1)}, bf16[192,768]{1,0:T(8,128)(2,1)S(1)}, u32[]{:S(2)}, u32[]{:S(2)}) collective-permute-start(bf16[192,768]{1,0:T(8,128)(2,1)S(1)} %get-tuple-element.340), channel_id=1, source_target_pairs={{0,24},{2,26},{4,28},{6,30},{8,0},{10,2},{12,4},{14,6},{16,8},{18,... | collective-permute-start | bytes 884744 | tf_op jit(solution)/shard_map/ppermute | solution.py:236
  886.8 49.7 %collective-permute-start.84 = (bf16[4,2,128,1280]{3,2,1,0:T(8,128)(2,1)S(1)}, bf16[4,2,128,1280]{3,2,1,0:T(8,128)(2,1)S(1)}, u32[]{:S(2)}, u32[]{:S(2)}) collective-permute-start(bf16[4,2,128,1280]{3,2,1,0:T(8,128)(2,1)S(1)} %copy-done.72), channel_id=1, source_target_pairs={{0,2},{2,0},{4,6},{6,4},{8,10},{10,8},{12,14},{14,12},{16,18},{18,... | collective-permute-start | bytes 7864328 | tf_op jit(solution)/shard_map/ppermute | solution.py:244
  886.9 55.4 %collective-permute-start.79 = (bf16[2,4,128,1408]{3,2,1,0:T(8,128)(2,1)S(1)}, bf16[2,4,128,1408]{3,2,1,0:T(8,128)(2,1)S(1)}, u32[]{:S(2)}, u32[]{:S(2)}) collective-permute-start(bf16[2,4,128,1408]{3,2,1,0:T(8,128)(2,1)S(1)} %copy-done.71), channel_id=1, source_target_pairs={{0,2},{2,0},{4,6},{6,4},{8,10},{10,8},{12,14},{14,12},{16,18},{18,... | collective-permute-start | bytes 8650760 | tf_op jit(solution)/shard_map/ppermute | solution.py:244
  943.2 34.0 %collective-permute-start.80 = (bf16[4,128,1408]{2,1,0:T(8,128)(2,1)S(1)}, bf16[4,128,1408]{2,1,0:T(8,128)(2,1)S(1)}, u32[]{:S(2)}, u32[]{:S(2)}) collective-permute-start(bf16[4,128,1408]{2,1,0:T(8,128)(2,1)S(1)} %slice_bitcast_fusion.6), channel_id=1, source_target_pairs={{0,4},{2,6},{4,0},{6,2},{8,12},{10,14},{12,8},{14,10},{16,20},{18,... | collective-permute-start | bytes 4325384 | tf_op jit(solution)/shard_map/ppermute | solution.py:240
  (123 other events, 1952.3 us)
Sparse Core Ops, SparseCore 0:
  11.0 110.8 all-gather.2
  123.5 173.1 all-gather.4
  783.7 127.6 reduce-scatter.1
